TPU v7x, 32 devices: a whole 2x2x4 slice. The times are simulated.
32 devices in a mesh: groups: 2 (over x), ctx: 16 (over z, y, core).
Axes of the slice: x: 2, y: 2, z: 4, core: 2. Of those that a mesh axis runs over, the one named last changes fastest.
Arguments:
- features: bfloat16 [8192, 3, 4096], P(('groups', 'ctx')), parts along dimension 0, may hold values from -6 to 6
- short_weight: float32 [3, 3, 4096], replicated, may hold values from -3 to 3
- residues: float32 [256, 16], replicated, may hold values from -4 to 4
- rates: float32 [256, 16], replicated, may hold values from 0 to 1, as said below
- skip: float32 [4096], replicated, may hold values from -4 to 4
- carry_state: float32 [32, 4096], P('groups'), parts along dimension 0, may hold values from -120 to 120
- earlier_rows: bfloat16 [4, 3, 4096], P('groups'), parts along dimension 0, may hold values from -6 to 6
- segment_ids: int32 [8192], P('groups'), parts along dimension 0, may hold values from 0 to 7, never falling along the last dimension, each value on 1 to 3072 neighbouring positions
Outputs:
- mixed: bfloat16 [8192, 4096], P(('groups', 'ctx')), parts along dimension 0
There are 2 independent parts, one for each index of `groups`. A program takes and returns all parts, laid end to end along the dimension named above; an argument that names none is the same for every part. Nothing has to cross between parts.
Inputs may be any that keep to these rules, and one draw needn't show every extreme that they name: Positive decay rates, at most 1 / 30. `segment_ids`: never falling, starting at record 0, which continues the record that closes the earlier span; each record holds at most 3072 tokens, one exactly that many.
All inputs are finite; a program needn't handle non-finite values.
Results may differ from a plain program's by a relative error of at most 0.0065.
Values may be sent and summed in bfloat16 or wider, within the bound.
No kernel may reach another device: no remote copies, remote signals or barrier semaphores. Data moves between devices by JAX's collectives and lax.ppermute only.
A program may use at most 128 MiB of HBM per device.

v0:
```python
import jax
import jax.numpy as jnp
from jax import lax
from jax.sharding import PartitionSpec as P


def shifted(value, axis, steps):
    count = lax.axis_size(axis)
    first, last = (max(0, -steps), min(count, count - steps))
    return lax.ppermute(value, axis, [(source, source + steps) for source in range(first, last)])


def short_filter(rows_ext, short_weight, seg_ext):
    count = rows_ext.shape[0] - 2
    total = jnp.zeros((count,) + rows_ext.shape[1:], jnp.float32)
    for offset in range(short_weight.shape[0]):
        begin = 2 - offset
        piece = rows_ext[begin : begin + count].astype(jnp.float32)
        keep = seg_ext[begin : begin + count] == seg_ext[2:]
        total = total + short_weight[offset][None] * jnp.where(
            keep[:, None, None], piece, jnp.float32(0.0)
        )
    return total


def local_conv(u_block, seg_blk, residues, rates):
    count, width = u_block.shape
    groups, modes = rates.shape
    members = width // groups
    step_groups = min(groups, 16)
    rounds = groups // step_groups
    places = jnp.arange(count, dtype=jnp.int32)
    keep = (places[:, None] >= places[None, :]) & (seg_blk[:, None] == seg_blk[None, :])
    steps_f = places.astype(jnp.float32)
    weight_mode = residues * jnp.sqrt(rates)
    grouped = u_block.reshape(count, rounds, step_groups, members).transpose(1, 0, 2, 3)
    rate_steps = rates.reshape(rounds, step_groups, modes)
    weight_steps = weight_mode.reshape(rounds, step_groups, modes)

    def one_step(triple):
        rate_now, weight_now, values = triple
        falling = weight_now[:, :, None] * jnp.exp(-rate_now[:, :, None] * steps_f[None, None, :])
        rising = jnp.exp(rate_now[:, :, None] * steps_f[None, None, :])
        matrix = jnp.einsum("gmt,gms->gts", falling, rising, precision=lax.Precision.HIGHEST)
        matrix = jnp.where(keep[None], matrix, jnp.float32(0.0)).astype(jnp.bfloat16)
        return jnp.einsum("gts,sgf->tgf", matrix, values, preferred_element_type=jnp.float32)

    result = lax.map(one_step, (rate_steps, weight_steps, grouped))
    return result.transpose(1, 0, 2, 3).reshape(count, width)


def block_state(u_block, seg_blk, seg_prev, rates):
    count, width = u_block.shape
    groups = rates.shape[0]
    members = width // groups
    lags_end = (count - 1 - jnp.arange(count)).astype(jnp.float32)
    keep_end = seg_blk == seg_blk[count - 1]
    decay = jnp.where(
        keep_end[None, None, :],
        jnp.exp(-rates[:, :, None] * lags_end[None, None, :]),
        jnp.float32(0.0),
    )
    decay = decay.astype(jnp.bfloat16)
    grouped = u_block.reshape(count, groups, members)
    block_sum = jnp.einsum("gms,sgf->mgf", decay, grouped, preferred_element_type=jnp.float32)
    factor = jnp.where(seg_prev == seg_blk[count - 1], jnp.exp(-rates * count), jnp.float32(0.0))
    return (factor.T[:, :, None], block_sum)


def cross_term(state_in, seg_blk, seg_prev, residues, rates):
    count = seg_blk.shape[0]
    offsets = jnp.arange(1, count + 1).astype(jnp.float32)
    weights = (residues * jnp.sqrt(rates))[None] * jnp.exp(-rates[None] * offsets[:, None, None])
    weights = jnp.where((seg_blk == seg_prev)[:, None, None], weights, jnp.float32(0.0))
    result = jnp.einsum("tgm,mgf->tgf", weights, state_in, precision=lax.Precision.HIGHEST)
    return result.reshape(count, -1)


def body(features, short_weight, residues, rates, skip, carry_state, earlier_rows, segment_ids):
    count = features.shape[0]
    width = features.shape[2]
    groups, modes = rates.shape
    members = width // groups
    seq_total = segment_ids.shape[0]
    position = lax.axis_index("ctx")
    first = position * count
    tail_rows = shifted(features[count - 2 :], "ctx", 1)
    previous = jnp.where(position == 0, earlier_rows, tail_rows)
    spots = first - 2 + jnp.arange(count + 2, dtype=jnp.int32)
    seg_ext = segment_ids[jnp.maximum(spots, 0)]
    seg_blk = seg_ext[2:]
    seg_prev = seg_ext[1]
    extended = jnp.concatenate([previous, features], axis=0)
    filtered = short_filter(extended, short_weight, seg_ext)
    u_block = (filtered[:, 1] * filtered[:, 2]).astype(jnp.bfloat16)
    factor, block_sum = block_state(u_block, seg_blk, seg_prev, rates)
    carry_modes = carry_state.reshape(modes, groups, members)
    piece = lax.all_gather(block_sum[None], "ctx", axis=0, tiled=True)
    number = piece.shape[0]
    owners = jnp.arange(number, dtype=jnp.int32)
    ends = segment_ids[jnp.clip((owners + 1) * count - 1, 0, seq_total - 1)]
    distance = jnp.maximum(position - 1 - owners, 0).astype(jnp.float32)
    usable = (owners < position) & (ends == seg_prev)
    weights = jnp.where(
        usable[:, None, None],
        jnp.exp(-rates[None] * count * distance[:, None, None]),
        jnp.float32(0.0),
    )
    collected = jnp.einsum("ngm,nmgf->mgf", weights, piece, precision=lax.Precision.HIGHEST)
    reach = (count * position).astype(jnp.float32)
    lead = jnp.where(seg_prev == 0, jnp.exp(-rates * reach), jnp.float32(0.0)).T[:, :, None]
    state_in = lead * carry_modes + collected
    local = local_conv(u_block, seg_blk, residues, rates)
    cross = cross_term(state_in, seg_blk, seg_prev, residues, rates)
    return (filtered[:, 0] * (local + cross + skip[None] * u_block.astype(jnp.float32))).astype(
        jnp.bfloat16
    )


def solution(mesh):
    placed = (
        P(("groups", "ctx"), None, None),
        P(),
        P(),
        P(),
        P(),
        P("groups", None),
        P("groups", None, None),
        P("groups"),
    )
    return jax.shard_map(
        body, mesh=mesh, in_specs=placed, out_specs=P(("groups", "ctx"), None), check_vma=False
    )
```

profile of v0, /device:TPU:0, one launch (start us, length us, event | category | flops | bytes accessed | tf_op | source)
XLA Modules:
  0.0 178.0 jit_solution(13402360730277487780)
XLA Ops:
  19.0 8.7 %copy.47 = bf16[256,3,4096]{0,2,1:T(8,128)(2,1)} copy(bf16[256,3,4096]{2,0,1:T(8,128)(2,1)} %param.10) | data formatting | bytes 12582912 | tf_op args[0]
  38.8 10.6 %multiply_add_fusion = f32[256,3,4096]{0,2,1:T(8,128)S(1)} fusion(bf16[256,3,4096]{0,2,1:T(8,128)(2,1)S(1)} %bitcast.69, bf16[2,3,4096]{0,2,1:T(8,128)(2,1)S(1)} %broadcast_select_fusion, f32[3,4096]{1,0:T(4,128)S(1)} %get-tuple-element.95, f32[3,4096]{1,0:T(4,128)S(1)} %get-tuple-element.96, f32[3,4096]{1,0:T(4,128)S(1)} %get-tuple-element.94, ...), kind=kLoop, calls=%fused_computation.24 | loop fusion | flops 50331648 | bytes 19071488 | tf_op jit(solution)/shard_map/add | solution.py:20
  49.4 4.5 %copy-done.1 = f32[256,3,4096]{0,2,1:T(8,128)} copy-done((f32[256,3,4096]{0,2,1:T(8,128)}, f32[256,3,4096]{0,2,1:T(8,128)S(1)}, u32[]{:S(2)}) %copy-start.1) | copy-done | bytes 12582936
  56.4 3.3 %copy.54 = f32[16,256,16]{1,2,0:T(8,128)} copy(f32[16,256,16]{0,2,1:T(8,128)} %fusion.39) | data formatting | bytes 524288 | tf_op jit(solution)/shard_map/gms,sgf->mgf/transpose | solution.py:65
  59.7 89.9 %while.12 = (s32[]{:T(128)}, f32[16,256,16,16]{1,3,2,0:T(8,128)}, bf16[16,256,16,16]{1,3,2,0:T(8,128)(2,1)S(1)}, f32[16,16,16]{2,1,0:T(8,128)S(1)}, f32[16,16,16]{2,1,0:T(8,128)S(1)}, /*index=5*/s32[256]{0:T(256)S(1)}, s32[]{:T(128)}) while((s32[]{:T(128)}, f32[16,256,16,16]{1,3,2,0:T(8,128)}, ...), condition=%wide.region_1.2_spmd.clone.clone, body=%wide.region_0.1_spmd.clone.clone.sunk | while | flops 237371904 | bytes 4730973 | solution.py:48
  59.9 4.1 %select_convert_fusion.6 = bf16[16,256,256]{2,1,0:T(8,128)(2,1)S(1)} fusion(pred[256,256]{1,0:T(8,128)(4,1)S(1)} %fusion.58, f32[16,16]{1,0:T(8,128)S(1)} %get-tuple-element.146, f32[256]{0:T(256)S(1)} %iota_convert_fusion.2, f32[16,16]{1,0:T(8,128)S(1)} %get-tuple-element.147, f32[16,16]{1,0:T(8,128)S(1)} %dynamic-slice_bitcast_fusion.4), kind=kOutput, calls=%fused_computation.4.clone.1 | convolution fusion | flops 203620352 | bytes 2166784 | tf_op jit(solution)/shard_map/while/body/eval_jaxpr/gmt,gms->gts/dot_general | solution.py:44
  65.5 4.1 %select_convert_fusion.6 = bf16[16,256,256]{2,1,0:T(8,128)(2,1)S(1)} fusion(pred[256,256]{1,0:T(8,128)(4,1)S(1)} %fusion.58, f32[16,16]{1,0:T(8,128)S(1)} %get-tuple-element.146, f32[256]{0:T(256)S(1)} %iota_convert_fusion.2, f32[16,16]{1,0:T(8,128)S(1)} %get-tuple-element.147, f32[16,16]{1,0:T(8,128)S(1)} %dynamic-slice_bitcast_fusion.4), kind=kOutput, calls=%fused_computation.4.clone.1 | convolution fusion | flops 203620352 | bytes 2166784 | tf_op jit(solution)/shard_map/while/body/eval_jaxpr/gmt,gms->gts/dot_general | solution.py:44
  71.1 4.1 %select_convert_fusion.6 = bf16[16,256,256]{2,1,0:T(8,128)(2,1)S(1)} fusion(pred[256,256]{1,0:T(8,128)(4,1)S(1)} %fusion.58, f32[16,16]{1,0:T(8,128)S(1)} %get-tuple-element.146, f32[256]{0:T(256)S(1)} %iota_convert_fusion.2, f32[16,16]{1,0:T(8,128)S(1)} %get-tuple-element.147, f32[16,16]{1,0:T(8,128)S(1)} %dynamic-slice_bitcast_fusion.4), kind=kOutput, calls=%fused_computation.4.clone.1 | convolution fusion | flops 203620352 | bytes 2166784 | tf_op jit(solution)/shard_map/while/body/eval_jaxpr/gmt,gms->gts/dot_general | solution.py:44
  76.7 4.1 %select_convert_fusion.6 = bf16[16,256,256]{2,1,0:T(8,128)(2,1)S(1)} fusion(pred[256,256]{1,0:T(8,128)(4,1)S(1)} %fusion.58, f32[16,16]{1,0:T(8,128)S(1)} %get-tuple-element.146, f32[256]{0:T(256)S(1)} %iota_convert_fusion.2, f32[16,16]{1,0:T(8,128)S(1)} %get-tuple-element.147, f32[16,16]{1,0:T(8,128)S(1)} %dynamic-slice_bitcast_fusion.4), kind=kOutput, calls=%fused_computation.4.clone.1 | convolution fusion | flops 203620352 | bytes 2166784 | tf_op jit(solution)/shard_map/while/body/eval_jaxpr/gmt,gms->gts/dot_general | solution.py:44
  82.3 4.1 %select_convert_fusion.6 = bf16[16,256,256]{2,1,0:T(8,128)(2,1)S(1)} fusion(pred[256,256]{1,0:T(8,128)(4,1)S(1)} %fusion.58, f32[16,16]{1,0:T(8,128)S(1)} %get-tuple-element.146, f32[256]{0:T(256)S(1)} %iota_convert_fusion.2, f32[16,16]{1,0:T(8,128)S(1)} %get-tuple-element.147, f32[16,16]{1,0:T(8,128)S(1)} %dynamic-slice_bitcast_fusion.4), kind=kOutput, calls=%fused_computation.4.clone.1 | convolution fusion | flops 203620352 | bytes 2166784 | tf_op jit(solution)/shard_map/while/body/eval_jaxpr/gmt,gms->gts/dot_general | solution.py:44
  88.0 4.1 %select_convert_fusion.6 = bf16[16,256,256]{2,1,0:T(8,128)(2,1)S(1)} fusion(pred[256,256]{1,0:T(8,128)(4,1)S(1)} %fusion.58, f32[16,16]{1,0:T(8,128)S(1)} %get-tuple-element.146, f32[256]{0:T(256)S(1)} %iota_convert_fusion.2, f32[16,16]{1,0:T(8,128)S(1)} %get-tuple-element.147, f32[16,16]{1,0:T(8,128)S(1)} %dynamic-slice_bitcast_fusion.4), kind=kOutput, calls=%fused_computation.4.clone.1 | convolution fusion | flops 203620352 | bytes 2166784 | tf_op jit(solution)/shard_map/while/body/eval_jaxpr/gmt,gms->gts/dot_general | solution.py:44
  93.6 4.1 %select_convert_fusion.6 = bf16[16,256,256]{2,1,0:T(8,128)(2,1)S(1)} fusion(pred[256,256]{1,0:T(8,128)(4,1)S(1)} %fusion.58, f32[16,16]{1,0:T(8,128)S(1)} %get-tuple-element.146, f32[256]{0:T(256)S(1)} %iota_convert_fusion.2, f32[16,16]{1,0:T(8,128)S(1)} %get-tuple-element.147, f32[16,16]{1,0:T(8,128)S(1)} %dynamic-slice_bitcast_fusion.4), kind=kOutput, calls=%fused_computation.4.clone.1 | convolution fusion | flops 203620352 | bytes 2166784 | tf_op jit(solution)/shard_map/while/body/eval_jaxpr/gmt,gms->gts/dot_general | solution.py:44
  99.2 4.1 %select_convert_fusion.6 = bf16[16,256,256]{2,1,0:T(8,128)(2,1)S(1)} fusion(pred[256,256]{1,0:T(8,128)(4,1)S(1)} %fusion.58, f32[16,16]{1,0:T(8,128)S(1)} %get-tuple-element.146, f32[256]{0:T(256)S(1)} %iota_convert_fusion.2, f32[16,16]{1,0:T(8,128)S(1)} %get-tuple-element.147, f32[16,16]{1,0:T(8,128)S(1)} %dynamic-slice_bitcast_fusion.4), kind=kOutput, calls=%fused_computation.4.clone.1 | convolution fusion | flops 203620352 | bytes 2166784 | tf_op jit(solution)/shard_map/while/body/eval_jaxpr/gmt,gms->gts/dot_general | solution.py:44
  104.9 4.1 %select_convert_fusion.6 = bf16[16,256,256]{2,1,0:T(8,128)(2,1)S(1)} fusion(pred[256,256]{1,0:T(8,128)(4,1)S(1)} %fusion.58, f32[16,16]{1,0:T(8,128)S(1)} %get-tuple-element.146, f32[256]{0:T(256)S(1)} %iota_convert_fusion.2, f32[16,16]{1,0:T(8,128)S(1)} %get-tuple-element.147, f32[16,16]{1,0:T(8,128)S(1)} %dynamic-slice_bitcast_fusion.4), kind=kOutput, calls=%fused_computation.4.clone.1 | convolution fusion | flops 203620352 | bytes 2166784 | tf_op jit(solution)/shard_map/while/body/eval_jaxpr/gmt,gms->gts/dot_general | solution.py:44
  110.5 4.1 %select_convert_fusion.6 = bf16[16,256,256]{2,1,0:T(8,128)(2,1)S(1)} fusion(pred[256,256]{1,0:T(8,128)(4,1)S(1)} %fusion.58, f32[16,16]{1,0:T(8,128)S(1)} %get-tuple-element.146, f32[256]{0:T(256)S(1)} %iota_convert_fusion.2, f32[16,16]{1,0:T(8,128)S(1)} %get-tuple-element.147, f32[16,16]{1,0:T(8,128)S(1)} %dynamic-slice_bitcast_fusion.4), kind=kOutput, calls=%fused_computation.4.clone.1 | convolution fusion | flops 203620352 | bytes 2166784 | tf_op jit(solution)/shard_map/while/body/eval_jaxpr/gmt,gms->gts/dot_general | solution.py:44
  116.1 4.1 %select_convert_fusion.6 = bf16[16,256,256]{2,1,0:T(8,128)(2,1)S(1)} fusion(pred[256,256]{1,0:T(8,128)(4,1)S(1)} %fusion.58, f32[16,16]{1,0:T(8,128)S(1)} %get-tuple-element.146, f32[256]{0:T(256)S(1)} %iota_convert_fusion.2, f32[16,16]{1,0:T(8,128)S(1)} %get-tuple-element.147, f32[16,16]{1,0:T(8,128)S(1)} %dynamic-slice_bitcast_fusion.4), kind=kOutput, calls=%fused_computation.4.clone.1 | convolution fusion | flops 203620352 | bytes 2166784 | tf_op jit(solution)/shard_map/while/body/eval_jaxpr/gmt,gms->gts/dot_general | solution.py:44
  121.7 4.1 %select_convert_fusion.6 = bf16[16,256,256]{2,1,0:T(8,128)(2,1)S(1)} fusion(pred[256,256]{1,0:T(8,128)(4,1)S(1)} %fusion.58, f32[16,16]{1,0:T(8,128)S(1)} %get-tuple-element.146, f32[256]{0:T(256)S(1)} %iota_convert_fusion.2, f32[16,16]{1,0:T(8,128)S(1)} %get-tuple-element.147, f32[16,16]{1,0:T(8,128)S(1)} %dynamic-slice_bitcast_fusion.4), kind=kOutput, calls=%fused_computation.4.clone.1 | convolution fusion | flops 203620352 | bytes 2166784 | tf_op jit(solution)/shard_map/while/body/eval_jaxpr/gmt,gms->gts/dot_general | solution.py:44
  127.3 4.1 %select_convert_fusion.6 = bf16[16,256,256]{2,1,0:T(8,128)(2,1)S(1)} fusion(pred[256,256]{1,0:T(8,128)(4,1)S(1)} %fusion.58, f32[16,16]{1,0:T(8,128)S(1)} %get-tuple-element.146, f32[256]{0:T(256)S(1)} %iota_convert_fusion.2, f32[16,16]{1,0:T(8,128)S(1)} %get-tuple-element.147, f32[16,16]{1,0:T(8,128)S(1)} %dynamic-slice_bitcast_fusion.4), kind=kOutput, calls=%fused_computation.4.clone.1 | convolution fusion | flops 203620352 | bytes 2166784 | tf_op jit(solution)/shard_map/while/body/eval_jaxpr/gmt,gms->gts/dot_general | solution.py:44
  132.9 4.1 %select_convert_fusion.6 = bf16[16,256,256]{2,1,0:T(8,128)(2,1)S(1)} fusion(pred[256,256]{1,0:T(8,128)(4,1)S(1)} %fusion.58, f32[16,16]{1,0:T(8,128)S(1)} %get-tuple-element.146, f32[256]{0:T(256)S(1)} %iota_convert_fusion.2, f32[16,16]{1,0:T(8,128)S(1)} %get-tuple-element.147, f32[16,16]{1,0:T(8,128)S(1)} %dynamic-slice_bitcast_fusion.4), kind=kOutput, calls=%fused_computation.4.clone.1 | convolution fusion | flops 203620352 | bytes 2166784 | tf_op jit(solution)/shard_map/while/body/eval_jaxpr/gmt,gms->gts/dot_general | solution.py:44
  138.5 4.1 %select_convert_fusion.6 = bf16[16,256,256]{2,1,0:T(8,128)(2,1)S(1)} fusion(pred[256,256]{1,0:T(8,128)(4,1)S(1)} %fusion.58, f32[16,16]{1,0:T(8,128)S(1)} %get-tuple-element.146, f32[256]{0:T(256)S(1)} %iota_convert_fusion.2, f32[16,16]{1,0:T(8,128)S(1)} %get-tuple-element.147, f32[16,16]{1,0:T(8,128)S(1)} %dynamic-slice_bitcast_fusion.4), kind=kOutput, calls=%fused_computation.4.clone.1 | convolution fusion | flops 203620352 | bytes 2166784 | tf_op jit(solution)/shard_map/while/body/eval_jaxpr/gmt,gms->gts/dot_general | solution.py:44
  144.2 4.1 %select_convert_fusion.6 = bf16[16,256,256]{2,1,0:T(8,128)(2,1)S(1)} fusion(pred[256,256]{1,0:T(8,128)(4,1)S(1)} %fusion.58, f32[16,16]{1,0:T(8,128)S(1)} %get-tuple-element.146, f32[256]{0:T(256)S(1)} %iota_convert_fusion.2, f32[16,16]{1,0:T(8,128)S(1)} %get-tuple-element.147, f32[16,16]{1,0:T(8,128)S(1)} %dynamic-slice_bitcast_fusion.4), kind=kOutput, calls=%fused_computation.4.clone.1 | convolution fusion | flops 203620352 | bytes 2166784 | tf_op jit(solution)/shard_map/while/body/eval_jaxpr/gmt,gms->gts/dot_general | solution.py:44
  149.6 3.0 %multiply_reduce_fusion = f32[16,256,16]{1,2,0:T(8,128)S(1)} fusion(f32[16,256,16,16]{1,3,0,2:T(8,128)} %bitcast.70, f32[16,256,16]{1,0,2:T(8,128)S(1)} %select_bitcast_fusion), kind=kLoop, calls=%fused_computation.37 | loop fusion | flops 2031616 | bytes 4718592
  156.7 6.3 %fusion.23 = f32[256,16,256]{2,1,0:T(8,128)S(1)} fusion(f32[16,256,16]{2,1,0:T(8,128)S(1)} %multiply_add_fusion.1, f32[256]{0:T(256)S(1)} %add_convert_fusion, f32[256,16]{1,0:T(8,128)S(1)} %copy.53, f32[256,16]{1,0:T(8,128)S(1)} %bitcast.74, pred[256]{0:T(512)(128)(4,1)S(1)} %get-tuple-element.101), kind=kOutput, calls=%fused_computation.38 | convolution fusion | flops 204472320 | bytes 4490496 | tf_op jit(solution)/shard_map/tgm,mgf->tgf/dot_general | solution.py:75
  163.1 5.3 %fusion.21 = bf16[256,4096]{0,1:T(8,128)(2,1)S(1)} fusion(f32[256,3,4096]{0,2,1:T(8,128)} %copy-done.1, f32[256,16,256]{2,1,0:T(8,128)S(1)} %fusion.23, f32[16,256,16,16]{1,3,2,0:T(8,128)S(1)} %copy-done.3, f32[4096]{0:T(1024)S(1)} %copy-done.6), kind=kLoop, calls=%fused_computation.33 | loop fusion | flops 8388608 | bytes 23085056 | tf_op jit(solution)/shard_map/convert_element_type | solution.py:115
  (133 shorter events, 56.0 us)
Async XLA Ops:
  6.5 3.5 %copy-start = (s32[4096]{0:T(1024)S(1)}, s32[4096]{0:T(1024)}, u32[]{:S(2)}) copy-start(s32[4096]{0:T(1024)} %param.17) | copy-start | bytes 49156
  6.5 143.1 %all-gather.3.cloned.1.call-start = ((), (), s32[]{:S(2)}) async-start(), calls=%async_computation | async-start | bytes 4456448 | tf_op jit(solution)/shard_map/all_gather | solution.py:98
  7.5 25.3 %collective-permute-start = (bf16[2,3,4096]{2,0,1:T(2,128)(2,1)S(1)}, bf16[2,3,4096]{2,0,1:T(2,128)(2,1)S(1)}, u32[]{:S(2)}, u32[]{:S(2)}) collective-permute-start(bf16[2,3,4096]{2,0,1:T(2,128)(2,1)S(1)} %slice.51), channel_id=1, source_target_pairs={{0,1},{1,2},{2,3},{3,4},{4,5},{5,6},{6,7},{7,8},{8,9},{9,10},{10,1... | collective-permute-start | bytes 147464 | tf_op jit(solution)/shard_map/ppermute | solution.py:10
  18.9 8.9 %copy-start.4 = (f32[16,4096]{1,0:T(8,128)S(1)}, f32[16,4096]{1,0:T(8,128)}, u32[]{:S(2)}) copy-start(f32[16,4096]{1,0:T(8,128)} %param.15) | copy-start | bytes 786436
  18.9 11.0 %copy-start.5 = (bf16[2,3,4096]{2,0,1:T(2,128)(2,1)S(1)}, bf16[2,3,4096]{2,0,1:T(2,128)(2,1)}, u32[]{:S(2)}) copy-start(bf16[2,3,4096]{2,0,1:T(2,128)(2,1)} %param.16) | copy-start | bytes 147460
  32.8 5.2 %slice-start = ((s8[6291456]{0:T(1024)(128)(4,1)}), s8[2097152]{0:T(1024)(128)(4,1)S(1)}, s32[]{:S(2)}) async-start(s8[6291456]{0:T(1024)(128)(4,1)} %bitcast.68), calls=%async_computation.1 | async-start | bytes 4194304
  35.6 3.1 %slice-start.1 = ((s8[6291456]{0:T(1024)(128)(4,1)}), s8[4194304]{0:T(1024)(128)(4,1)S(1)}, s32[]{:S(2)}) async-start(s8[6291456]{0:T(1024)(128)(4,1)} %bitcast.68), calls=%async_computation.2 | async-start | bytes 8388608
  49.4 4.5 %copy-start.1 = (f32[256,3,4096]{0,2,1:T(8,128)}, f32[256,3,4096]{0,2,1:T(8,128)S(1)}, u32[]{:S(2)}) copy-start(f32[256,3,4096]{0,2,1:T(8,128)S(1)} %multiply_add_fusion) | copy-start | bytes 37748740
  149.6 4.9 %copy-start.2 = (f32[16,256,16]{2,1,0:T(8,128)S(1)}, f32[16,256,16]{2,1,0:T(8,128)}, u32[]{:S(2)}) copy-start(f32[16,256,16]{2,1,0:T(8,128)} %reshape.119) | copy-start | bytes 786436
  156.7 6.4 %copy-start.3 = (f32[16,256,16,16]{1,3,2,0:T(8,128)S(1)}, f32[16,256,16,16]{1,3,2,0:T(8,128)}, u32[]{:S(2)}) copy-start(f32[16,256,16,16]{1,3,2,0:T(8,128)} %get-tuple-element.45) | copy-start | bytes 12582916
  156.7 6.4 %copy-start.6 = (f32[4096]{0:T(1024)S(1)}, f32[4096]{0:T(1024)}, u32[]{:S(2)}) copy-start(f32[4096]{0:T(1024)} %param.14) | copy-start | bytes 49156
Sparse Core Ops, SparseCore 0:
  59.8 53.3 all-gather.2
where the time goes:
time: 181 us; the launch traced here: 178 us
  matrix products  96.3 us (53%)
  local copies, waits for them, and re-layouts  36.4 us (20%)
  other arithmetic  28.4 us (16%)
  between operations  14.3 us (8%)
  starting transfers between devices  2.36 us (1%)
    dot_general x16, matrix products, one_step(): jnp.einsum('gmt,gms->gts', falling, rising, precision=lax.Precision.HIGHEST)  65.8 us
    dot_general x16, matrix products, one_step(): jnp.einsum('gts,sgf->tgf', matrix, values, preferred_element_type=jnp.flo...  22 us
    unnamed x21, local copies, waits for them, and re-layouts  17.7 us
    add x1, other arithmetic, short_filter(): total + short_weight[offset][None] * jnp.where(keep[:, None, None], piece...  10.6 us
    dot_general x1, matrix products, cross_term(): jnp.einsum('tgm,mgf->tgf', weights, state_in, precision=lax.Precision.HIG...  6.33 us
    convert_element_type x1, other arithmetic, body(): (filtered[:, 0] * (local + cross + skip[None] * u_block.astype(jnp.float3...  5.26 us
  transfers between devices with their start and end apart: 2, of which 0 were waited for; matrix products, arithmetic and copies ran while one was open for 63% of the time, Pallas kernels for 0%

commit v1 on v0

v1 whole, which is shorter than its diff:
```python
import functools

import jax
import jax.numpy as jnp
from jax import lax
from jax.experimental import pallas as pl
from jax.experimental.pallas import tpu as pltpu
from jax.sharding import PartitionSpec as P

BF = jnp.bfloat16
F32 = jnp.float32
LANES = 128
SET = 256
HALF = 128


def iota(shape, dim):
    return lax.broadcasted_iota(jnp.int32, shape, dim)


def split3(x):
    hi = x.astype(BF)
    rest = x - hi.astype(F32)
    mid = rest.astype(BF)
    low = (rest - mid.astype(F32)).astype(BF)
    return [hi, mid, low]


def segment_columns(pos, seg_ref):
    halves, rows = [], []
    for part in range(2):
        row = seg_ref[pl.ds(2 * pos + part, 1), :].astype(F32)
        rows.append(row)
        halves.append(jnp.transpose(jnp.broadcast_to(row, (HALF, LANES))))
    before = seg_ref[pl.ds(jnp.maximum(2 * pos - 1, 0), 1), :].astype(F32)
    before = jnp.where(pos == 0, jnp.zeros_like(before), before)
    last = jnp.broadcast_to(before[:, LANES - 1 :], (1, LANES))
    second = jnp.broadcast_to(before[:, LANES - 2 : LANES - 1], (1, LANES))
    return jnp.concatenate(halves, axis=0), rows, last, second


def first_kernel(pos_ref, seg_ref, rates_ref, res_ref, k_ref, v_ref, sw_ref,
                 u_ref, sum_ref, rate_ref, rflat_ref, wflat_ref, col_ref, tri_ref, keep_ref):
    step = pl.program_id(0)
    pos = pos_ref[0]
    count = k_ref.shape[0]
    modes = rates_ref.shape[0]
    members = SET // modes

    @pl.when(step == 0)
    def _():
        col, rows, last, second = segment_columns(pos, seg_ref)
        token = iota((count, LANES), 0)
        one = jnp.where(token == 0, last, pltpu.roll(col, 1, 0))
        two = jnp.where(token == 0, second, jnp.where(token == 1, last, pltpu.roll(col, 2, 0)))
        col_ref[0] = (col == one).astype(F32)
        col_ref[1] = (col == two).astype(F32)
        col_ref[2] = (col == last).astype(F32)
        end = jnp.broadcast_to(rows[1][:, LANES - 1 :], (1, LANES))
        keep_ref[...] = (col == end).astype(F32)
        t = iota((HALF, HALF), 0)
        s = iota((HALF, HALF), 1)
        same = [[col[a * HALF : (a + 1) * HALF] == rows[b] for b in range(2)] for a in range(2)]
        tri_ref[0] = ((t >= s) & same[0][0]).astype(F32).astype(BF)
        tri_ref[1] = ((t >= s) & same[1][0]).astype(F32).astype(BF)
        tri_ref[2] = ((t < s) & same[1][0]).astype(F32).astype(BF)
        tri_ref[3] = ((t >= s) & same[1][1]).astype(F32).astype(BF)

    spot = iota((LANES, SET), 0)
    lane = iota((LANES, SET), 1)
    onehot = (spot == lane // members + members * lax.rem(step, LANES // members)).astype(F32).astype(BF)
    rates = rates_ref[...]
    weight = res_ref[...] * jnp.sqrt(rates)
    spread = jnp.dot(jnp.concatenate(split3(rates) + split3(weight), axis=0), onehot, preferred_element_type=F32)
    rate = (spread[:modes] + spread[modes : 2 * modes]) + spread[2 * modes : 3 * modes]
    wide = (spread[3 * modes : 4 * modes] + spread[4 * modes : 5 * modes]) + spread[5 * modes :]
    rate_ref[...] = rate
    pick = iota((modes, SET), 0) == lax.rem(iota((modes, SET), 1), modes)
    rflat = jnp.sum(jnp.where(pick, rate, 0.0), axis=0, keepdims=True)
    wflat = jnp.sum(jnp.where(pick, wide, 0.0), axis=0, keepdims=True)
    rflat_ref[...] = rflat
    wflat_ref[...] = wflat

    token = iota((count, LANES), 0)
    one = col_ref[0]
    two = col_ref[1]
    pieces = []
    for half in range(SET // LANES):
        at = slice(half * LANES, (half + 1) * LANES)
        made = []
        for index, ref in ((1, k_ref), (2, v_ref)):
            x = ref[:, at].astype(F32)
            made.append(
                sw_ref[index, 0:1, at] * x
                + sw_ref[index, 1:2, at] * (one * pltpu.roll(x, 1, 0))
                + sw_ref[index, 2:3, at] * (two * pltpu.roll(x, 2, 0))
            )
        pieces.append(jnp.where(token < 2, 0.0, made[0] * made[1]).astype(BF))
    u = jnp.concatenate(pieces, axis=1)
    u_ref[...] = u

    fine = iota((16, SET), 0).astype(F32)
    coarse = jnp.exp(-rflat * (count - 16.0 - 16.0 * fine))
    fine = jnp.exp(-rflat * (15.0 - fine))
    keep = keep_ref[...]
    keep = jnp.concatenate([keep] * (SET // LANES), axis=1)
    decay = jnp.concatenate([coarse[a : a + 1] * fine for a in range(count // 16)], axis=0)
    decay = (decay * keep).astype(BF)
    sums = lax.dot_general(decay, u, (((0,), (0,)), ((), ())), preferred_element_type=F32)
    owner = iota((modes, SET), 1) // members
    total = jnp.zeros((modes, SET), F32)
    for g in range(SET // members):
        total = jnp.where(owner == g, sums[g * modes : (g + 1) * modes], total)
    sum_ref[...] = total


def head_kernel(pos_ref, seg_ref, feat_ref, halo_ref, sw_ref, rate_ref, sum_ref, total_ref, head_ref):
    pos = pos_ref[0]
    width = rate_ref.shape[1]
    count = 2 * LANES
    row = seg_ref[pl.ds(2 * pos, 1), :].astype(F32)
    tail = seg_ref[pl.ds(2 * pos + 1, 1), :].astype(F32)
    before = seg_ref[pl.ds(jnp.maximum(2 * pos - 1, 0), 1), :].astype(F32)
    before = jnp.where(pos == 0, jnp.zeros_like(before), before)
    s0, s1 = row[:, 0:1], row[:, 1:2]
    end = tail[:, LANES - 1 :]
    p1, p2 = before[:, LANES - 1 :], before[:, LANES - 2 : LANES - 1]

    def same(a, b):
        return jnp.broadcast_to((a == b).astype(F32), (1, width))

    made = []
    for index in (1, 2):
        x = feat_ref[index].astype(F32)
        h = halo_ref[index].astype(F32)
        x0, x1 = x[0:1], x[1:2]
        h2, h1 = h[0:1], h[1:2]
        w = [sw_ref[index, j : j + 1, :] for j in range(3)]
        f0 = w[0] * x0 + w[1] * (same(p1, s0) * h1) + w[2] * (same(p2, s0) * h2)
        f1 = w[0] * x1 + w[1] * (same(s0, s1) * x0) + w[2] * (same(p1, s1) * h1)
        made.append((f0, f1))
    u0 = (made[0][0] * made[1][0]).astype(BF).astype(F32)
    u1 = (made[0][1] * made[1][1]).astype(BF).astype(F32)
    head_ref[0:1, :] = u0
    head_ref[1:2, :] = u1
    rate = rate_ref[...]
    total = sum_ref[...]
    total = total + jnp.exp(-rate * (count - 1.0)) * (same(s0, end) * u0)
    total = total + jnp.exp(-rate * (count - 2.0)) * (same(s1, end) * u1)
    half = width // 2
    total_ref[0] = total[:, :half].astype(BF)
    total_ref[1] = total[:, half:].astype(BF)


def local_kernel(u_ref, head_ref, q_ref, halo_ref, sw_ref, skip_ref, rates_ref, res_ref, rflat_ref, wflat_ref,
                 col_ref, tri_ref, out_ref, gate_ref, cross_ref, top_ref, low_ref, rhs_ref):
    count = u_ref.shape[0]
    modes = rates_ref.shape[1]
    members = LANES // rates_ref.shape[0]
    groups = rates_ref.shape[0]
    rates = rates_ref[...]
    weight = res_ref[...] * jnp.sqrt(rates)
    lane = iota((groups, LANES), 1)
    lag = jnp.where(lane == 0, 0, LANES - lane).astype(F32)
    near = jnp.zeros((groups, LANES), F32)
    far = jnp.zeros((groups, LANES), F32)
    for m in range(modes):
        r = rates[:, m : m + 1]
        table = weight[:, m : m + 1] * jnp.exp(-r * lag)
        near = near + table
        far = far + weight[:, m : m + 1] * jnp.exp(-r * (lag + LANES))
    token = iota((count, LANES), 0)
    u = u_ref[...].astype(F32)
    u = jnp.where(token == 0, head_ref[0:1, :], jnp.where(token == 1, head_ref[1:2, :], u))
    ub = u.astype(BF)
    owner = iota((1, LANES), 1) // members
    for g in range(groups):
        first = pltpu.roll(jnp.broadcast_to(near[g : g + 1], (HALF, LANES)), 0, 1, stride=1, stride_axis=0).astype(BF)
        second = pltpu.roll(jnp.broadcast_to(far[g : g + 1], (HALF, LANES)), 0, 1, stride=1, stride_axis=0).astype(BF)
        at = slice(g * HALF, (g + 1) * HALF)
        top_ref[0:HALF, at] = first * tri_ref[0]
        top_ref[HALF:, at] = second * tri_ref[1] + first * tri_ref[2]
        low_ref[:, at] = first * tri_ref[3]
        mine = jnp.broadcast_to((owner == g).astype(F32), (HALF, LANES)).astype(BF)
        rhs_ref[g * HALF : (g + 1) * HALF, :] = ub[:HALF] * mine
        rhs_ref[(groups + g) * HALF : (groups + g + 1) * HALF, :] = ub[HALF:] * mine
    depth = groups * HALF
    upper = jnp.dot(top_ref[...], rhs_ref[:depth, :], preferred_element_type=F32)
    lower = jnp.dot(low_ref[...], rhs_ref[depth:, :], preferred_element_type=F32)
    x = q_ref[...].astype(F32)
    h = halo_ref[...].astype(F32)
    one = jnp.where(token == 0, h[1:2], pltpu.roll(x, 1, 0))
    two = jnp.where(token == 0, h[0:1], jnp.where(token == 1, h[1:2], pltpu.roll(x, 2, 0)))
    q = sw_ref[0, 0:1] * x + sw_ref[0, 1:2] * (col_ref[0] * one) + sw_ref[0, 2:3] * (col_ref[1] * two)
    gate_ref[...] = q
    base = skip_ref[...] * u
    out_ref[:HALF] = q[:HALF] * (upper[:HALF] + base[:HALF])
    out_ref[HALF:] = q[HALF:] * (upper[HALF:] + lower + base[HALF:])
    rflat = rflat_ref[...]
    fine = iota((16, LANES), 0).astype(F32)
    coarse = wflat_ref[...] * jnp.exp(-rflat * (16.0 * fine))
    fine = jnp.exp(-rflat * (fine + 1.0))
    table = jnp.concatenate([coarse[a : a + 1] * fine for a in range(count // 16)], axis=0)
    cross_ref[...] = (table * col_ref[2]).astype(BF)


def last_kernel(state_ref, table_ref, gate_ref, part_ref, out_ref):
    modes = state_ref.shape[0]
    groups = SET // modes
    state = state_ref[...]
    owner = iota((modes, SET), 1) // (SET // groups)
    spread = jnp.concatenate([jnp.where(owner == g, state, 0.0).astype(BF) for g in range(groups)], axis=0)
    cross = jnp.dot(table_ref[...], spread, preferred_element_type=F32)
    out_ref[...] = (part_ref[...] + gate_ref[...] * cross).astype(BF)


def params(limit=None):
    return pltpu.CompilerParams(vmem_limit_bytes=limit or (16 << 20))


def fixed(shape):
    return pl.BlockSpec(shape, lambda i, *_: (0,) * len(shape))


def body(features, short_weight, residues, rates, skip, carry_state, earlier_rows, segment_ids):
    count, _, width = features.shape
    groups, modes = rates.shape
    blocks = lax.axis_size("ctx")
    pos = lax.axis_index("ctx")
    pos1 = pos.reshape(1)
    feat = jnp.transpose(features, (1, 0, 2))
    taps = jnp.transpose(short_weight, (1, 0, 2))
    segs = segment_ids.reshape(-1, LANES)
    rates_t = rates.T
    res_t = residues.T
    skip = skip.reshape(1, width)

    halo = lax.ppermute(feat[:, count - 2 :], "ctx", [(i, i + 1) for i in range(blocks - 1)])
    halo = jnp.where(pos == 0, jnp.transpose(earlier_rows, (1, 0, 2)), halo)

    sets = width // SET
    per = LANES // (groups // sets)
    lane_out = lambda rows, dt: jax.ShapeDtypeStruct((rows, width), dt)
    lane_spec = lambda rows, size: pl.BlockSpec((rows, size), lambda i, *_: (0, i))
    u, sums, rate, rflat, wflat, cols, tris = pl.pallas_call(
        first_kernel,
        grid_spec=pltpu.PrefetchScalarGridSpec(
            num_scalar_prefetch=1,
            grid=(sets,),
            in_specs=[
                fixed(segs.shape),
                pl.BlockSpec((modes, LANES), lambda i, *_: (0, i // per)),
                pl.BlockSpec((modes, LANES), lambda i, *_: (0, i // per)),
                pl.BlockSpec((None, count, SET), lambda i, *_: (1, 0, i)),
                pl.BlockSpec((None, count, SET), lambda i, *_: (2, 0, i)),
                pl.BlockSpec((3, 3, SET), lambda i, *_: (0, 0, i)),
            ],
            out_specs=[
                lane_spec(count, SET),
                lane_spec(modes, SET),
                lane_spec(modes, SET),
                lane_spec(1, SET),
                lane_spec(1, SET),
                fixed((3, count, LANES)),
                fixed((4, HALF, HALF)),
            ],
            scratch_shapes=[pltpu.VMEM((count, LANES), F32)],
        ),
        out_shape=[
            lane_out(count, BF),
            lane_out(modes, F32),
            lane_out(modes, F32),
            lane_out(1, F32),
            lane_out(1, F32),
            jax.ShapeDtypeStruct((3, count, LANES), F32),
            jax.ShapeDtypeStruct((4, HALF, HALF), BF),
        ],
        compiler_params=params(),
        name="first",
    )(pos1, segs, rates_t, res_t, feat, feat, taps)

    vm = pl.BlockSpec(memory_space=pltpu.VMEM)
    total, head = pl.pallas_call(
        head_kernel,
        in_specs=[pl.BlockSpec(memory_space=pltpu.SMEM)] + [vm] * 6,
        out_specs=[vm, vm],
        out_shape=[jax.ShapeDtypeStruct((2, modes, width // 2), BF), lane_out(2, F32)],
        compiler_params=params(),
        name="head",
    )(pos1, segs, feat[:, :2], halo, taps, rate, sums)

    def local(piece, pieces, u):
        tiles = width // LANES // pieces
        first = piece * tiles
        size = tiles * LANES
        per_tile = groups // (width // LANES)
        spec = lambda rows: pl.BlockSpec((rows, LANES), lambda i: (0, first + i))
        mine = lambda rows: pl.BlockSpec((rows, LANES), lambda i: (0, i))
        return pl.pallas_call(
            local_kernel,
            grid=(tiles,),
            in_specs=[
                spec(count),
                spec(2),
                pl.BlockSpec((None, count, LANES), lambda i: (0, 0, first + i)),
                pl.BlockSpec((None, 2, LANES), lambda i: (0, 0, first + i)),
                pl.BlockSpec((3, 3, LANES), lambda i: (0, 0, first + i)),
                spec(1),
                pl.BlockSpec((per_tile, modes), lambda i: (first + i, 0)),
                pl.BlockSpec((per_tile, modes), lambda i: (first + i, 0)),
                spec(1),
                spec(1),
                fixed((3, count, LANES)),
                fixed((4, HALF, HALF)),
            ],
            out_specs=[mine(count), mine(count), mine(count)],
            out_shape=[
                jax.ShapeDtypeStruct((count, size), F32),
                jax.ShapeDtypeStruct((count, size), F32),
                jax.ShapeDtypeStruct((count, size), BF),
            ],
            scratch_shapes=[
                pltpu.VMEM((count, per_tile * HALF), BF),
                pltpu.VMEM((HALF, per_tile * HALF), BF),
                pltpu.VMEM((2 * per_tile * HALF, LANES), BF),
            ],
            compiler_params=params(),
            cost_estimate=pl.CostEstimate(flops=tiles * 2 * 400 * 1024 * 256, bytes_accessed=tiles * 600000, transcendentals=0),
            name="local",
        )(u, head, feat, halo, taps, skip, rates, residues, rflat, wflat, cols, tris)

    ends = segment_ids.reshape(blocks, count)[:, count - 1]
    at_end = lambda b: jnp.where(b < 0, 0, lax.dynamic_index_in_dim(ends, jnp.maximum(b, 0), 0, keepdims=False))
    def decay(rate, low, high):
        alive = at_end(low - 1) == at_end(high - 1)
        return jnp.where(alive, jnp.exp(-rate * (count * (high - low)).astype(F32)), 0.0)

    core = pos % 2
    chip = pos // 2
    chips = blocks // 2
    rate2 = rate.reshape(modes, 2, width // 2)
    rate_half = jnp.where(core == 0, rate2[:, 0], rate2[:, 1])
    swap = lambda value: lax.ppermute(value, "ctx", [(i, i ^ 1) for i in range(blocks)])
    pieces = 4
    parts = []
    other = swap(total)
    low_total = jnp.where(core == 0, total, other)
    own_half = lambda value: jnp.where(core == 0, value[0], value[1]).astype(F32)
    t_low = own_half(low_total)
    t_high = own_half(jnp.where(core == 0, other, total))
    chip_total = decay(rate_half, 2 * chip + 1, 2 * chip + 2) * t_low + t_high
    before = jnp.zeros_like(chip_total)
    reach = 1
    while reach < chips:
        sent = chip_total.astype(BF)
        got = lax.ppermute(sent, "ctx", [(i, i ^ (2 * reach)) for i in range(blocks)]).astype(F32)
        base = (chip // reach) * reach
        upper = (chip // reach) % 2 == 1
        mate = jnp.where(upper, base - reach, base + reach)
        before = before + jnp.where(upper, decay(rate_half, 2 * base, 2 * chip), 0.0) * got
        own = jnp.where(upper, 1.0, decay(rate_half, 2 * mate, 2 * mate + 2 * reach))
        theirs = jnp.where(upper, decay(rate_half, 2 * base, 2 * base + 2 * reach), 1.0)
        chip_total = own * chip_total + theirs * got
        reach *= 2
    mine = before.astype(BF)
    yours = swap(mine)
    full = jnp.concatenate([jnp.where(core == 0, mine, yours), jnp.where(core == 0, yours, mine)], axis=1).astype(F32)
    low_full = jnp.concatenate([low_total[0], low_total[1]], axis=1).astype(F32)
    state = jnp.where(core == 0, full, decay(rate, 2 * chip, 2 * chip + 1) * full + low_full)
    state = state + decay(rate, 0, pos) * carry_state
    for piece in range(pieces):
        parts.append(local(piece, pieces, u))

    outs = []
    size = width // pieces
    done = []
    for piece in range(pieces):
        part, gate, table = parts[piece]
        n = size // SET
        spec = lambda rows: pl.BlockSpec((rows, SET), lambda i: (0, i))
        done.append(pl.pallas_call(
            last_kernel,
            grid=(n,),
            in_specs=[pl.BlockSpec((modes, SET), lambda i, piece=piece: (0, piece * n + i)), spec(count), spec(count), spec(count)],
            out_specs=spec(count),
            out_shape=jax.ShapeDtypeStruct((count, size), BF),
            compiler_params=params(),
            name="last",
        )(state, table, gate, part))
    return jnp.concatenate(done, axis=1)


def solution(mesh):
    placed = (
        P(("groups", "ctx"), None, None),
        P(),
        P(),
        P(),
        P(),
        P("groups", None),
        P("groups", None, None),
        P("groups"),
    )
    return jax.shard_map(
        body, mesh=mesh, in_specs=placed, out_specs=P(("groups", "ctx"), None), check_vma=False
    )
```

time: 181 us -> 78.4 us (0.43); the launches traced: 178 us -> 77.8 us
  matrix products: 96.3 us -> 0 us
  Pallas kernels: 0 us -> 41.5 us
  other arithmetic: 28.4 us -> 2.16 us
  local copies, waits for them, and re-layouts: 36.4 us -> 15.3 us
  starting transfers between devices: 2.36 us -> 10.3 us
  between operations: 14.3 us -> 7.28 us
    dot_general x34 -> x0, matrix products: 96.3 us -> none  [the longest x16 65.8 us: one_step(): jnp.einsum('gmt,gms->gts', falling, rising, precision=lax.Precision.HIGHEST)]
    pallas_call x0 -> x10, Pallas kernels: none -> 41.5 us  [the longest x4 25.7 us: local(): pl.pallas_call(local_kernel, grid=(tiles,), in_specs=[spec(count), spec(2...]
    add x2 -> x1, other arithmetic: 12.7 us -> 0.15 us  [body(): state = state + decay(rate, 0, pos) * carry_state]
    ppermute x1 -> x6, starting transfers between devices: 2.36 us -> 10.3 us  [the longest x3 4.41 us: body(): lax.ppermute(sent, 'ctx', [(i, i ^ 2 * reach) for i in range(blocks)])]
    unnamed x21 -> x33, local copies, waits for them, and re-layouts: 17.7 us -> 9.93 us
    convert_element_type x21 -> x4, other arithmetic: 5.77 us -> 0.41 us  [the longest x3 0.3 us: body(): sent = chip_total.astype(BF)]
    transpose x1 -> x0, local copies, waits for them, and re-layouts: 3.26 us -> none  [block_state(): jnp.einsum('gms,sgf->mgf', decay, grouped, preferred_element_type=jnp.flo...]
    unnamed x3 -> x0, other arithmetic: 3.1 us -> none
  transfers between devices with their start and end apart: 2 -> 6, of which waited for: 0 -> 1; matrix products, arithmetic and copies ran while one was open for 63% -> 6% of each run, Pallas kernels for 0% -> 47%
where the time goes in v1:
time: 78.4 us; the launch traced here: 77.8 us
  Pallas kernels  41.5 us (53%)
  local copies, waits for them, and re-layouts  15.3 us (20%)
  starting transfers between devices  10.3 us (13%)
  between operations  7.28 us (9%)
  other arithmetic  2.16 us (3%)
  waiting for transfers between devices  1.24 us (2%)
    pallas_call x4, Pallas kernels, local(): pl.pallas_call(local_kernel, grid=(tiles,), in_specs=[spec(count), spec(2...  25.7 us
    pallas_call x1, Pallas kernels, body(): pl.pallas_call(first_kernel, grid_spec=pltpu.PrefetchScalarGridSpec(num_s...  10.8 us
    unnamed x33, local copies, waits for them, and re-layouts  9.93 us
    pallas_call x4, Pallas kernels, body(): pl.pallas_call(last_kernel, grid=(n,), in_specs=[pl.BlockSpec((modes, SET...  4.59 us
    ppermute x3, starting transfers between devices, body(): lax.ppermute(sent, 'ctx', [(i, i ^ 2 * reach) for i in range(blocks)])  4.41 us
    ppermute x1, starting transfers between devices, body(): lax.ppermute(feat[:, count - 2:], 'ctx', [(i, i + 1) for i in range(block...  2.97 us
    ppermute x2, starting transfers between devices, body(): lax.ppermute(value, 'ctx', [(i, i ^ 1) for i in range(blocks)])  2.95 us
    slice x1, local copies, waits for them, and re-layouts, body(): rate_half = jnp.where(core == 0, rate2[:, 0], rate2[:, 1])  1.99 us
  transfers between devices with their start and end apart: 6, of which 1 were waited for; matrix products, arithmetic and copies ran while one was open for 6% of the time, Pallas kernels for 47%

profile of v1, /device:TPU:0, one launch (start us, length us, event | category | flops | bytes accessed | tf_op | source)
XLA Modules:
  0.0 77.8 jit_solution(4284956298328256268)
XLA Ops:
  0.0 1.7 %fusion.14 = (bf16[3,2,4096]{2,1,0:T(2,128)(2,1)}, bf16[3,2,4096]{2,1,0:T(2,128)(2,1)S(1)}) fusion(bf16[3,256,4096]{2,1,0:T(8,128)(2,1)} %bitcast.75), kind=kLoop, calls=%fused_computation.46 | loop fusion | bytes 196608 | tf_op jit(solution)/shard_map/slice | solution.py:238
  1.7 3.0 %collective-permute-start = (bf16[3,2,4096]{2,1,0:T(2,128)(2,1)}, bf16[3,2,4096]{2,1,0:T(2,128)(2,1)}, u32[]{:S(2)}, u32[]{:S(2)}) collective-permute-start(bf16[3,2,4096]{2,1,0:T(2,128)(2,1)} %get-tuple-element.51), channel_id=1, source_target_pairs={{0,1},{1,2},{2,3},{3,4},{4,5},{5,6},{6,7},{7,8},{8,9},{9,10},{10,1... | collective-permute-start | bytes 147464 | tf_op jit(solution)/shard_map/ppermute | solution.py:238
  4.7 1.0 %copy.38 = f32[3,3,4096]{2,0,1:T(4,128)S(1)} copy(f32[3,3,4096]{2,1,0:T(4,128)} %param.9) | data formatting | bytes 294912 | tf_op args[1]
  5.7 2.8 %copy-done = bf16[256,3,4096]{2,0,1:T(8,128)(2,1)S(1)} copy-done((bf16[256,3,4096]{2,0,1:T(8,128)(2,1)S(1)}, bf16[256,3,4096]{2,0,1:T(8,128)(2,1)}, u32[]{:S(2)}) %copy-start) | copy-done | bytes 6291480
  8.5 0.7 copy-done.5
  10.7 10.8 %first.1 = (bf16[256,4096]{1,0:T(8,128)(2,1)S(1)}, f32[16,4096]{1,0:T(8,128)S(1)}, f32[16,4096]{1,0:T(8,128)S(1)}, f32[1,4096]{1,0:T(1,128)S(1)}, f32[1,4096]{1,...) custom-call(s32[1]{0:T(128)} %bitcast.pos_ref, s32[32,128]{1,0:T(8,128)S(1)} %bitcast.92, ...), custom_call_target="tpu_custom_call" | custom-call | tf_op jit(solution)/shard_map/first/pallas_call | solution.py:245
  21.5 0.9 %reshape.70 = f32[16,2,2048]{2,1,0:T(2,128)} reshape(f32[16,4096]{1,0:T(8,128)S(1)} %get-tuple-element.26.rate_ref) | data formatting | bytes 524288 | tf_op jit(solution)/shard_map/reshape | solution.py:341
  22.4 2.0 %fusion.15 = (f32[16,1,2048]{2,1,0:T(1,128)}, f32[16,1,2048]{2,1,0:T(1,128)}) fusion(f32[16,2,2048]{2,1,0:T(2,128)} %reshape.70), kind=kLoop, calls=%fused_computation.47 | loop fusion | bytes 524288 | tf_op jit(solution)/shard_map/slice | solution.py:342
  32.4 0.9 %copy-done.4 = f32[16,4096]{1,0:T(8,128)S(1)} copy-done((f32[16,4096]{1,0:T(8,128)S(1)}, f32[16,4096]{1,0:T(8,128)}, u32[]{:S(2)}) %copy-start.4) | copy-done | bytes 262168
  33.8 2.9 %collective-permute-start.1 = (bf16[2,16,2048]{2,1,0:T(8,128)(2,1)S(1)}, bf16[2,16,2048]{2,1,0:T(8,128)(2,1)S(1)}, u32[]{:S(2)}, u32[]{:S(2)}) collective-permute-start(bf16[2,16,2048]{2,1,0:T(8,128)(2,1)S(1)} %get-tuple-element.28), channel_id=1, source_target_pairs={{0,1},{1,0},{2,3},{3,2},{4,5},{5,4},{6,7},{7,6},{8,9},{9,8},{10,11... | collective-permute-start | bytes 393224 | tf_op jit(solution)/shard_map/ppermute | solution.py:343
  36.7 2.8 %copy-done.1 = bf16[256,3,4096]{2,0,1:T(8,128)(2,1)S(1)} copy-done((bf16[256,3,4096]{2,0,1:T(8,128)(2,1)S(1)}, bf16[256,3,4096]{2,0,1:T(8,128)(2,1)}, u32[]{:S(2)}) %copy-start.1) | copy-done | bytes 6291480
  39.5 6.4 %local.4 = (f32[256,1024]{1,0:T(8,128)S(1)}, f32[256,1024]{1,0:T(8,128)S(1)}, bf16[256,1024]{1,0:T(8,128)(2,1)S(1)}) custom-call(bf16[256,4096]{1,0:T(8,128)(2,1)S(1)} %get-tuple-element.29.u_ref, f32[2,4096]{1,0:T(2,128)S(1)} %get-tuple-element.30.head_ref, bf16[3,256,4096]{2,1,0:T(8,128)(2,1)S(1)} %bitcast.78, ...), custom_call_target="tpu_custom_call" | custom-call | flops 1677721600 | bytes 4800000 | tf_op jit(solution)/shard_map/local/pallas_call | solution.py:299
  46.1 1.6 %collective-permute-start.2 = (bf16[16,2048]{1,0:T(8,128)(2,1)S(1)}, bf16[16,2048]{1,0:T(8,128)(2,1)S(1)}, u32[]{:S(2)}, u32[]{:S(2)}) collective-permute-start(bf16[16,2048]{1,0:T(8,128)(2,1)S(1)} %get-tuple-element.49), channel_id=1, source_target_pairs={{0,2},{1,3},{2,0},{3,1},{4,6},{5,7},{6,4},{7,5},{8,10},{9,11},{10,... | collective-permute-start | bytes 196616 | tf_op jit(solution)/shard_map/ppermute | solution.py:356
  47.7 6.4 %local.5 = (f32[256,1024]{1,0:T(8,128)S(1)}, f32[256,1024]{1,0:T(8,128)S(1)}, bf16[256,1024]{1,0:T(8,128)(2,1)S(1)}) custom-call(bf16[256,4096]{1,0:T(8,128)(2,1)S(1)} %get-tuple-element.29.u_ref, f32[2,4096]{1,0:T(2,128)S(1)} %get-tuple-element.30.head_ref, bf16[3,256,4096]{2,1,0:T(8,128)(2,1)S(1)} %bitcast.79, ...), custom_call_target="tpu_custom_call" | custom-call | flops 1677721600 | bytes 4800000 | tf_op jit(solution)/shard_map/local/pallas_call | solution.py:299
  54.2 1.6 %collective-permute-start.3 = (bf16[16,2048]{1,0:T(8,128)(2,1)S(1)}, bf16[16,2048]{1,0:T(8,128)(2,1)S(1)}, u32[]{:S(2)}, u32[]{:S(2)}) collective-permute-start(bf16[16,2048]{1,0:T(8,128)(2,1)S(1)} %get-tuple-element.47), channel_id=1, source_target_pairs={{0,4},{1,5},{2,6},{3,7},{4,0},{5,1},{6,2},{7,3},{8,12},{9,13},{10,... | collective-permute-start | bytes 196616 | tf_op jit(solution)/shard_map/ppermute | solution.py:356
  55.9 6.4 %local.6 = (f32[256,1024]{1,0:T(8,128)S(1)}, f32[256,1024]{1,0:T(8,128)S(1)}, bf16[256,1024]{1,0:T(8,128)(2,1)S(1)}) custom-call(bf16[256,4096]{1,0:T(8,128)(2,1)S(1)} %get-tuple-element.29.u_ref, f32[2,4096]{1,0:T(2,128)S(1)} %get-tuple-element.30.head_ref, bf16[3,256,4096]{2,1,0:T(8,128)(2,1)S(1)} %bitcast.80, ...), custom_call_target="tpu_custom_call" | custom-call | flops 1677721600 | bytes 4800000 | tf_op jit(solution)/shard_map/local/pallas_call | solution.py:299
  62.4 1.2 %collective-permute-start.4 = (bf16[16,2048]{1,0:T(8,128)(2,1)S(1)}, bf16[16,2048]{1,0:T(8,128)(2,1)S(1)}, u32[]{:S(2)}, u32[]{:S(2)}) collective-permute-start(bf16[16,2048]{1,0:T(8,128)(2,1)S(1)} %fusion.7), channel_id=1, source_target_pairs={{0,8},{1,9},{2,10},{3,11},{4,12},{5,13},{6,14},{7,15},{8,0},{9,1},... | collective-permute-start | bytes 196616 | tf_op jit(solution)/shard_map/ppermute | solution.py:356
  63.6 6.4 %local.7 = (f32[256,1024]{1,0:T(8,128)S(1)}, f32[256,1024]{1,0:T(8,128)S(1)}, bf16[256,1024]{1,0:T(8,128)(2,1)S(1)}) custom-call(bf16[256,4096]{1,0:T(8,128)(2,1)S(1)} %get-tuple-element.29.u_ref, f32[2,4096]{1,0:T(2,128)S(1)} %get-tuple-element.30.head_ref, bf16[3,256,4096]{2,1,0:T(8,128)(2,1)S(1)} %bitcast.81, ...), custom_call_target="tpu_custom_call" | custom-call | flops 1677721600 | bytes 4800000 | tf_op jit(solution)/shard_map/local/pallas_call | solution.py:299
  70.3 1.2 %collective-permute-done.5 = bf16[16,2048]{1,0:T(8,128)(2,1)S(1)} collective-permute-done((bf16[16,2048]{1,0:T(8,128)(2,1)S(1)}, bf16[16,2048]{1,0:T(8,128)(2,1)S(1)}, u32[]{:S(2)}, u32[]{:S(2)}) %collective-permute-start.5) | collective-permute-done | bytes 65568 | tf_op jit(solution)/shard_map/ppermute | solution.py:343
  71.7 1.1 %last.4 = bf16[256,1024]{1,0:T(8,128)(2,1)S(1)} custom-call(f32[16,4096]{1,0:T(8,128)S(1)} %fusion.1.state_ref, bf16[256,1024]{1,0:T(8,128)(2,1)S(1)} %get-tuple-element.35.table_ref, f32[256,1024]{1,0:T(8,128)S(1)} %get-tuple-element.36.gate_ref, f32[256,1024]{1,0:T(8,128)S(1)} %get-tuple-element.37.part_ref), custom_call_target="tpu_custom_call" | custom-call | tf_op jit(solution)/shard_map/last/pallas_call | solution.py:381
  72.8 1.2 %last.5 = bf16[256,1024]{1,0:T(8,128)(2,1)S(1)} custom-call(f32[16,4096]{1,0:T(8,128)S(1)} %fusion.1.state_ref, bf16[256,1024]{1,0:T(8,128)(2,1)S(1)} %get-tuple-element.38.table_ref, f32[256,1024]{1,0:T(8,128)S(1)} %get-tuple-element.39.gate_ref, f32[256,1024]{1,0:T(8,128)S(1)} %get-tuple-element.40.part_ref), custom_call_target="tpu_custom_call" | custom-call | tf_op jit(solution)/shard_map/last/pallas_call | solution.py:381
  74.0 1.2 %last.6 = bf16[256,1024]{1,0:T(8,128)(2,1)S(1)} custom-call(f32[16,4096]{1,0:T(8,128)S(1)} %fusion.1.state_ref, bf16[256,1024]{1,0:T(8,128)(2,1)S(1)} %get-tuple-element.41.table_ref, f32[256,1024]{1,0:T(8,128)S(1)} %get-tuple-element.42.gate_ref, f32[256,1024]{1,0:T(8,128)S(1)} %get-tuple-element.43.part_ref), custom_call_target="tpu_custom_call" | custom-call | tf_op jit(solution)/shard_map/last/pallas_call | solution.py:381
  75.1 1.2 %last.7 = bf16[256,1024]{1,0:T(8,128)(2,1)S(1)} custom-call(f32[16,4096]{1,0:T(8,128)S(1)} %fusion.1.state_ref, bf16[256,1024]{1,0:T(8,128)(2,1)S(1)} %get-tuple-element.44.table_ref, f32[256,1024]{1,0:T(8,128)S(1)} %get-tuple-element.45.gate_ref, f32[256,1024]{1,0:T(8,128)S(1)} %get-tuple-element.46.part_ref), custom_call_target="tpu_custom_call" | custom-call | tf_op jit(solution)/shard_map/last/pallas_call | solution.py:381
  76.3 1.5 %pad_maximum_fusion = bf16[256,4096]{1,0:T(8,128)(2,1)} fusion(bf16[256,1024]{1,0:T(8,128)(2,1)S(1)} %last.7, bf16[256,1024]{1,0:T(8,128)(2,1)S(1)} %last.6, bf16[256,1024]{1,0:T(8,128)(2,1)S(1)} %last.5, bf16[256,1024]{1,0:T(8,128)(2,1)S(1)} %last.4), kind=kLoop, calls=%fused_computation | loop fusion | flops 8388608 | bytes 4194304 | tf_op jit(solution)/shard_map/concatenate | solution.py:390
  (47 shorter events, 3.6 us)
Async XLA Ops:
  1.7 30.6 %collective-permute-start = (bf16[3,2,4096]{2,1,0:T(2,128)(2,1)}, bf16[3,2,4096]{2,1,0:T(2,128)(2,1)}, u32[]{:S(2)}, u32[]{:S(2)}) collective-permute-start(bf16[3,2,4096]{2,1,0:T(2,128)(2,1)} %get-tuple-element.51), channel_id=1, source_target_pairs={{0,1},{1,2},{2,3},{3,4},{4,5},{5,6},{6,7},{7,8},{8,9},{9,10},{10,1... | collective-permute-start | bytes 147464 | tf_op jit(solution)/shard_map/ppermute | solution.py:238
  5.7 2.8 %copy-start = (bf16[256,3,4096]{2,0,1:T(8,128)(2,1)S(1)}, bf16[256,3,4096]{2,0,1:T(8,128)(2,1)}, u32[]{:S(2)}) copy-start(bf16[256,3,4096]{2,0,1:T(8,128)(2,1)} %param.8) | copy-start | bytes 18874372
  8.5 0.7 copy-start.5
  9.2 0.7 copy-start.7
  9.9 0.7 copy-start.9
  10.7 13.7 %copy-start.6 = (s32[4096]{0:T(1024)S(1)}, s32[4096]{0:T(1024)}, u32[]{:S(2)}) copy-start(s32[4096]{0:T(1024)} %param.15) | copy-start | bytes 49156
  10.7 16.4 %copy-start.8 = (f32[256,16]{0,1:T(8,128)S(1)}, f32[256,16]{0,1:T(8,128)}, u32[]{:S(2)}) copy-start(f32[256,16]{0,1:T(8,128)} %param.11) | copy-start | bytes 49156
  10.7 16.6 %copy-start.10 = (f32[256,16]{0,1:T(8,128)S(1)}, f32[256,16]{0,1:T(8,128)}, u32[]{:S(2)}) copy-start(f32[256,16]{0,1:T(8,128)} %param.10) | copy-start | bytes 49156
  10.7 21.6 %copy-start.14 = (bf16[2,3,4096]{2,0,1:T(2,128)(2,1)S(1)}, bf16[2,3,4096]{2,0,1:T(2,128)(2,1)}, u32[]{:S(2)}) copy-start(bf16[2,3,4096]{2,0,1:T(2,128)(2,1)} %param.14) | copy-start | bytes 147460
  10.7 26.0 %copy-start.2 = (f32[4096]{0:T(1024)S(1)}, f32[4096]{0:T(1024)}, u32[]{:S(2)}) copy-start(f32[4096]{0:T(1024)} %param.12) | copy-start | bytes 49156
  21.4 5.6 %copy-start.3 = (f32[16,4096]{1,0:T(8,128)}, f32[16,4096]{1,0:T(8,128)S(1)}, u32[]{:S(2)}) copy-start(f32[16,4096]{1,0:T(8,128)S(1)} %get-tuple-element.27.sum_ref) | copy-start | bytes 786436
  32.4 1.0 %copy-start.4 = (f32[16,4096]{1,0:T(8,128)S(1)}, f32[16,4096]{1,0:T(8,128)}, u32[]{:S(2)}) copy-start(f32[16,4096]{1,0:T(8,128)} %copy-done.3) | copy-start | bytes 786436
  33.8 12.1 %collective-permute-start.1 = (bf16[2,16,2048]{2,1,0:T(8,128)(2,1)S(1)}, bf16[2,16,2048]{2,1,0:T(8,128)(2,1)S(1)}, u32[]{:S(2)}, u32[]{:S(2)}) collective-permute-start(bf16[2,16,2048]{2,1,0:T(8,128)(2,1)S(1)} %get-tuple-element.28), channel_id=1, source_target_pairs={{0,1},{1,0},{2,3},{3,2},{4,5},{5,4},{6,7},{7,6},{8,9},{9,8},{10,11... | collective-permute-start | bytes 393224 | tf_op jit(solution)/shard_map/ppermute | solution.py:343
  36.7 2.8 %copy-start.1 = (bf16[256,3,4096]{2,0,1:T(8,128)(2,1)S(1)}, bf16[256,3,4096]{2,0,1:T(8,128)(2,1)}, u32[]{:S(2)}) copy-start(bf16[256,3,4096]{2,0,1:T(8,128)(2,1)} %param.8) | copy-start | bytes 18874372
  39.5 6.5 %copy-start.11 = (f32[16,1,2048]{2,1,0:T(1,128)S(1)}, f32[16,1,2048]{2,1,0:T(1,128)}, u32[]{:S(2)}) copy-start(f32[16,1,2048]{2,1,0:T(1,128)} %get-tuple-element.53) | copy-start | bytes 393220
  39.5 6.5 %copy-start.12 = (f32[16,1,2048]{2,1,0:T(1,128)S(1)}, f32[16,1,2048]{2,1,0:T(1,128)}, u32[]{:S(2)}) copy-start(f32[16,1,2048]{2,1,0:T(1,128)} %get-tuple-element.54) | copy-start | bytes 393220
  46.1 8.0 %collective-permute-start.2 = (bf16[16,2048]{1,0:T(8,128)(2,1)S(1)}, bf16[16,2048]{1,0:T(8,128)(2,1)S(1)}, u32[]{:S(2)}, u32[]{:S(2)}) collective-permute-start(bf16[16,2048]{1,0:T(8,128)(2,1)S(1)} %get-tuple-element.49), channel_id=1, source_target_pairs={{0,2},{1,3},{2,0},{3,1},{4,6},{5,7},{6,4},{7,5},{8,10},{9,11},{10,... | collective-permute-start | bytes 196616 | tf_op jit(solution)/shard_map/ppermute | solution.py:356
  54.2 8.1 %collective-permute-start.3 = (bf16[16,2048]{1,0:T(8,128)(2,1)S(1)}, bf16[16,2048]{1,0:T(8,128)(2,1)S(1)}, u32[]{:S(2)}, u32[]{:S(2)}) collective-permute-start(bf16[16,2048]{1,0:T(8,128)(2,1)S(1)} %get-tuple-element.47), channel_id=1, source_target_pairs={{0,4},{1,5},{2,6},{3,7},{4,0},{5,1},{6,2},{7,3},{8,12},{9,13},{10,... | collective-permute-start | bytes 196616 | tf_op jit(solution)/shard_map/ppermute | solution.py:356
  62.4 9.1 %copy-start.13 = (f32[16,4096]{1,0:T(8,128)S(1)}, f32[16,4096]{1,0:T(8,128)}, u32[]{:S(2)}) copy-start(f32[16,4096]{1,0:T(8,128)} %param.13) | copy-start | bytes 786436
  62.4 7.6 %collective-permute-start.4 = (bf16[16,2048]{1,0:T(8,128)(2,1)S(1)}, bf16[16,2048]{1,0:T(8,128)(2,1)S(1)}, u32[]{:S(2)}, u32[]{:S(2)}) collective-permute-start(bf16[16,2048]{1,0:T(8,128)(2,1)S(1)} %fusion.7), channel_id=1, source_target_pairs={{0,8},{1,9},{2,10},{3,11},{4,12},{5,13},{6,14},{7,15},{8,0},{9,1},... | collective-permute-start | bytes 196616 | tf_op jit(solution)/shard_map/ppermute | solution.py:356
  70.2 1.3 %collective-permute-start.5 = (bf16[16,2048]{1,0:T(8,128)(2,1)S(1)}, bf16[16,2048]{1,0:T(8,128)(2,1)S(1)}, u32[]{:S(2)}, u32[]{:S(2)}) collective-permute-start(bf16[16,2048]{1,0:T(8,128)(2,1)S(1)} %fusion.4), channel_id=1, source_target_pairs={{0,1},{1,0},{2,3},{3,2},{4,5},{5,4},{6,7},{7,6},{8,9},{9,8},{10,11... | collective-permute-start | bytes 196616 | tf_op jit(solution)/shard_map/ppermute | solution.py:343

commit v2 on v0

v2 whole, which is shorter than its diff:
```python
import jax
import jax.numpy as jnp
from jax import lax
from jax.experimental import pallas as pl
from jax.experimental.pallas import tpu as pltpu
from jax.sharding import PartitionSpec as P

BF = jnp.bfloat16
F32 = jnp.float32
LANES = 128
SET = 256
WIDE = 1024
SUB = 32


def iota(shape, dim):
    return lax.broadcasted_iota(jnp.int32, shape, dim)


def flag(x):
    return x.astype(F32)


def split3(x):
    hi = x.astype(BF)
    rest = x - hi.astype(F32)
    mid = rest.astype(BF)
    low = (rest - mid.astype(F32)).astype(BF)
    return [hi, mid, low]


def spread_out(values, onehot):
    rows = values[0].shape[0]
    pieces = sum([split3(value) for value in values], [])
    got = jnp.dot(jnp.concatenate(pieces, axis=0), onehot, preferred_element_type=F32)
    part = lambda i: got[i * rows : (i + 1) * rows]
    return [(part(3 * i) + part(3 * i + 1)) + part(3 * i + 2) for i in range(len(values))]


def plan_kernel(count, rounds, pos_ref, seg_ref, ids_ref, rates_ref, res_ref,
                rate_ref, flat_ref, col_ref, tri_ref, keep_ref, half_ref, full_ref):
    pos = pos_ref[0]
    modes = rates_ref.shape[0]
    width = rate_ref.shape[1]
    members = width // rates_ref.shape[1]
    halves, rows = [], []
    for part in range(count // LANES):
        row = seg_ref[pl.ds((count // LANES) * pos + part, 1), :].astype(F32)
        rows.append(row)
        halves.append(jnp.transpose(jnp.broadcast_to(row, (LANES, LANES))))
    col = jnp.concatenate(halves, axis=0)

    def seg_at(spot):
        at = jnp.maximum(spot, 0)
        return jnp.where(spot < 0, 0, ids_ref[at])

    first = pos * count
    last = seg_at(first - 1).astype(F32)
    second = seg_at(first - 2).astype(F32)
    end = seg_at(first + count - 1).astype(F32)
    token = iota((count, LANES), 0)
    one = jnp.where(token == 0, last, pltpu.roll(col, 1, 0))
    two = jnp.where(token == 0, second, jnp.where(token == 1, last, pltpu.roll(col, 2, 0)))
    col_ref[0] = flag(col == one)
    col_ref[1] = flag(col == two)
    col_ref[2] = flag(col == last)
    col_ref[3] = flag(col == end)
    start = iota((count, LANES), 0) // SUB
    lead = jnp.zeros((count, LANES), F32)
    for c in range(count // SUB):
        lead = jnp.where(start == c, seg_at(first + c * SUB - 1).astype(F32), lead)
    col_ref[4] = flag(col == lead)
    lane = iota((SUB, SET), 1)
    inner = lax.rem(lane, SUB)
    tall = iota((SUB, SET), 0)
    for c in range(count // SUB):
        row = rows[c * SUB // LANES]
        shift = (c * SUB) % LANES
        base = row if shift == 0 else pltpu.roll(row, LANES - shift, 1)
        base = jnp.where(iota((1, LANES), 1) < SUB, base, 0.0)
        base = base + pltpu.roll(base, SUB, 1)
        base = base + pltpu.roll(base, 2 * SUB, 1)
        base = jnp.concatenate([base] * (SET // LANES), axis=1)
        mine = jnp.concatenate([col[c * SUB : (c + 1) * SUB]] * (SET // LANES), axis=1)
        tri_ref[c * SUB : (c + 1) * SUB, :] = flag((tall >= inner) & (mine == base)).astype(BF)
        keep_ref[c * 16 : (c + 1) * 16, :] = jnp.broadcast_to(
            flag(base == ids_ref[first + (c + 1) * SUB - 1].astype(F32)), (16, SET)).astype(BF)
    rates = rates_ref[...]
    weight = res_ref[...] * jnp.sqrt(rates)
    per = LANES * members
    onehot = flag(iota((LANES, per), 0) == iota((LANES, per), 1) // members).astype(BF)
    pick = iota((modes, per), 0) == lax.rem(iota((modes, per), 1), modes)
    for block in range(width // per):
        at = slice(block * LANES, (block + 1) * LANES)
        to = slice(block * per, (block + 1) * per)
        rate, wide = spread_out([rates[:, at], weight[:, at]], onehot)
        rate_ref[:, to] = rate
        flat_ref[0:1, to] = jnp.sum(jnp.where(pick, rate, 0.0), axis=0, keepdims=True)
        flat_ref[1:2, to] = jnp.sum(jnp.where(pick, wide, 0.0), axis=0, keepdims=True)

    def decay(rate, low, high):
        alive = flag(seg_at(low * count - 1) == seg_at(high * count - 1))
        return jnp.exp(-rate * (count * (high - low)).astype(F32)) * alive

    core = lax.rem(pos, 2)
    chip = pos // 2
    upper_half = rate_ref[:, pl.ds(pl.multiple_of(core * (width // 2), LANES), width // 2)]
    half_ref[0] = decay(upper_half, 2 * chip + 1, 2 * chip + 2)
    for k in range(rounds):
        reach = 1 << k
        base = (chip // reach) * reach
        up = lax.rem(chip // reach, 2)
        mate = base + reach * (1 - 2 * up)
        upf = up.astype(F32)
        half_ref[1 + 3 * k] = upf * decay(upper_half, 2 * base, 2 * chip)
        half_ref[2 + 3 * k] = jnp.where(up == 1, 1.0, decay(upper_half, 2 * mate, 2 * mate + 2 * reach))
        half_ref[3 + 3 * k] = jnp.where(up == 1, decay(upper_half, 2 * base, 2 * base + 2 * reach), 1.0)
    rate = rate_ref[...]
    full_ref[0] = jnp.where(core == 0, 1.0, decay(rate, 2 * chip, 2 * chip + 1))
    full_ref[1] = decay(rate, jnp.zeros_like(pos), pos)


def first_kernel(k_ref, v_ref, sw_ref, flat_ref, col_ref, u_ref, sum_ref):
    count, wide = u_ref.shape
    modes = sum_ref.shape[0]
    members = SET // modes
    token = iota((count, LANES), 0)
    one = col_ref[0]
    two = col_ref[1]
    owner = iota((modes, LANES), 1) // members
    for half in range(wide // LANES):
        at = slice(half * LANES, (half + 1) * LANES)
        made = []
        for index, ref in ((1, k_ref), (2, v_ref)):
            x = ref[:, at].astype(F32)
            made.append(
                sw_ref[index, 0:1, at] * x
                + sw_ref[index, 1:2, at] * (one * pltpu.roll(x, 1, 0))
                + sw_ref[index, 2:3, at] * (two * pltpu.roll(x, 2, 0))
            )
        u = jnp.where(token < 2, 0.0, made[0] * made[1]).astype(BF)
        u_ref[:, at] = u
        rflat = flat_ref[0:1, at]
        fine = jnp.exp(-rflat * (SUB - 1.0 - iota((SUB, LANES), 0).astype(F32)))
        spans = count // SUB
        coarse = jnp.exp(-rflat * (SUB * (spans - 1.0 - iota((spans, LANES), 0).astype(F32))))
        decay = jnp.concatenate([coarse[a : a + 1] * fine for a in range(spans)], axis=0)
        decay = (decay * col_ref[3]).astype(BF)
        sums = lax.dot_general(decay, u, (((0,), (0,)), ((), ())), preferred_element_type=F32)
        total = jnp.zeros((modes, LANES), F32)
        for g in range(LANES // members):
            total = jnp.where(owner == g, sums[g * modes : (g + 1) * modes], total)
        sum_ref[:, at] = total


def head_kernel(count, pos_ref, ids_ref, feat_ref, halo_ref, early_ref, sw_ref, rate_ref, sum_ref,
                total_ref, head_ref, use_ref):
    pos = pos_ref[0]
    width = rate_ref.shape[1]

    def seg_at(spot):
        at = jnp.maximum(spot, 0)
        return jnp.where(spot < 0, 0, ids_ref[at])

    first = pos * count
    s0, s1 = seg_at(first), seg_at(first + 1)
    end = seg_at(first + count - 1)
    p1, p2 = seg_at(first - 1), seg_at(first - 2)
    same = lambda a, b: (a == b).astype(F32)
    made = []
    for index in (0, 1, 2):
        h = jnp.where(pos == 0, early_ref[index].astype(F32), halo_ref[index].astype(F32))
        if index == 0:
            use_ref[...] = h
            continue
        x = feat_ref[index].astype(F32)
        x0, x1 = x[0:1], x[1:2]
        h2, h1 = h[0:1], h[1:2]
        w = [sw_ref[index, j : j + 1, :] for j in range(3)]
        f0 = w[0] * x0 + w[1] * (same(p1, s0) * h1) + w[2] * (same(p2, s0) * h2)
        f1 = w[0] * x1 + w[1] * (same(s0, s1) * x0) + w[2] * (same(p1, s1) * h1)
        made.append((f0, f1))
    u0 = (made[0][0] * made[1][0]).astype(BF).astype(F32)
    u1 = (made[0][1] * made[1][1]).astype(BF).astype(F32)
    head_ref[0:1, :] = u0
    head_ref[1:2, :] = u1
    half = width // 2
    for part in range(2):
        at = slice(part * half, (part + 1) * half)
        rate = rate_ref[:, at]
        total = sum_ref[:, at]
        total = total + jnp.exp(-rate * (count - 1.0)) * (same(s0, end) * u0[:, at])
        total = total + jnp.exp(-rate * (count - 2.0)) * (same(s1, end) * u1[:, at])
        total_ref[part] = total.astype(BF)


def local_kernel(piece, u_ref, head_ref, q_ref, halo_ref, sw_ref, skip_ref, rates_ref, res_ref, rate_ref, flat_ref,
                 col_ref, tri_ref, keep_ref, out_ref, gate_ref, cross_ref):
    count, wide = u_ref.shape
    modes = rates_ref.shape[0]
    members = 16
    groups = LANES // members
    spans = count // SUB
    at0 = (piece * (wide // members)) % LANES
    cols = wide // members * SUB
    lane = iota((1, cols), 1)
    rates = rates_ref[...]
    weight = res_ref[...] * jnp.sqrt(rates)
    filt = lane // SUB
    onehot = flag(iota((LANES, cols), 0) == filt + at0).astype(BF)
    (rate_to_end,) = spread_out([rates], onehot)
    decays = jnp.exp(-rate_to_end * (SUB - 1.0 - lax.rem(lane, SUB).astype(F32))).astype(BF)
    spot = lax.rem(lane, LANES)
    within = lax.rem((spot + SUB - 1) // SUB, LANES // SUB)
    lag = jnp.where(spot == 0, 0, lax.rem(SUB - lax.rem(spot, SUB), SUB)).astype(F32)
    filt = (lane // LANES) * (LANES // SUB) + within
    onehot = flag(iota((LANES, cols), 0) == filt + at0).astype(BF)
    rate_tap, weight_tap = spread_out([rates, weight], onehot)
    taps = jnp.sum(weight_tap * jnp.exp(-rate_tap * lag), axis=0, keepdims=True)

    token = iota((count, LANES), 0)
    owns = flag(iota((groups * SUB, LANES), 0) // SUB == iota((groups * SUB, LANES), 1) // members).astype(BF)
    holds = flag(iota((groups * modes, LANES), 0) // modes == iota((groups * modes, LANES), 1) // members).astype(BF)
    for tile in range(wide // LANES):
        at = slice(tile * LANES, (tile + 1) * LANES)
        u = u_ref[:, at].astype(F32)
        u = jnp.where(token == 0, head_ref[0:1, at], jnp.where(token == 1, head_ref[1:2, at], u))
        ub = u.astype(BF)
        rflat, wflat = flat_ref[0:1, at], flat_ref[1:2, at]
        near = []
        for part in range(SET // LANES):
            row = taps[:, tile * SET + part * LANES : tile * SET + (part + 1) * LANES]
            near.append(pltpu.roll(jnp.broadcast_to(row, (SUB, LANES)), 0, 1, stride=1, stride_axis=0))
        near = jnp.concatenate(near, axis=1).astype(BF)
        ends = decays[:, tile * SET : (tile + 1) * SET]
        table = wflat * jnp.exp(-rflat * (iota((SUB, LANES), 0).astype(F32) + 1.0))
        fall = jnp.exp(-rate_ref[:, at] * float(SUB))
        far = jnp.exp(-rflat * (SUB * iota((spans, LANES), 0).astype(F32)))
        inner, sums = [], []
        for c in range(spans):
            rows = slice(c * SUB, (c + 1) * SUB)
            left = jnp.concatenate([near * tri_ref[rows], ends * keep_ref[c * 16 : (c + 1) * 16]], axis=0)
            right = jnp.concatenate([ub[rows]] * groups, axis=0) * owns
            got = jnp.dot(left, right, preferred_element_type=F32)
            inner.append(got[:SUB])
            sums.append(got[SUB:])
            cross_ref[rows, at] = (table * far[c : c + 1] * col_ref[2, rows]).astype(BF)
        state = sums[0]
        local = [inner[0]]
        for c in range(1, spans):
            rows = slice(c * SUB, (c + 1) * SUB)
            seg_ok = flag_rows(col_ref, c)
            right = jnp.concatenate([state.astype(BF)] * groups, axis=0) * holds
            local.append(inner[c] + jnp.dot((table * seg_ok[0]).astype(BF), right, preferred_element_type=F32))
            state = fall * seg_ok[1] * state + sums[c]
        x = q_ref[:, at].astype(F32)
        h = halo_ref[:, at]
        one = jnp.where(token == 0, h[1:2], pltpu.roll(x, 1, 0))
        two = jnp.where(token == 0, h[0:1], jnp.where(token == 1, h[1:2], pltpu.roll(x, 2, 0)))
        q = sw_ref[0:1, at] * x + sw_ref[1:2, at] * (col_ref[0] * one) + sw_ref[2:3, at] * (col_ref[1] * two)
        gate_ref[:, at] = q
        out_ref[:, at] = q * (jnp.concatenate(local, axis=0) + skip_ref[:, at] * u)


def flag_rows(col_ref, c):
    rows = slice(c * SUB, (c + 1) * SUB)
    reach = col_ref[4, rows]
    return reach, reach[SUB - 1 : SUB]


def last_kernel(state_ref, table_ref, gate_ref, part_ref, out_ref):
    modes, wide = state_ref.shape
    members = 16
    groups = SET // members
    owner = iota((modes, SET), 1) // members
    for half in range(wide // SET):
        at = slice(half * SET, (half + 1) * SET)
        state = state_ref[:, at]
        spread = jnp.concatenate([jnp.where(owner == g, state, 0.0).astype(BF) for g in range(groups)], axis=0)
        cross = jnp.dot(table_ref[:, at], spread, preferred_element_type=F32)
        out_ref[:, at] = (part_ref[:, at] + gate_ref[:, at] * cross).astype(BF)


def params(limit=16 << 20):
    return pltpu.CompilerParams(vmem_limit_bytes=limit)


def fixed(shape):
    return pl.BlockSpec(shape, lambda i: (0,) * len(shape))


def lanes(rows, size, offset=0):
    return pl.BlockSpec((rows, size), lambda i: (0, offset + i))


def body(features, short_weight, residues, rates, skip, carry_state, earlier_rows, segment_ids):
    count, _, width = features.shape
    groups, modes = rates.shape
    blocks = lax.axis_size("ctx")
    pos = lax.axis_index("ctx")
    pos1 = pos.reshape(1)
    chips = blocks // 2
    rounds = chips.bit_length() - 1
    assert blocks == 2 << rounds and count == 2 * LANES and width == 16 * groups and modes == 16
    feat = jnp.transpose(features, (1, 0, 2))
    taps = jnp.transpose(short_weight, (1, 0, 2))
    early = jnp.transpose(earlier_rows, (1, 0, 2))
    segs = segment_ids.reshape(-1, LANES)
    rates_t = rates.T
    res_t = residues.T
    skip = skip.reshape(1, width)
    vm = pl.BlockSpec(memory_space=pltpu.VMEM)
    sm = pl.BlockSpec(memory_space=pltpu.SMEM)
    out = lambda *shape, dtype=F32: jax.ShapeDtypeStruct(shape, dtype)

    halo = lax.ppermute(feat[:, count - 2 :], "ctx", [(i, i + 1) for i in range(blocks - 1)])

    rate, flat, cols, tris, keeps, halves, fulls = pl.pallas_call(
        lambda *refs: plan_kernel(count, rounds, *refs),
        in_specs=[sm, vm, sm, vm, vm],
        out_specs=[vm] * 7,
        out_shape=[
            out(modes, width), out(2, width), out(5, count, LANES), out(count, SET, dtype=BF),
            out(count // SUB * 16, SET, dtype=BF), out(1 + 3 * rounds, modes, width // 2), out(2, modes, width),
        ],
        compiler_params=params(),
        name="plan",
    )(pos1, segs, segment_ids, rates_t, res_t)

    u, sums = pl.pallas_call(
        first_kernel,
        grid=(width // WIDE,),
        in_specs=[
            pl.BlockSpec((None, count, WIDE), lambda i: (1, 0, i)),
            pl.BlockSpec((None, count, WIDE), lambda i: (2, 0, i)),
            pl.BlockSpec((3, 3, WIDE), lambda i: (0, 0, i)),
            lanes(2, WIDE),
            fixed((5, count, LANES)),
        ],
        out_specs=[lanes(count, WIDE), lanes(modes, WIDE)],
        out_shape=[out(count, width, dtype=BF), out(modes, width)],
        compiler_params=params(),
        name="first",
    )(feat, feat, taps, flat, cols)

    total, head, halo_q = pl.pallas_call(
        lambda *refs: head_kernel(count, *refs),
        in_specs=[sm, sm] + [vm] * 6,
        out_specs=[vm] * 3,
        out_shape=[out(2, modes, width // 2, dtype=BF), out(2, width), out(2, width)],
        compiler_params=params(),
        name="head",
    )(pos1, segment_ids, feat[:, :2], halo, early, taps, rate, sums)

    pieces = width // WIDE
    parts = []
    for piece in range(pieces):
        mine = lambda rows, piece=piece: pl.BlockSpec((rows, WIDE), lambda i: (0, piece))
        group_block = piece * (WIDE // 16) // LANES
        few = pl.BlockSpec((modes, LANES), lambda i, b=group_block: (0, b))
        parts.append(pl.pallas_call(
            lambda *refs, piece=piece: local_kernel(piece, *refs),
            grid=(1,),
            in_specs=[
                mine(count), mine(2),
                pl.BlockSpec((None, count, WIDE), lambda i, piece=piece: (0, 0, piece)),
                mine(2),
                pl.BlockSpec((None, 3, WIDE), lambda i, piece=piece: (0, 0, piece)),
                mine(1), few, few, mine(modes), mine(2),
                fixed((5, count, LANES)), fixed((count, SET)), fixed((count // SUB * 16, SET)),
            ],
            out_specs=[lanes(count, WIDE)] * 3,
            out_shape=[out(count, WIDE), out(count, WIDE), out(count, WIDE, dtype=BF)],
            compiler_params=params(),
            cost_estimate=pl.CostEstimate(flops=4 << 30, bytes_accessed=5 << 20, transcendentals=0),
            name="local",
        )(u, head, feat, halo_q, taps, skip, rates_t, res_t, rate, flat, cols, tris, keeps))

    even = (pos & 1) == 0
    swap = lambda value: lax.ppermute(value, "ctx", [(i, i ^ 1) for i in range(blocks)])
    other = swap(total)
    low_total = jnp.where(even, total, other)
    own_half = lambda value: jnp.where(even, value[0], value[1]).astype(F32)
    chip_total = halves[0] * own_half(low_total) + own_half(jnp.where(even, other, total))
    before = jnp.zeros_like(chip_total)
    for k in range(rounds):
        got = lax.ppermute(chip_total.astype(BF), "ctx", [(i, i ^ (2 << k)) for i in range(blocks)]).astype(F32)
        before = before + halves[1 + 3 * k] * got
        chip_total = halves[2 + 3 * k] * chip_total + halves[3 + 3 * k] * got
    mine = before.astype(BF)
    yours = swap(mine)
    full = jnp.concatenate([jnp.where(even, mine, yours), jnp.where(even, yours, mine)], axis=1).astype(F32)
    low_full = jnp.where(even, 0.0, jnp.concatenate([low_total[0], low_total[1]], axis=1).astype(F32))
    state = fulls[0] * full + low_full + fulls[1] * carry_state

    done = []
    for piece in range(pieces):
        part, gate, table = parts[piece]
        done.append(pl.pallas_call(
            last_kernel,
            grid=(1,),
            in_specs=[pl.BlockSpec((modes, WIDE), lambda i, piece=piece: (0, piece))] + [lanes(count, WIDE)] * 3,
            out_specs=lanes(count, WIDE),
            out_shape=out(count, WIDE, dtype=BF),
            compiler_params=params(),
            name="last",
        )(state, table, gate, part))
    return jnp.concatenate(done, axis=1)


def solution(mesh):
    placed = (
        P(("groups", "ctx"), None, None),
        P(),
        P(),
        P(),
        P(),
        P("groups", None),
        P("groups", None, None),
        P("groups"),
    )
    return jax.shard_map(
        body, mesh=mesh, in_specs=placed, out_specs=P(("groups", "ctx"), None), check_vma=False
    )
```

time: 181 us -> 41.6 us (0.23); the launches traced: 178 us -> 41.1 us
  matrix products: 96.3 us -> 0 us
  local copies, waits for them, and re-layouts: 36.4 us -> 7.1 us
  other arithmetic: 28.4 us -> 1.77 us
  Pallas kernels: 0 us -> 18.7 us
  between operations: 14.3 us -> 0.2 us
  starting transfers between devices: 2.36 us -> 11 us
  waiting for transfers between devices: 0.02 us -> 2.37 us
    dot_general x34 -> x0, matrix products: 96.3 us -> none  [the longest x16 65.8 us: one_step(): jnp.einsum('gmt,gms->gts', falling, rising, precision=lax.Precision.HIGHEST)]
    pallas_call x0 -> x11, Pallas kernels: none -> 18.7 us  [the longest x4 9.18 us: body(): pl.pallas_call(lambda *refs, piece=piece: local_kernel(piece, *refs), gri...]
    add x2 -> x1, other arithmetic: 12.7 us -> 0.08 us  [body(): state = fulls[0] * full + low_full + fulls[1] * carry_state]
    unnamed x21 -> x23, local copies, waits for them, and re-layouts: 17.7 us -> 5.99 us
    ppermute x1 -> x6, starting transfers between devices: 2.36 us -> 11 us  [the longest x3 5.88 us: body(): lax.ppermute(chip_total.astype(BF), 'ctx', [(i, i ^ 2 << k) for i in rang...]
    convert_element_type x21 -> x4, other arithmetic: 5.77 us -> 0.15 us  [the longest x3 0.11 us: body(): chip_total.astype(BF)]
    transpose x1 -> x0, local copies, waits for them, and re-layouts: 3.26 us -> none  [block_state(): jnp.einsum('gms,sgf->mgf', decay, grouped, preferred_element_type=jnp.flo...]
    unnamed x3 -> x0, other arithmetic: 3.1 us -> none
  transfers between devices with their start and end apart: 2 -> 6, of which waited for: 0 -> 4; matrix products, arithmetic and copies ran while one was open for 63% -> 3% of each run, Pallas kernels for 0% -> 40%
where the time goes in v2:
time: 41.6 us; the launch traced here: 41.1 us
  Pallas kernels  18.7 us (45%)
  starting transfers between devices  11 us (26%)
  local copies, waits for them, and re-layouts  7.1 us (17%)
  waiting for transfers between devices  2.37 us (6%)
  other arithmetic  1.77 us (4%)
    pallas_call x4, Pallas kernels, body(): pl.pallas_call(lambda *refs, piece=piece: local_kernel(piece, *refs), gri...  9.18 us
    unnamed x23, local copies, waits for them, and re-layouts  5.99 us
    ppermute x3, starting transfers between devices, body(): lax.ppermute(chip_total.astype(BF), 'ctx', [(i, i ^ 2 << k) for i in rang...  5.88 us
    pallas_call x1, Pallas kernels, body(): pl.pallas_call(first_kernel, grid=(width // WIDE,), in_specs=[pl.BlockSpe...  5.79 us
    ppermute x2, starting transfers between devices, body(): lax.ppermute(value, 'ctx', [(i, i ^ 1) for i in range(blocks)])  2.77 us
    ppermute x1, starting transfers between devices, body(): lax.ppermute(feat[:, count - 2:], 'ctx', [(i, i + 1) for i in range(block...  2.36 us
    concatenate x1, other arithmetic, body(): return jnp.concatenate(done, axis=1)  1.49 us
    pallas_call x1, Pallas kernels, body(): pl.pallas_call(lambda *refs: plan_kernel(count, rounds, *refs), in_specs=...  1.46 us
  transfers between devices with their start and end apart: 6, of which 4 were waited for; matrix products, arithmetic and copies ran while one was open for 3% of the time, Pallas kernels for 40%

profile of v2, /device:TPU:0, one launch (start us, length us, event | category | flops | bytes accessed | tf_op | source)
XLA Modules:
  0.0 41.1 jit_solution(15843193510357324164)
XLA Ops:
  0.0 1.1 %fusion.12 = (bf16[3,2,4096]{2,1,0:T(2,128)(2,1)S(1)}, bf16[3,2,4096]{2,1,0:T(2,128)(2,1)S(1)}) fusion(bf16[3,256,4096]{2,1,0:T(8,128)(2,1)} %bitcast.63), kind=kLoop, calls=%fused_computation.31 | loop fusion | bytes 196608 | tf_op jit(solution)/shard_map/slice | solution.py:316
  1.1 2.4 %collective-permute-start = (bf16[3,2,4096]{2,1,0:T(2,128)(2,1)S(1)}, bf16[3,2,4096]{2,1,0:T(2,128)(2,1)S(1)}, u32[]{:S(2)}, u32[]{:S(2)}) collective-permute-start(bf16[3,2,4096]{2,1,0:T(2,128)(2,1)S(1)} %get-tuple-element.57), channel_id=1, source_target_pairs={{0,1},{1,2},{2,3},{3,4},{4,5},{5,6},{6,7},{7,8},{8,9},{9,10},{10,1... | collective-permute-start | bytes 147464 | tf_op jit(solution)/shard_map/ppermute | solution.py:316
  3.5 1.0 %copy.11 = f32[3,3,4096]{2,0,1:T(4,128)S(1)} copy(f32[3,3,4096]{2,1,0:T(4,128)} %param.9) | data formatting | bytes 294912 | tf_op args[1]
  4.5 0.7 %copy-done.2 = s32[4096]{0:T(1024)S(1)} copy-done((s32[4096]{0:T(1024)S(1)}, s32[4096]{0:T(1024)}, u32[]{:S(2)}) %copy-start.2) | copy-done | bytes 16408
  5.2 0.7 %copy-done.5 = f32[256,16]{0,1:T(8,128)S(1)} copy-done((f32[256,16]{0,1:T(8,128)S(1)}, f32[256,16]{0,1:T(8,128)}, u32[]{:S(2)}) %copy-start.5) | copy-done | bytes 16408
  6.0 0.7 %copy-done.7 = f32[256,16]{0,1:T(8,128)S(1)} copy-done((f32[256,16]{0,1:T(8,128)S(1)}, f32[256,16]{0,1:T(8,128)}, u32[]{:S(2)}) %copy-start.7) | copy-done | bytes 16408
  6.7 1.5 %plan.1 = (f32[16,4096]{1,0:T(8,128)S(1)}, f32[2,4096]{1,0:T(2,128)S(1)}, f32[5,256,128]{2,1,0:T(8,128)S(1)}, bf16[256,256]{1,0:T(8,128)(2,1)S(1)}, bf16[128,256...) custom-call(s32[1]{0:T(128)} %bitcast.refs_0_, s32[32,128]{1,0:T(8,128)S(1)} %bitcast.76, ...), custom_call_target="tpu_custom_call" | custom-call | tf_op jit(solution)/shard_map/plan/pallas_call | solution.py:318
  8.1 2.8 %copy-done = bf16[256,3,4096]{2,0,1:T(8,128)(2,1)S(1)} copy-done((bf16[256,3,4096]{2,0,1:T(8,128)(2,1)S(1)}, bf16[256,3,4096]{2,0,1:T(8,128)(2,1)}, u32[]{:S(2)}) %copy-start) | copy-done | bytes 6291480
  11.0 5.8 %first.1 = (bf16[256,4096]{1,0:T(8,128)(2,1)S(1)}, f32[16,4096]{1,0:T(8,128)S(1)}) custom-call(bf16[3,256,4096]{2,1,0:T(8,128)(2,1)S(1)} %bitcast.64, bf16[3,256,4096]{2,1,0:T(8,128)(2,1)S(1)} %bitcast.65, f32[3,3,4096]{2,1,0:T(4,128)S(1)} %bitcast.70, f32[2,4096]{1,0:T(2,128)S(1)} %get-tuple-element.32.flat_ref.refs_9_, ...), custom_call_target="tpu_custom_call" | custom-call | tf_op jit(solution)/shard_map/first/pallas_call | solution.py:330
  16.8 1.0 %head.1 = (bf16[2,16,2048]{2,1,0:T(8,128)(2,1)S(1)}, f32[2,4096]{1,0:T(2,128)S(1)}, f32[2,4096]{1,0:T(2,128)S(1)}) custom-call(s32[1]{0:T(128)} %bitcast.refs_0_, s32[4096]{0:T(1024)S(1)} %copy-done.3, bf16[3,2,4096]{2,1,0:T(2,128)(2,1)S(1)} %get-tuple-element.58.refs_2_, bf16[3,2,4096]{2,1,0:T(2,128)(2,1)S(1)} %collective-permute-done.refs_3_, ...), custom_call_target="tpu_custom_call" | custom-call | tf_op jit(solution)/shard_map/head/pallas_call | solution.py:346
  17.8 2.7 %collective-permute-start.1 = (bf16[2,16,2048]{2,1,0:T(8,128)(2,1)S(1)}, bf16[2,16,2048]{2,1,0:T(8,128)(2,1)S(1)}, u32[]{:S(2)}, u32[]{:S(2)}) collective-permute-start(bf16[2,16,2048]{2,1,0:T(8,128)(2,1)S(1)} %get-tuple-element.35), channel_id=1, source_target_pairs={{0,1},{1,0},{2,3},{3,2},{4,5},{5,4},{6,7},{7,6},{8,9},{9,8},{10,11... | collective-permute-start | bytes 393224 | tf_op jit(solution)/shard_map/ppermute | solution.py:380
  20.5 2.3 %local.7 = (f32[256,1024]{1,0:T(8,128)S(1)}, f32[256,1024]{1,0:T(8,128)S(1)}, bf16[256,1024]{1,0:T(8,128)(2,1)S(1)}) custom-call(bf16[256,4096]{1,0:T(8,128)(2,1)S(1)} %get-tuple-element.36.refs_0_, f32[2,4096]{1,0:T(2,128)S(1)} %get-tuple-element.37.refs_1_, bf16[3,256,4096]{2,1,0:T(8,128)(2,1)S(1)} %bitcast.66, f32[2,4096]{1,0:T(2,128)S(1)} %get-tuple-element.38.refs_3_, ...), custom_call_target="tpu_custom_call" | custom-call | flops 4294967296 | bytes 5242880 | tf_op jit(solution)/shard_map/local/pallas_call | solution.py:361
  22.9 1.6 %collective-permute-start.2 = (bf16[16,2048]{1,0:T(8,128)(2,1)S(1)}, bf16[16,2048]{1,0:T(8,128)(2,1)S(1)}, u32[]{:S(2)}, u32[]{:S(2)}) collective-permute-start(bf16[16,2048]{1,0:T(8,128)(2,1)S(1)} %get-tuple-element.55), channel_id=1, source_target_pairs={{0,2},{1,3},{2,0},{3,1},{4,6},{5,7},{6,4},{7,5},{8,10},{9,11},{10,... | collective-permute-start | bytes 196616 | tf_op jit(solution)/shard_map/ppermute | solution.py:387
  24.5 2.3 %local.6 = (f32[256,1024]{1,0:T(8,128)S(1)}, f32[256,1024]{1,0:T(8,128)S(1)}, bf16[256,1024]{1,0:T(8,128)(2,1)S(1)}) custom-call(bf16[256,4096]{1,0:T(8,128)(2,1)S(1)} %get-tuple-element.36.refs_0_, f32[2,4096]{1,0:T(2,128)S(1)} %get-tuple-element.37.refs_1_, bf16[3,256,4096]{2,1,0:T(8,128)(2,1)S(1)} %bitcast.67, f32[2,4096]{1,0:T(2,128)S(1)} %get-tuple-element.38.refs_3_, ...), custom_call_target="tpu_custom_call" | custom-call | flops 4294967296 | bytes 5242880 | tf_op jit(solution)/shard_map/local/pallas_call | solution.py:361
  26.8 0.5 %collective-permute-done.2 = bf16[16,2048]{1,0:T(8,128)(2,1)S(1)} collective-permute-done((bf16[16,2048]{1,0:T(8,128)(2,1)S(1)}, bf16[16,2048]{1,0:T(8,128)(2,1)S(1)}, u32[]{:S(2)}, u32[]{:S(2)}) %collective-permute-start.2) | collective-permute-done | bytes 65568 | tf_op jit(solution)/shard_map/ppermute | solution.py:387
  27.3 1.6 %collective-permute-start.3 = (bf16[16,2048]{1,0:T(8,128)(2,1)S(1)}, bf16[16,2048]{1,0:T(8,128)(2,1)S(1)}, u32[]{:S(2)}, u32[]{:S(2)}) collective-permute-start(bf16[16,2048]{1,0:T(8,128)(2,1)S(1)} %get-tuple-element.53), channel_id=1, source_target_pairs={{0,4},{1,5},{2,6},{3,7},{4,0},{5,1},{6,2},{7,3},{8,12},{9,13},{10,... | collective-permute-start | bytes 196616 | tf_op jit(solution)/shard_map/ppermute | solution.py:387
  29.0 2.3 %local.5 = (f32[256,1024]{1,0:T(8,128)S(1)}, f32[256,1024]{1,0:T(8,128)S(1)}, bf16[256,1024]{1,0:T(8,128)(2,1)S(1)}) custom-call(bf16[256,4096]{1,0:T(8,128)(2,1)S(1)} %get-tuple-element.36.refs_0_, f32[2,4096]{1,0:T(2,128)S(1)} %get-tuple-element.37.refs_1_, bf16[3,256,4096]{2,1,0:T(8,128)(2,1)S(1)} %bitcast.68, f32[2,4096]{1,0:T(2,128)S(1)} %get-tuple-element.38.refs_3_, ...), custom_call_target="tpu_custom_call" | custom-call | flops 4294967296 | bytes 5242880 | tf_op jit(solution)/shard_map/local/pallas_call | solution.py:361
  31.3 0.4 collective-permute-done.3
  31.7 2.7 %collective-permute-start.4 = (bf16[16,2048]{1,0:T(8,128)(2,1)S(1)}, bf16[16,2048]{1,0:T(8,128)(2,1)S(1)}, u32[]{:S(2)}, u32[]{:S(2)}) collective-permute-start(bf16[16,2048]{1,0:T(8,128)(2,1)S(1)} %fusion.7), channel_id=1, source_target_pairs={{0,8},{1,9},{2,10},{3,11},{4,12},{5,13},{6,14},{7,15},{8,0},{9,1},... | collective-permute-start | bytes 196616 | tf_op jit(solution)/shard_map/ppermute | solution.py:387
  34.3 2.3 %local.4 = (f32[256,1024]{1,0:T(8,128)S(1)}, f32[256,1024]{1,0:T(8,128)S(1)}, bf16[256,1024]{1,0:T(8,128)(2,1)S(1)}) custom-call(bf16[256,4096]{1,0:T(8,128)(2,1)S(1)} %get-tuple-element.36.refs_0_, f32[2,4096]{1,0:T(2,128)S(1)} %get-tuple-element.37.refs_1_, bf16[3,256,4096]{2,1,0:T(8,128)(2,1)S(1)} %bitcast.69, f32[2,4096]{1,0:T(2,128)S(1)} %get-tuple-element.38.refs_3_, ...), custom_call_target="tpu_custom_call" | custom-call | flops 4294967296 | bytes 5242880 | tf_op jit(solution)/shard_map/local/pallas_call | solution.py:361
  37.1 1.2 %collective-permute-done.5 = bf16[16,2048]{1,0:T(8,128)(2,1)S(1)} collective-permute-done((bf16[16,2048]{1,0:T(8,128)(2,1)S(1)}, bf16[16,2048]{1,0:T(8,128)(2,1)S(1)}, u32[]{:S(2)}, u32[]{:S(2)}) %collective-permute-start.5) | collective-permute-done | bytes 65568 | tf_op jit(solution)/shard_map/ppermute | solution.py:380
  38.7 0.3 last.6
  39.0 0.3 last.5
  39.7 1.5 %pad_maximum_fusion = bf16[256,4096]{1,0:T(8,128)(2,1)} fusion(bf16[256,1024]{1,0:T(8,128)(2,1)S(1)} %last.7, bf16[256,1024]{1,0:T(8,128)(2,1)S(1)} %last.6, bf16[256,1024]{1,0:T(8,128)(2,1)S(1)} %last.5, bf16[256,1024]{1,0:T(8,128)(2,1)S(1)} %last.4), kind=kLoop, calls=%fused_computation | loop fusion | flops 8388608 | bytes 4194304 | tf_op jit(solution)/shard_map/concatenate | solution.py:408
  (32 shorter events, 1.3 us)
Async XLA Ops:
  1.1 15.7 %collective-permute-start = (bf16[3,2,4096]{2,1,0:T(2,128)(2,1)S(1)}, bf16[3,2,4096]{2,1,0:T(2,128)(2,1)S(1)}, u32[]{:S(2)}, u32[]{:S(2)}) collective-permute-start(bf16[3,2,4096]{2,1,0:T(2,128)(2,1)S(1)} %get-tuple-element.57), channel_id=1, source_target_pairs={{0,1},{1,2},{2,3},{3,4},{4,5},{5,6},{6,7},{7,8},{8,9},{9,10},{10,1... | collective-permute-start | bytes 147464 | tf_op jit(solution)/shard_map/ppermute | solution.py:316
  4.5 0.7 %copy-start.2 = (s32[4096]{0:T(1024)S(1)}, s32[4096]{0:T(1024)}, u32[]{:S(2)}) copy-start(s32[4096]{0:T(1024)} %refs_1_.1) | copy-start | bytes 49156
  5.2 0.7 %copy-start.5 = (f32[256,16]{0,1:T(8,128)S(1)}, f32[256,16]{0,1:T(8,128)}, u32[]{:S(2)}) copy-start(f32[256,16]{0,1:T(8,128)} %param.11) | copy-start | bytes 49156
  6.0 0.7 %copy-start.7 = (f32[256,16]{0,1:T(8,128)S(1)}, f32[256,16]{0,1:T(8,128)}, u32[]{:S(2)}) copy-start(f32[256,16]{0,1:T(8,128)} %param.10) | copy-start | bytes 49156
  8.1 2.8 %copy-start = (bf16[256,3,4096]{2,0,1:T(8,128)(2,1)S(1)}, bf16[256,3,4096]{2,0,1:T(8,128)(2,1)}, u32[]{:S(2)}) copy-start(bf16[256,3,4096]{2,0,1:T(8,128)(2,1)} %param.8) | copy-start | bytes 18874372
  10.9 5.8 %copy-start.3 = (s32[4096]{0:T(1024)S(1)}, s32[4096]{0:T(1024)}, u32[]{:S(2)}) copy-start(s32[4096]{0:T(1024)} %refs_1_.1) | copy-start | bytes 49156
  10.9 5.9 %copy-start.4 = (bf16[2,3,4096]{2,0,1:T(2,128)(2,1)S(1)}, bf16[2,3,4096]{2,0,1:T(2,128)(2,1)}, u32[]{:S(2)}) copy-start(bf16[2,3,4096]{2,0,1:T(2,128)(2,1)} %param.14) | copy-start | bytes 147460
  10.9 9.6 %copy-start.1 = (bf16[256,3,4096]{2,0,1:T(8,128)(2,1)S(1)}, bf16[256,3,4096]{2,0,1:T(8,128)(2,1)}, u32[]{:S(2)}) copy-start(bf16[256,3,4096]{2,0,1:T(8,128)(2,1)} %param.8) | copy-start | bytes 18874372
  10.9 9.6 %copy-start.6 = (f32[256,16]{0,1:T(8,128)S(1)}, f32[256,16]{0,1:T(8,128)}, u32[]{:S(2)}) copy-start(f32[256,16]{0,1:T(8,128)} %param.11) | copy-start | bytes 49156
  10.9 9.6 %copy-start.8 = (f32[256,16]{0,1:T(8,128)S(1)}, f32[256,16]{0,1:T(8,128)}, u32[]{:S(2)}) copy-start(f32[256,16]{0,1:T(8,128)} %param.10) | copy-start | bytes 49156
  10.9 9.6 %copy-start.9 = (f32[4096]{0:T(1024)S(1)}, f32[4096]{0:T(1024)}, u32[]{:S(2)}) copy-start(f32[4096]{0:T(1024)} %param.12) | copy-start | bytes 49156
  17.8 5.0 %collective-permute-start.1 = (bf16[2,16,2048]{2,1,0:T(8,128)(2,1)S(1)}, bf16[2,16,2048]{2,1,0:T(8,128)(2,1)S(1)}, u32[]{:S(2)}, u32[]{:S(2)}) collective-permute-start(bf16[2,16,2048]{2,1,0:T(8,128)(2,1)S(1)} %get-tuple-element.35), channel_id=1, source_target_pairs={{0,1},{1,0},{2,3},{3,2},{4,5},{5,4},{6,7},{7,6},{8,9},{9,8},{10,11... | collective-permute-start | bytes 393224 | tf_op jit(solution)/shard_map/ppermute | solution.py:380
  22.9 4.3 %collective-permute-start.2 = (bf16[16,2048]{1,0:T(8,128)(2,1)S(1)}, bf16[16,2048]{1,0:T(8,128)(2,1)S(1)}, u32[]{:S(2)}, u32[]{:S(2)}) collective-permute-start(bf16[16,2048]{1,0:T(8,128)(2,1)S(1)} %get-tuple-element.55), channel_id=1, source_target_pairs={{0,2},{1,3},{2,0},{3,1},{4,6},{5,7},{6,4},{7,5},{8,10},{9,11},{10,... | collective-permute-start | bytes 196616 | tf_op jit(solution)/shard_map/ppermute | solution.py:387
  27.3 4.3 %collective-permute-start.3 = (bf16[16,2048]{1,0:T(8,128)(2,1)S(1)}, bf16[16,2048]{1,0:T(8,128)(2,1)S(1)}, u32[]{:S(2)}, u32[]{:S(2)}) collective-permute-start(bf16[16,2048]{1,0:T(8,128)(2,1)S(1)} %get-tuple-element.53), channel_id=1, source_target_pairs={{0,4},{1,5},{2,6},{3,7},{4,0},{5,1},{6,2},{7,3},{8,12},{9,13},{10,... | collective-permute-start | bytes 196616 | tf_op jit(solution)/shard_map/ppermute | solution.py:387
  31.7 6.6 %copy-start.10 = (f32[16,4096]{1,0:T(8,128)S(1)}, f32[16,4096]{1,0:T(8,128)}, u32[]{:S(2)}) copy-start(f32[16,4096]{1,0:T(8,128)} %param.13) | copy-start | bytes 786436
  31.7 5.2 %collective-permute-start.4 = (bf16[16,2048]{1,0:T(8,128)(2,1)S(1)}, bf16[16,2048]{1,0:T(8,128)(2,1)S(1)}, u32[]{:S(2)}, u32[]{:S(2)}) collective-permute-start(bf16[16,2048]{1,0:T(8,128)(2,1)S(1)} %fusion.7), channel_id=1, source_target_pairs={{0,8},{1,9},{2,10},{3,11},{4,12},{5,13},{6,14},{7,15},{8,0},{9,1},... | collective-permute-start | bytes 196616 | tf_op jit(solution)/shard_map/ppermute | solution.py:387
  37.0 1.3 %collective-permute-start.5 = (bf16[16,2048]{1,0:T(8,128)(2,1)S(1)}, bf16[16,2048]{1,0:T(8,128)(2,1)S(1)}, u32[]{:S(2)}, u32[]{:S(2)}) collective-permute-start(bf16[16,2048]{1,0:T(8,128)(2,1)S(1)} %fusion.4), channel_id=1, source_target_pairs={{0,1},{1,0},{2,3},{3,2},{4,5},{5,4},{6,7},{7,6},{8,9},{9,8},{10,11... | collective-permute-start | bytes 196616 | tf_op jit(solution)/shard_map/ppermute | solution.py:380

commit v3 on v2

v3 whole, which is shorter than its diff:
```python
import jax
import jax.numpy as jnp
from jax import lax
from jax.experimental import pallas as pl
from jax.experimental.pallas import tpu as pltpu
from jax.sharding import PartitionSpec as P

BF = jnp.bfloat16
F32 = jnp.float32
LANES = 128
SET = 256
WIDE = 1024
SUB = 32


def iota(shape, dim):
    return lax.broadcasted_iota(jnp.int32, shape, dim)


def flag(x):
    return x.astype(F32)


def split3(x):
    hi = x.astype(BF)
    rest = x - hi.astype(F32)
    mid = rest.astype(BF)
    low = (rest - mid.astype(F32)).astype(BF)
    return [hi, mid, low]


def spread_out(values, onehot):
    rows = values[0].shape[0]
    pieces = sum([split3(value) for value in values], [])
    got = jnp.dot(jnp.concatenate(pieces, axis=0), onehot, preferred_element_type=F32)
    part = lambda i: got[i * rows : (i + 1) * rows]
    return [(part(3 * i) + part(3 * i + 1)) + part(3 * i + 2) for i in range(len(values))]


def first_kernel(pos_ref, seg_hbm, rates_hbm, feat_ref, taps_hbm,
                 u_ref, q_ref, sum_ref, rate_ref, flat_ref, edge_ref, col_ref, shift_ref, taps_ref,
                 keep_ref, kv_ref, seg_ref, rates_ref, sems):
    pos = pos_ref[0]
    count, width = u_ref.shape
    modes = sum_ref.shape[0]
    members = SET // modes
    chunks = width // WIDE

    def copies(chunk):
        at = slice(chunk * WIDE, (chunk + 1) * WIDE)
        return [
            pltpu.make_async_copy(feat_ref.at[1 + i, :, at], kv_ref.at[i, :, at], sems.at[2 * chunk + i])
            for i in range(2)
        ]

    small = [
        pltpu.make_async_copy(source, target, sems.at[2 * chunks + i])
        for i, (source, target) in enumerate(((seg_hbm, seg_ref), (rates_hbm, rates_ref), (taps_hbm, taps_ref)))
    ]
    q_copy = pltpu.make_async_copy(feat_ref.at[0], q_ref, sems.at[2 * chunks + 3])
    for copy in small:
        copy.start()
    for chunk in range(chunks):
        for copy in copies(chunk):
            copy.start()
    q_copy.start()
    for copy in small:
        copy.wait()

    @pl.when(pos >= 0)
    def _():
        token = iota((count, LANES), 0)
        halves, rows = [], []
        for part in range(count // LANES):
            row = seg_ref[pl.ds((count // LANES) * pos + part, 1), :].astype(F32)
            rows.append(row)
            halves.append(jnp.transpose(jnp.broadcast_to(row, (LANES, LANES))))
        col = jnp.concatenate(halves, axis=0)
        before = seg_ref[pl.ds(jnp.maximum((count // LANES) * pos - 1, 0), 1), :].astype(F32)
        before = jnp.where(pos == 0, 0.0, before)
        last = jnp.broadcast_to(before[:, LANES - 1 :], (1, LANES))
        end = jnp.broadcast_to(rows[-1][:, LANES - 1 :], (1, LANES))
        col_ref[0] = flag(col == last)
        col_ref[1] = col
        keep_ref[...] = flag((col == end) & (token >= 2)).astype(BF)
        every = jnp.concatenate(rows, axis=1)
        there = jnp.concatenate([col] * (count // LANES), axis=1)
        gap = iota((count, count), 0) - iota((count, count), 1)
        for step in (1, 2):
            shift_ref[(step - 1) * count : step * count, :] = flag((gap == step) & (there == every)).astype(BF)

        per = LANES * members
        onehot = flag(iota((LANES, per), 0) == iota((LANES, per), 1) // members).astype(BF)
        pick = iota((modes, per), 0) == lax.rem(iota((modes, per), 1), modes)
        for block in range(width // per):
            at = slice(block * LANES, (block + 1) * LANES)
            to = slice(block * per, (block + 1) * per)
            (rate,) = spread_out([rates_ref[:, at]], onehot)
            rate_ref[:, to] = rate
            flat_ref[:, to] = jnp.sum(jnp.where(pick, rate, 0.0), axis=0, keepdims=True)

    owner = iota((modes, LANES), 1) // members
    spans = count // SUB

    def two_tiles(start):
        both = pl.ds(start, SET)
        shifted = []
        for index in (1, 2):
            edge_ref[2 * index - 2 : 2 * index, both] = kv_ref[index - 1, :16, both].astype(F32)[:2]
            shifted.append(jnp.dot(shift_ref[...], kv_ref[index - 1, :, both], preferred_element_type=F32))
        for part in range(SET // LANES):
            at = pl.ds(start + part * LANES, LANES)
            cut = slice(part * LANES, (part + 1) * LANES)
            made = []
            for index in (1, 2):
                moved = shifted[index - 1]
                made.append(
                    taps_ref[0, index : index + 1, at] * kv_ref[index - 1, :, at].astype(F32)
                    + taps_ref[1, index : index + 1, at] * moved[:count, cut]
                    + taps_ref[2, index : index + 1, at] * moved[count:, cut]
                )
            u = (made[0] * made[1]).astype(BF)
            u_ref[:, at] = u

    def sums_of(start):
        at = pl.ds(start, SET)
        rflat = flat_ref[:, at]
        fine = jnp.exp(-rflat * (SUB - 1.0 - iota((SUB, SET), 0).astype(F32)))
        coarse = jnp.exp(-rflat * (SUB * (spans - 1.0 - iota((spans, SET), 0).astype(F32))))
        decay = jnp.concatenate([(coarse[a : a + 1] * fine).astype(BF) for a in range(spans)], axis=0)
        decay = decay * jnp.concatenate([keep_ref[...]] * (SET // LANES), axis=1)
        sums = lax.dot_general(decay, u_ref[:, at], (((0,), (0,)), ((), ())), preferred_element_type=F32)
        for part in range(SET // LANES):
            cut = slice(part * LANES, (part + 1) * LANES)
            total = jnp.zeros((modes, LANES), F32)
            for g in range(LANES // members):
                row = part * LANES + g * modes
                total = jnp.where(owner == g, sums[row : row + modes, cut], total)
            sum_ref[:, pl.ds(start + part * LANES, LANES)] = total

    for chunk in range(chunks):
        for copy in copies(chunk):
            copy.wait()

        @pl.when(pos >= 0)
        def _():
            for i in range(WIDE // SET):
                two_tiles(chunk * WIDE + i * SET)

    @pl.when(pos >= 0)
    def _():
        for i in range(width // SET):
            sums_of(i * SET)

    q_copy.wait()


def head_kernel(count, pos_ref, seg_ref, edge_ref, halo_ref, early_ref, sw_ref, rate_ref, sum_ref, u_ref, q_ref,
                total_ref, head_ref, use_ref):
    pos = pos_ref[0]
    width = rate_ref.shape[1]
    per = count // LANES
    row = seg_ref[pl.ds(per * pos, 1), :]
    tail = seg_ref[pl.ds(per * pos + per - 1, 1), :]
    before = seg_ref[pl.ds(jnp.maximum(per * pos - 1, 0), 1), :]
    before = jnp.where(pos == 0, 0, before)
    s0, s1 = row[:, 0:1], row[:, 1:2]
    end = tail[:, LANES - 1 :]
    p1, p2 = before[:, LANES - 1 :], before[:, LANES - 2 : LANES - 1]
    same = lambda a, b: jnp.broadcast_to(flag(a == b), (1, width))
    near, far = same(p1, s0), same(p2, s0)
    step, skip = same(s0, s1), same(p1, s1)
    made = []
    for index in (0, 1, 2):
        h = jnp.where(pos == 0, early_ref[index].astype(F32), halo_ref[index].astype(F32))
        h2, h1 = h[0:1], h[1:2]
        w = [sw_ref[j, index : index + 1, :] for j in range(3)]
        if index == 0:
            use_ref[0:1, :] = w[1] * (near * h1) + w[2] * (far * h2)
            use_ref[1:2, :] = w[2] * (skip * h1)
            continue
        x0, x1 = edge_ref[2 * index - 2 : 2 * index - 1], edge_ref[2 * index - 1 : 2 * index]
        f0 = w[0] * x0 + w[1] * (near * h1) + w[2] * (far * h2)
        f1 = w[0] * x1 + w[1] * (step * x0) + w[2] * (skip * h1)
        made.append((f0, f1))
    u0 = (made[0][0] * made[1][0]).astype(BF).astype(F32)
    u1 = (made[0][1] * made[1][1]).astype(BF).astype(F32)
    head_ref[0:1, :] = u0
    head_ref[1:2, :] = u1
    u0 = same(s0, end) * u0
    u1 = same(s1, end) * u1
    half = width // 2
    for part in range(2):
        at = slice(part * half, (part + 1) * half)
        rate = rate_ref[:, at]
        drop = jnp.exp(-rate * (count - 2.0))
        total_ref[part] = (sum_ref[:, at] + drop * (u1[:, at] + jnp.exp(-rate) * u0[:, at])).astype(BF)


def plan_kernel(count, rounds, pos_ref, seg_ref, ids_ref, rates_ref, res_ref, rate_ref, col_ref, u_ref, q_ref,
                wide_ref, lead_ref, tri_ref, keep_ref, half_ref, full_ref):
    pos = pos_ref[0]
    modes = rates_ref.shape[0]
    width = rate_ref.shape[1]
    members = width // rates_ref.shape[1]

    def seg_at(spot):
        at = jnp.maximum(spot, 0)
        return jnp.where(spot < 0, 0, ids_ref[at])

    first = pos * count
    col = col_ref[1]
    start = iota((count, LANES), 0) // SUB
    lead = jnp.zeros((count, LANES), F32)
    for c in range(count // SUB):
        lead = jnp.where(start == c, seg_at(first + c * SUB - 1).astype(F32), lead)
    lead_ref[...] = flag(col == lead)
    inner = lax.rem(iota((SUB, SET), 1), SUB)
    tall = iota((SUB, SET), 0)
    for c in range(count // SUB):
        row = seg_ref[pl.ds((count // LANES) * pos + c * SUB // LANES, 1), :].astype(F32)
        shift = (c * SUB) % LANES
        base = row if shift == 0 else pltpu.roll(row, LANES - shift, 1)
        base = jnp.where(iota((1, LANES), 1) < SUB, base, 0.0)
        base = base + pltpu.roll(base, SUB, 1)
        base = base + pltpu.roll(base, 2 * SUB, 1)
        base = jnp.concatenate([base] * (SET // LANES), axis=1)
        mine = jnp.concatenate([col[c * SUB : (c + 1) * SUB]] * (SET // LANES), axis=1)
        tri_ref[c * SUB : (c + 1) * SUB, :] = flag((tall >= inner) & (mine == base)).astype(BF)
        keep_ref[c * modes : (c + 1) * modes, :] = jnp.broadcast_to(
            flag(base == ids_ref[first + (c + 1) * SUB - 1].astype(F32)), (modes, SET)).astype(BF)
    weight = res_ref[...] * jnp.sqrt(rates_ref[...])
    per = LANES * members
    onehot = flag(iota((LANES, per), 0) == iota((LANES, per), 1) // members).astype(BF)
    pick = iota((modes, per), 0) == lax.rem(iota((modes, per), 1), modes)
    for block in range(width // per):
        at = slice(block * LANES, (block + 1) * LANES)
        to = slice(block * per, (block + 1) * per)
        (spread,) = spread_out([weight[:, at]], onehot)
        wide_ref[:, to] = jnp.sum(jnp.where(pick, spread, 0.0), axis=0, keepdims=True)

    def decay(rate, low, high):
        alive = flag(seg_at(low * count - 1) == seg_at(high * count - 1))
        return jnp.exp(-rate * (count * (high - low)).astype(F32)) * alive

    core = lax.rem(pos, 2)
    chip = pos // 2
    rate = rate_ref[:, pl.ds(pl.multiple_of(core * (width // 2), LANES), width // 2)]
    half_ref[0] = decay(rate, 2 * chip + 1, 2 * chip + 2)
    spot = 1
    reach = 1
    for radix in rounds:
        size = reach * radix
        top = 2 * (chip // size) * size + 2 * size
        own = 2 * (chip // reach) * reach + 2 * reach
        half_ref[spot] = decay(rate, own, top)
        for other in range(1, radix):
            group = (chip // reach) ^ other
            finish = 2 * (group + 1) * reach
            ahead = group < chip // reach
            half_ref[spot + 1] = flag(ahead) * decay(rate, jnp.where(ahead, finish, 0), 2 * chip)
            half_ref[spot + 2] = decay(rate, finish, top)
            spot += 2
        spot += 1
        reach = size
    rate = rate_ref[...]
    full_ref[0] = jnp.where(core == 0, 1.0, decay(rate, 2 * chip, 2 * chip + 1))
    full_ref[1] = decay(rate, jnp.zeros_like(pos), pos)


def local_kernel(base, u_ref, head_ref, q_ref, halo_ref, sw_ref, skip_ref, rates_ref, res_ref, rate_ref, flat_ref,
                 wide_ref, lead_ref, col_ref, shift_ref, tri_ref, keep_ref, out_ref, gate_ref, cross_ref):
    count, wide = out_ref.shape
    modes = rates_ref.shape[0]
    members = 16
    groups = LANES // members
    spans = count // SUB
    first = base // members
    block = slice(first // LANES * LANES, first // LANES * LANES + LANES)
    cols = wide // members * SUB
    lane = iota((1, cols), 1)
    rates = rates_ref[:, block]
    weight = res_ref[:, block] * jnp.sqrt(rates)
    filt = lane // SUB + first % LANES
    onehot = flag(iota((LANES, cols), 0) == filt).astype(BF)
    (rate_to_end,) = spread_out([rates], onehot)
    decays = jnp.exp(-rate_to_end * (SUB - 1.0 - lax.rem(lane, SUB).astype(F32))).astype(BF)
    spot = lax.rem(lane, LANES)
    within = lax.rem((spot + SUB - 1) // SUB, LANES // SUB)
    lag = jnp.where(spot == 0, 0, lax.rem(SUB - lax.rem(spot, SUB), SUB)).astype(F32)
    filt = (lane // LANES) * (LANES // SUB) + within + first % LANES
    onehot = flag(iota((LANES, cols), 0) == filt).astype(BF)
    rate_tap, weight_tap = spread_out([rates, weight], onehot)
    taps = jnp.sum(weight_tap * jnp.exp(-rate_tap * lag), axis=0, keepdims=True)

    token = iota((16, LANES), 0)
    pad = lambda x, rows: jnp.concatenate([x, jnp.zeros((rows - x.shape[0], x.shape[1]), F32)], axis=0)
    owns = flag(iota((groups * SUB, LANES), 0) // SUB == iota((groups * SUB, LANES), 1) // members).astype(BF)
    holds = flag(iota((groups * modes, LANES), 0) // modes == iota((groups * modes, LANES), 1) // members).astype(BF)
    for tile in range(wide // LANES):
        at = slice(tile * LANES, (tile + 1) * LANES)
        to = slice(base + tile * LANES, base + (tile + 1) * LANES)
        ub = u_ref[:, to]
        start = jnp.where(token < 2, pad(head_ref[:, to], 16), ub[:16].astype(F32)).astype(BF)
        ub = jnp.concatenate([start, ub[16:]], axis=0)
        rflat, wflat = flat_ref[:, to], wide_ref[:, to]
        near = []
        for part in range(SET // LANES):
            row = taps[:, tile * SET + part * LANES : tile * SET + (part + 1) * LANES]
            near.append(pltpu.roll(jnp.broadcast_to(row, (SUB, LANES)), 0, 1, stride=1, stride_axis=0))
        near = jnp.concatenate(near, axis=1).astype(BF)
        ends = decays[:, tile * SET : (tile + 1) * SET]
        table = wflat * jnp.exp(-rflat * (iota((SUB, LANES), 0).astype(F32) + 1.0))
        fall = jnp.exp(-rate_ref[:, to] * float(SUB))
        far = jnp.exp(-rflat * (SUB * iota((spans, LANES), 0).astype(F32)))
        inner, sums = [], []
        for c in range(spans):
            rows = slice(c * SUB, (c + 1) * SUB)
            left = jnp.concatenate([near * tri_ref[rows], ends * keep_ref[c * 16 : (c + 1) * 16]], axis=0)
            right = jnp.concatenate([ub[rows]] * groups, axis=0) * owns
            got = jnp.dot(left, right, preferred_element_type=F32)
            inner.append(got[:SUB])
            sums.append(got[SUB:])
            cross_ref[rows, at] = (table * far[c : c + 1] * col_ref[0, rows]).astype(BF)
        state = sums[0]
        local = [inner[0]]
        for c in range(1, spans):
            rows = slice(c * SUB, (c + 1) * SUB)
            reach = lead_ref[rows]
            right = jnp.concatenate([state.astype(BF)] * groups, axis=0) * holds
            local.append(inner[c] + jnp.dot((table * reach).astype(BF), right, preferred_element_type=F32))
            state = fall * reach[SUB - 1 :] * state + sums[c]
        out_ref[:, at] = jnp.concatenate(local, axis=0) + skip_ref[:, to] * ub.astype(F32)
    for part in range(wide // SET):
        at = slice(part * SET, (part + 1) * SET)
        to = slice(base + part * SET, base + (part + 1) * SET)
        moved = jnp.dot(shift_ref[...], q_ref[:, to], preferred_element_type=F32)
        q = (
            sw_ref[0, 0:1, to] * q_ref[:, to].astype(F32)
            + sw_ref[1, 0:1, to] * moved[:count]
            + sw_ref[2, 0:1, to] * moved[count:]
        )
        q = jnp.concatenate([q[:8] + pad(halo_ref[:, to], 8), q[8:]], axis=0)
        gate_ref[:, at] = q
        out_ref[:, at] = q * out_ref[:, at]


def last_kernel(pieces, state_ref, *refs):
    modes = state_ref.shape[0]
    members = 16
    groups = SET // members
    owner = iota((modes, SET), 1) // members
    out_ref, made_ref, sems = refs[3 * pieces :]
    copies = []
    for piece in range(pieces):
        part_ref, gate_ref, table_ref = refs[3 * piece : 3 * piece + 3]
        wide = part_ref.shape[1]
        for half in range(wide // SET):
            at = slice(half * SET, (half + 1) * SET)
            to = slice(piece * wide + half * SET, piece * wide + (half + 1) * SET)
            state = state_ref[:, to]
            spread = jnp.concatenate([jnp.where(owner == g, state, 0.0).astype(BF) for g in range(groups)], axis=0)
            cross = jnp.dot(table_ref[:, at], spread, preferred_element_type=F32)
            made_ref[:, to] = (part_ref[:, at] + gate_ref[:, at] * cross).astype(BF)
        to = slice(piece * wide, (piece + 1) * wide)
        copies.append(pltpu.make_async_copy(made_ref.at[:, to], out_ref.at[:, to], sems.at[piece]))
        copies[-1].start()
    for copy in copies:
        copy.wait()


def params(limit=16 << 20):
    return pltpu.CompilerParams(vmem_limit_bytes=limit)


def body(features, short_weight, residues, rates, skip, carry_state, earlier_rows, segment_ids):
    count, _, width = features.shape
    groups, modes = rates.shape
    blocks = lax.axis_size("ctx")
    pos = lax.axis_index("ctx")
    pos1 = pos.reshape(1)
    chips = blocks // 2
    bits = chips.bit_length() - 1
    rounds = ([4] if bits > 1 else []) + [2] * (bits - 2 if bits > 1 else bits)
    assert blocks == 2 << bits and count == 2 * LANES and width == 16 * groups and modes == 16
    feat = jnp.transpose(features, (1, 0, 2))
    early = jnp.transpose(earlier_rows, (1, 0, 2))
    segs = segment_ids.reshape(-1, LANES)
    rates_t = rates.T
    res_t = residues.T
    skip = skip.reshape(1, width)
    vm = pl.BlockSpec(memory_space=pltpu.VMEM)
    sm = pl.BlockSpec(memory_space=pltpu.SMEM)
    out = lambda *shape, dtype=F32: jax.ShapeDtypeStruct(shape, dtype)
    stay = lambda value: pltpu.with_memory_space_constraint(value, pltpu.HBM)
    swap = lambda value, by: lax.ppermute(value, "ctx", [(i, i ^ by) for i in range(blocks)])
    tie = lambda *values: lax.optimization_barrier(values)

    halo = lax.ppermute(feat[:, count - 2 :], "ctx", [(i, i + 1) for i in range(blocks - 1)])

    hbm = pl.BlockSpec(memory_space=pltpu.HBM)
    u, q, sums, rate, flat, edge, cols, shifts, weights = pl.pallas_call(
        first_kernel,
        in_specs=[sm, hbm, hbm, hbm, hbm],
        out_specs=[vm] * 9,
        out_shape=[out(count, width, dtype=BF), out(count, width, dtype=BF), out(modes, width), out(modes, width),
                   out(1, width), out(4, width), out(2, count, LANES), out(2 * count, count, dtype=BF),
                   out(*short_weight.shape)],
        scratch_shapes=[
            pltpu.VMEM((count, LANES), BF), pltpu.VMEM((2, count, width), BF), pltpu.VMEM(segs.shape, jnp.int32),
            pltpu.VMEM(rates_t.shape, F32), pltpu.SemaphoreType.DMA((2 * (width // WIDE) + 4,)),
        ],
        compiler_params=params(),
        name="first",
    )(pos1, stay(segs), stay(rates_t), stay(feat), stay(short_weight))

    total, head, halo_q = pl.pallas_call(
        lambda *refs: head_kernel(count, *refs),
        in_specs=[sm] + [vm] * 9,
        out_specs=[vm] * 3,
        out_shape=[out(2, modes, width // 2, dtype=BF), out(2, width), out(2, width)],
        compiler_params=params(),
        name="head",
    )(pos1, segs, edge, halo, early, weights, rate, sums, u, q)

    even = (pos & 1) == 0
    other = swap(total, 1)
    steps = 1 + sum(2 * radix - 1 for radix in rounds)
    wflat, lead, tris, keeps, halves, fulls = pl.pallas_call(
        lambda *refs: plan_kernel(count, rounds, *refs),
        in_specs=[sm, vm, sm] + [vm] * 6,
        out_specs=[vm] * 6,
        out_shape=[
            out(1, width), out(count, LANES), out(count, SET, dtype=BF), out(count // SUB * 16, SET, dtype=BF),
            out(steps, modes, width // 2), out(2, modes, width),
        ],
        compiler_params=params(),
        cost_estimate=pl.CostEstimate(flops=1 << 30, bytes_accessed=5 << 20, transcendentals=0),
        name="plan",
    )(pos1, segs, segment_ids, rates_t, res_t, rate, cols, u, q)

    pieces = width // WIDE
    parts = []

    def local(piece, head):
        return pl.pallas_call(
            lambda *refs: local_kernel(piece * WIDE, *refs),
            in_specs=[vm] * 16,
            out_specs=[vm] * 3,
            out_shape=[out(count, WIDE), out(count, WIDE), out(count, WIDE, dtype=BF)],
            compiler_params=params(),
            cost_estimate=pl.CostEstimate(flops=4 << 30, bytes_accessed=5 << 20, transcendentals=0),
            name="local",
        )(u, head, q, halo_q, weights, skip, rates_t, res_t, rate, flat, wflat, lead, cols, shifts, tris, keeps)

    low_total = jnp.where(even, total, other)
    own_half = lambda value: jnp.where(even, value[0], value[1]).astype(F32)
    chip_total = halves[0] * own_half(low_total) + own_half(jnp.where(even, other, total))
    chip_total, head = tie(chip_total, head)
    before = jnp.zeros_like(chip_total)
    spot, reach = 1, 1
    left = list(range(pieces))
    for number, radix in enumerate(rounds):
        sent = chip_total.astype(BF)
        got = [swap(sent, 2 * reach * i).astype(F32) for i in range(1, radix)]
        share = -(-len(left) // (len(rounds) - number))
        for piece in left[:share]:
            parts.append(local(piece, head))
        left = left[share:]
        got, parts, head = tie(got, parts, head)
        chip_total = halves[spot] * chip_total
        for i in range(radix - 1):
            before = before + halves[spot + 1 + 2 * i] * got[i]
            chip_total = chip_total + halves[spot + 2 + 2 * i] * got[i]
        spot += 2 * radix - 1
        reach *= radix
    mine = before.astype(BF)
    yours = swap(mine, 1)
    full = jnp.concatenate([jnp.where(even, mine, yours), jnp.where(even, yours, mine)], axis=1).astype(F32)
    low_full = jnp.where(even, 0.0, jnp.concatenate([low_total[0], low_total[1]], axis=1).astype(F32))
    state = fulls[0] * full + low_full + fulls[1] * carry_state

    return pl.pallas_call(
        lambda *refs: last_kernel(pieces, *refs),
        in_specs=[vm] * (1 + 3 * pieces),
        out_specs=hbm,
        out_shape=out(count, width, dtype=BF),
        scratch_shapes=[pltpu.VMEM((count, width), BF), pltpu.SemaphoreType.DMA((pieces,))],
        compiler_params=params(),
        name="last",
    )(state, *[value for piece in parts for value in piece])


def solution(mesh):
    placed = (
        P(("groups", "ctx"), None, None),
        P(),
        P(),
        P(),
        P(),
        P("groups", None),
        P("groups", None, None),
        P("groups"),
    )
    return jax.shard_map(
        body, mesh=mesh, in_specs=placed, out_specs=P(("groups", "ctx"), None), check_vma=False
    )
```

time: 41.6 us -> 36 us (0.87)
  local copies, waits for them, and re-layouts: 7.1 us -> 3.37 us
  other arithmetic: 1.77 us -> 0.33 us
  waiting for transfers between devices: 2.37 us -> 1.24 us
    unnamed x23 -> x16, local copies, waits for them, and re-layouts: 5.99 us -> 2.38 us
    concatenate x1 -> x0, other arithmetic: 1.49 us -> none  [body(): return jnp.concatenate(done, axis=1)]
    ppermute x5 -> x6, waiting for transfers between devices: 2.37 us -> 1.24 us  [body(): lax.ppermute(value, 'ctx', [(i, i ^ by) for i in range(blocks)])]
    pallas_call x10 -> x7, Pallas kernels: 17.2 us -> 17.7 us  [the longest x4 10 us: local(): pl.pallas_call(lambda *refs: local_kernel(piece * WIDE, *refs), in_specs=...]
    ppermute x5 -> x6, starting transfers between devices: 8.65 us -> 8.91 us  [body(): lax.ppermute(value, 'ctx', [(i, i ^ by) for i in range(blocks)])]
  transfers between devices with their start and end apart: 6 -> 7, of which waited for: 4 -> 1; matrix products, arithmetic and copies ran while one was open for 3% -> 0% of each run, Pallas kernels for 40% -> 47%
where the time goes in v3:
time: 36 us; the launch traced here: 35.8 us
  Pallas kernels  19.1 us (53%)
  starting transfers between devices  11.3 us (31%)
  local copies, waits for them, and re-layouts  3.37 us (9%)
  waiting for transfers between devices  1.24 us (3%)
  between operations  0.43 us (1%)
    pallas_call x4, Pallas kernels, local(): pl.pallas_call(lambda *refs: local_kernel(piece * WIDE, *refs), in_specs=...  10 us
    ppermute x6, starting transfers between devices, body(): lax.ppermute(value, 'ctx', [(i, i ^ by) for i in range(blocks)])  8.91 us
    pallas_call x1, Pallas kernels, body(): pl.pallas_call(first_kernel, in_specs=[sm, hbm, hbm, hbm, hbm], out_specs...  5.53 us
    unnamed x16, local copies, waits for them, and re-layouts  2.38 us
    ppermute x1, starting transfers between devices, body(): lax.ppermute(feat[:, count - 2:], 'ctx', [(i, i + 1) for i in range(block...  2.36 us
    pallas_call x1, Pallas kernels, body(): pl.pallas_call(lambda *refs: last_kernel(pieces, *refs), in_specs=[vm] *...  1.66 us
    pallas_call x1, Pallas kernels, body(): pl.pallas_call(lambda *refs: plan_kernel(count, rounds, *refs), in_specs=...  1.41 us
    ppermute x6, waiting for transfers between devices, body(): lax.ppermute(value, 'ctx', [(i, i ^ by) for i in range(blocks)])  1.24 us
  transfers between devices with their start and end apart: 7, of which 1 were waited for; matrix products, arithmetic and copies ran while one was open for 0% of the time, Pallas kernels for 47%

profile of v3, /device:TPU:0, one launch (start us, length us, event | category | flops | bytes accessed | tf_op | source)
XLA Modules:
  0.0 35.8 jit_solution(4671759827206727759)
XLA Ops:
  0.0 1.0 %slice.66 = bf16[3,2,4096]{2,1,0:T(2,128)(2,1)S(1)} slice(bf16[3,256,4096]{2,1,0:T(8,128)(2,1)} %bitcast.97), slice={[0:3], [254:256], [0:4096]} | slice | bytes 98304 | tf_op jit(solution)/shard_map/slice | solution.py:399
  1.0 2.4 %collective-permute-start = (bf16[3,2,4096]{2,1,0:T(2,128)(2,1)S(1)}, bf16[3,2,4096]{2,1,0:T(2,128)(2,1)S(1)}, u32[]{:S(2)}, u32[]{:S(2)}) collective-permute-start(bf16[3,2,4096]{2,1,0:T(2,128)(2,1)S(1)} %slice.66), channel_id=1, source_target_pairs={{0,1},{1,2},{2,3},{3,4},{4,5},{5,6},{6,7},{7,8},{8,9},{9,10},{10,1... | collective-permute-start | bytes 147464 | tf_op jit(solution)/shard_map/ppermute | solution.py:399
  3.4 0.0 copy-start.2
  3.4 0.0 copy-start.4
  3.4 5.5 %first.1 = (bf16[256,4096]{1,0:T(8,128)(2,1)S(1)}, bf16[256,4096]{1,0:T(8,128)(2,1)S(1)}, f32[16,4096]{1,0:T(8,128)S(1)}, f32[16,4096]{1,0:T(8,128)S(1)}, f32[1,...) custom-call(s32[1]{0:T(128)} %bitcast.pos_ref.refs_0_, ...), custom_call_target="tpu_custom_call" | custom-call | tf_op jit(solution)/shard_map/first/pallas_call | solution.py:402
  9.0 0.5 %head.1 = (bf16[2,16,2048]{2,1,0:T(8,128)(2,1)S(1)}, f32[2,4096]{1,0:T(2,128)S(1)}, f32[2,4096]{1,0:T(2,128)S(1)}) custom-call(s32[1]{0:T(128)} %bitcast.pos_ref.refs_0_, s32[32,128]{1,0:T(8,128)S(1)} %bitcast.79, f32[4,4096]{1,0:T(4,128)S(1)} %get-tuple-element.66.refs_2_, bf16[3,2,4096]{2,1,0:T(2,128)(2,1)S(1)} %collective-permute-done.refs_3_, ...), custom_call_target="tpu_custom_call" | custom-call | tf_op jit(solution)/shard_map/head/pallas_call | solution.py:417
  9.5 0.8 %copy-done = bf16[256,4096]{1,0:T(8,128)(2,1)} copy-done((bf16[256,4096]{1,0:T(8,128)(2,1)}, bf16[256,4096]{1,0:T(8,128)(2,1)S(1)}, u32[]{:S(2)}) %copy-start) | copy-done | bytes 2097176
  10.2 2.6 %collective-permute-start.1 = (bf16[2,16,2048]{2,1,0:T(8,128)(2,1)S(1)}, bf16[2,16,2048]{2,1,0:T(8,128)(2,1)S(1)}, u32[]{:S(2)}, u32[]{:S(2)}) collective-permute-start(bf16[2,16,2048]{2,1,0:T(8,128)(2,1)S(1)} %get-tuple-element.69), channel_id=1, source_target_pairs={{0,1},{1,0},{2,3},{3,2},{4,5},{5,4},{6,7},{7,6},{8,9},{9,8},{10,11... | collective-permute-start | bytes 393224 | tf_op jit(solution)/shard_map/ppermute | solution.py:396
  12.9 1.6 %copy-done.1 = bf16[256,4096]{1,0:T(8,128)(2,1)S(1)} copy-done((bf16[256,4096]{1,0:T(8,128)(2,1)S(1)}, bf16[256,4096]{1,0:T(8,128)(2,1)}, u32[]{:S(2)}) %copy-start.1) | copy-done | bytes 2097176
  14.5 1.4 %plan.1 = (f32[1,4096]{1,0:T(1,128)S(1)}, f32[256,128]{1,0:T(8,128)S(1)}, bf16[256,256]{1,0:T(8,128)(2,1)S(1)}, bf16[128,256]{1,0:T(8,128)(2,1)S(1)}, f32[11,16,...) custom-call(s32[1]{0:T(128)} %bitcast.pos_ref.refs_0_, s32[32,128]{1,0:T(8,128)S(1)} %bitcast.80, s32[4096]{0:T(1024)S(1)} %copy-done.2, ...), custom_call_target="tpu_custom_call" | custom-call | flops 1073741824 | bytes 5242880 | tf_op jit(solution)/shard_map/plan/pallas_call | solution.py:429
  16.0 1.6 %collective-permute-start.2 = (bf16[16,2048]{1,0:T(8,128)(2,1)S(1)}, bf16[16,2048]{1,0:T(8,128)(2,1)S(1)}, u32[]{:S(2)}, u32[]{:S(2)}) collective-permute-start(bf16[16,2048]{1,0:T(8,128)(2,1)S(1)} %convert_element_type.39), channel_id=1, source_target_pairs={{0,2},{1,3},{2,0},{3,1},{4,6},{5,7},{6,4},{7,5},{8,10},{9,11},{10,... | collective-permute-start | bytes 196616 | tf_op jit(solution)/shard_map/ppermute | solution.py:396
  17.6 1.6 %collective-permute-start.3 = (bf16[16,2048]{1,0:T(8,128)(2,1)S(1)}, bf16[16,2048]{1,0:T(8,128)(2,1)S(1)}, u32[]{:S(2)}, u32[]{:S(2)}) collective-permute-start(bf16[16,2048]{1,0:T(8,128)(2,1)S(1)} %convert_element_type.39), channel_id=1, source_target_pairs={{0,4},{1,5},{2,6},{3,7},{4,0},{5,1},{6,2},{7,3},{8,12},{9,13},{10,... | collective-permute-start | bytes 196616 | tf_op jit(solution)/shard_map/ppermute | solution.py:396
  19.2 0.4 %collective-permute-start.4 = (bf16[16,2048]{1,0:T(8,128)(2,1)S(1)}, bf16[16,2048]{1,0:T(8,128)(2,1)S(1)}, u32[]{:S(2)}, u32[]{:S(2)}) collective-permute-start(bf16[16,2048]{1,0:T(8,128)(2,1)S(1)} %convert_element_type.39), channel_id=1, source_target_pairs={{0,6},{1,7},{2,4},{3,5},{4,2},{5,3},{6,0},{7,1},{8,14},{9,15},{10,... | collective-permute-start | bytes 196616 | tf_op jit(solution)/shard_map/ppermute | solution.py:396
  19.6 2.5 %local.4 = (f32[256,1024]{1,0:T(8,128)S(1)}, f32[256,1024]{1,0:T(8,128)S(1)}, bf16[256,1024]{1,0:T(8,128)(2,1)S(1)}) custom-call(bf16[256,4096]{1,0:T(8,128)(2,1)S(1)} %get-tuple-element.62.refs_7_.refs_8_.refs_0_, f32[2,4096]{1,0:T(2,128)S(1)} %get-tuple-element.95.refs_1_, bf16[256,4096]{1,0:T(8,128)(2,1)S(1)} %copy-done.1, ...), custom_call_target="tpu_custom_call" | custom-call | flops 4294967296 | bytes 5242880 | tf_op jit(solution)/shard_map/local/pallas_call | solution.py:446
  22.1 2.5 %local.5 = (f32[256,1024]{1,0:T(8,128)S(1)}, f32[256,1024]{1,0:T(8,128)S(1)}, bf16[256,1024]{1,0:T(8,128)(2,1)S(1)}) custom-call(bf16[256,4096]{1,0:T(8,128)(2,1)S(1)} %get-tuple-element.62.refs_7_.refs_8_.refs_0_, f32[2,4096]{1,0:T(2,128)S(1)} %get-tuple-element.95.refs_1_, bf16[256,4096]{1,0:T(8,128)(2,1)S(1)} %copy-done.1, ...), custom_call_target="tpu_custom_call" | custom-call | flops 4294967296 | bytes 5242880 | tf_op jit(solution)/shard_map/local/pallas_call | solution.py:446
  24.7 0.1 fusion.3
  24.8 2.7 %collective-permute-start.5 = (bf16[16,2048]{1,0:T(8,128)(2,1)S(1)}, bf16[16,2048]{1,0:T(8,128)(2,1)S(1)}, u32[]{:S(2)}, u32[]{:S(2)}) collective-permute-start(bf16[16,2048]{1,0:T(8,128)(2,1)S(1)} %fusion.3), channel_id=1, source_target_pairs={{0,8},{1,9},{2,10},{3,11},{4,12},{5,13},{6,14},{7,15},{8,0},{9,1},... | collective-permute-start | bytes 196616 | tf_op jit(solution)/shard_map/ppermute | solution.py:396
  27.4 2.5 %local.6 = (f32[256,1024]{1,0:T(8,128)S(1)}, f32[256,1024]{1,0:T(8,128)S(1)}, bf16[256,1024]{1,0:T(8,128)(2,1)S(1)}) custom-call(bf16[256,4096]{1,0:T(8,128)(2,1)S(1)} %get-tuple-element.62.refs_7_.refs_8_.refs_0_, f32[2,4096]{1,0:T(2,128)S(1)} %get-tuple-element.95.refs_1_, bf16[256,4096]{1,0:T(8,128)(2,1)S(1)} %copy-done.1, ...), custom_call_target="tpu_custom_call" | custom-call | flops 4294967296 | bytes 5242880 | tf_op jit(solution)/shard_map/local/pallas_call | solution.py:446
  29.9 2.5 %local.7 = (f32[256,1024]{1,0:T(8,128)S(1)}, f32[256,1024]{1,0:T(8,128)S(1)}, bf16[256,1024]{1,0:T(8,128)(2,1)S(1)}) custom-call(bf16[256,4096]{1,0:T(8,128)(2,1)S(1)} %get-tuple-element.62.refs_7_.refs_8_.refs_0_, f32[2,4096]{1,0:T(2,128)S(1)} %get-tuple-element.95.refs_1_, bf16[256,4096]{1,0:T(8,128)(2,1)S(1)} %copy-done.1, ...), custom_call_target="tpu_custom_call" | custom-call | flops 4294967296 | bytes 5242880 | tf_op jit(solution)/shard_map/local/pallas_call | solution.py:446
  32.5 0.1 fusion.7
  32.5 0.1 collective-permute-start.6
  32.6 1.2 %collective-permute-done.6 = bf16[16,2048]{1,0:T(8,128)(2,1)S(1)} collective-permute-done((bf16[16,2048]{1,0:T(8,128)(2,1)S(1)}, bf16[16,2048]{1,0:T(8,128)(2,1)S(1)}, u32[]{:S(2)}, u32[]{:S(2)}) %collective-permute-start.6) | collective-permute-done | bytes 65568 | tf_op jit(solution)/shard_map/ppermute | solution.py:396
  33.9 0.1 fusion.refs_0_
  34.0 1.7 %last.1 = bf16[256,4096]{1,0:T(8,128)(2,1)} custom-call(f32[16,4096]{1,0:T(8,128)S(1)} %fusion.refs_0_, f32[256,1024]{1,0:T(8,128)S(1)} %get-tuple-element.103.refs_1_, f32[256,1024]{1,0:T(8,128)S(1)} %get-tuple-element.104.refs_2_, bf16[256,1024]{1,0:T(8,128)(2,1)S(1)} %get-tuple-element.105.refs_3_, f32[256,1024]{1,0:T(8,128)S(1)} %get-tuple-element.106.refs_4_, ...), custom_call_target="tpu_custom_call" | custom-call | tf_op jit(solution)/shard_map/last/pallas_call | solution.py:483
  (27 shorter events, 0.2 us)
Async XLA Ops:
  1.0 8.0 %collective-permute-start = (bf16[3,2,4096]{2,1,0:T(2,128)(2,1)S(1)}, bf16[3,2,4096]{2,1,0:T(2,128)(2,1)S(1)}, u32[]{:S(2)}, u32[]{:S(2)}) collective-permute-start(bf16[3,2,4096]{2,1,0:T(2,128)(2,1)S(1)} %slice.66), channel_id=1, source_target_pairs={{0,1},{1,2},{2,3},{3,4},{4,5},{5,6},{6,7},{7,8},{8,9},{9,10},{10,1... | collective-permute-start | bytes 147464 | tf_op jit(solution)/shard_map/ppermute | solution.py:399
  3.4 5.6 %copy-start.2 = (s32[4096]{0:T(1024)S(1)}, s32[4096]{0:T(1024)}, u32[]{:S(2)}) copy-start(s32[4096]{0:T(1024)} %refs_2_.1) | copy-start | bytes 49156
  3.4 5.6 %copy-start.4 = (bf16[2,3,4096]{2,0,1:T(2,128)(2,1)S(1)}, bf16[2,3,4096]{2,0,1:T(2,128)(2,1)}, u32[]{:S(2)}) copy-start(bf16[2,3,4096]{2,0,1:T(2,128)(2,1)} %param.14) | copy-start | bytes 147460
  8.9 1.3 %copy-start = (bf16[256,4096]{1,0:T(8,128)(2,1)}, bf16[256,4096]{1,0:T(8,128)(2,1)S(1)}, u32[]{:S(2)}) copy-start(bf16[256,4096]{1,0:T(8,128)(2,1)S(1)} %get-tuple-element.63.refs_8_.refs_9_.refs_2_) | copy-start | bytes 6291460
  9.0 3.9 %copy-start.3 = (f32[256,16]{0,1:T(8,128)S(1)}, f32[256,16]{0,1:T(8,128)}, u32[]{:S(2)}) copy-start(f32[256,16]{0,1:T(8,128)} %param.11) | copy-start | bytes 49156
  9.0 3.9 %copy-start.5 = (f32[256,16]{0,1:T(8,128)S(1)}, f32[256,16]{0,1:T(8,128)}, u32[]{:S(2)}) copy-start(f32[256,16]{0,1:T(8,128)} %param.10) | copy-start | bytes 49156
  10.2 5.7 %collective-permute-start.1 = (bf16[2,16,2048]{2,1,0:T(8,128)(2,1)S(1)}, bf16[2,16,2048]{2,1,0:T(8,128)(2,1)S(1)}, u32[]{:S(2)}, u32[]{:S(2)}) collective-permute-start(bf16[2,16,2048]{2,1,0:T(8,128)(2,1)S(1)} %get-tuple-element.69), channel_id=1, source_target_pairs={{0,1},{1,0},{2,3},{3,2},{4,5},{5,4},{6,7},{7,6},{8,9},{9,8},{10,11... | collective-permute-start | bytes 393224 | tf_op jit(solution)/shard_map/ppermute | solution.py:396
  12.9 1.6 %copy-start.1 = (bf16[256,4096]{1,0:T(8,128)(2,1)S(1)}, bf16[256,4096]{1,0:T(8,128)(2,1)}, u32[]{:S(2)}) copy-start(bf16[256,4096]{1,0:T(8,128)(2,1)} %copy-done) | copy-start | bytes 6291460
  14.5 5.1 %copy-start.6 = (f32[4096]{0:T(1024)S(1)}, f32[4096]{0:T(1024)}, u32[]{:S(2)}) copy-start(f32[4096]{0:T(1024)} %param.12) | copy-start | bytes 49156
  16.0 8.6 %collective-permute-start.2 = (bf16[16,2048]{1,0:T(8,128)(2,1)S(1)}, bf16[16,2048]{1,0:T(8,128)(2,1)S(1)}, u32[]{:S(2)}, u32[]{:S(2)}) collective-permute-start(bf16[16,2048]{1,0:T(8,128)(2,1)S(1)} %convert_element_type.39), channel_id=1, source_target_pairs={{0,2},{1,3},{2,0},{3,1},{4,6},{5,7},{6,4},{7,5},{8,10},{9,11},{10,... | collective-permute-start | bytes 196616 | tf_op jit(solution)/shard_map/ppermute | solution.py:396
  17.6 7.0 %collective-permute-start.3 = (bf16[16,2048]{1,0:T(8,128)(2,1)S(1)}, bf16[16,2048]{1,0:T(8,128)(2,1)S(1)}, u32[]{:S(2)}, u32[]{:S(2)}) collective-permute-start(bf16[16,2048]{1,0:T(8,128)(2,1)S(1)} %convert_element_type.39), channel_id=1, source_target_pairs={{0,4},{1,5},{2,6},{3,7},{4,0},{5,1},{6,2},{7,3},{8,12},{9,13},{10,... | collective-permute-start | bytes 196616 | tf_op jit(solution)/shard_map/ppermute | solution.py:396
  19.2 5.5 %collective-permute-start.4 = (bf16[16,2048]{1,0:T(8,128)(2,1)S(1)}, bf16[16,2048]{1,0:T(8,128)(2,1)S(1)}, u32[]{:S(2)}, u32[]{:S(2)}) collective-permute-start(bf16[16,2048]{1,0:T(8,128)(2,1)S(1)} %convert_element_type.39), channel_id=1, source_target_pairs={{0,6},{1,7},{2,4},{3,5},{4,2},{5,3},{6,0},{7,1},{8,14},{9,15},{10,... | collective-permute-start | bytes 196616 | tf_op jit(solution)/shard_map/ppermute | solution.py:396
  24.8 7.7 %collective-permute-start.5 = (bf16[16,2048]{1,0:T(8,128)(2,1)S(1)}, bf16[16,2048]{1,0:T(8,128)(2,1)S(1)}, u32[]{:S(2)}, u32[]{:S(2)}) collective-permute-start(bf16[16,2048]{1,0:T(8,128)(2,1)S(1)} %fusion.3), channel_id=1, source_target_pairs={{0,8},{1,9},{2,10},{3,11},{4,12},{5,13},{6,14},{7,15},{8,0},{9,1},... | collective-permute-start | bytes 196616 | tf_op jit(solution)/shard_map/ppermute | solution.py:396
  29.9 4.0 %copy-start.7 = (f32[16,4096]{1,0:T(8,128)S(1)}, f32[16,4096]{1,0:T(8,128)}, u32[]{:S(2)}) copy-start(f32[16,4096]{1,0:T(8,128)} %param.13) | copy-start | bytes 786436
  32.5 1.3 %collective-permute-start.6 = (bf16[16,2048]{1,0:T(8,128)(2,1)S(1)}, bf16[16,2048]{1,0:T(8,128)(2,1)S(1)}, u32[]{:S(2)}, u32[]{:S(2)}) collective-permute-start(bf16[16,2048]{1,0:T(8,128)(2,1)S(1)} %fusion.7), channel_id=1, source_target_pairs={{0,1},{1,0},{2,3},{3,2},{4,5},{5,4},{6,7},{7,6},{8,9},{9,8},{10,11... | collective-permute-start | bytes 196616 | tf_op jit(solution)/shard_map/ppermute | solution.py:396

commit v4 on v3

--- a/solution.py
+++ b/solution.py
@@ -38,8 +38,8 @@
 
 
 def first_kernel(pos_ref, seg_hbm, rates_hbm, feat_ref, taps_hbm,
-                 u_ref, q_ref, sum_ref, rate_ref, flat_ref, edge_ref, col_ref, shift_ref, taps_ref,
-                 keep_ref, kv_ref, seg_ref, rates_ref, sems):
+                 u_ref, q_ref, sum_ref, rate_ref, flat_ref, edge_ref, col_ref, taps_ref,
+                 keep_ref, shift_ref, kv_ref, seg_ref, rates_ref, sems):
     pos = pos_ref[0]
     count, width = u_ref.shape
     modes = sum_ref.shape[0]
@@ -83,6 +83,8 @@
         col_ref[0] = flag(col == last)
         col_ref[1] = col
         keep_ref[...] = flag((col == end) & (token >= 2)).astype(BF)
+        col_ref[2] = flag((col == pltpu.roll(col, 1, 0)) & (token >= 1))
+        col_ref[3] = flag((col == pltpu.roll(col, 2, 0)) & (token >= 2))
         every = jnp.concatenate(rows, axis=1)
         there = jnp.concatenate([col] * (count // LANES), axis=1)
         gap = iota((count, count), 0) - iota((count, count), 1)
@@ -155,7 +157,7 @@
     q_copy.wait()
 
 
-def head_kernel(count, pos_ref, seg_ref, edge_ref, halo_ref, early_ref, sw_ref, rate_ref, sum_ref, u_ref, q_ref,
+def head_kernel(count, pos_ref, seg_ref, edge_ref, halo_ref, early_ref, sw_ref, rate_ref, sum_ref,
                 total_ref, head_ref, use_ref):
     pos = pos_ref[0]
     width = rate_ref.shape[1]
@@ -197,7 +199,7 @@
         total_ref[part] = (sum_ref[:, at] + drop * (u1[:, at] + jnp.exp(-rate) * u0[:, at])).astype(BF)
 
 
-def plan_kernel(count, rounds, pos_ref, seg_ref, ids_ref, rates_ref, res_ref, rate_ref, col_ref, u_ref, q_ref,
+def plan_kernel(count, rounds, pos_ref, seg_ref, ids_ref, rates_ref, res_ref, rate_ref, col_ref,
                 wide_ref, lead_ref, tri_ref, keep_ref, half_ref, full_ref):
     pos = pos_ref[0]
     modes = rates_ref.shape[0]
@@ -214,7 +216,7 @@
     lead = jnp.zeros((count, LANES), F32)
     for c in range(count // SUB):
         lead = jnp.where(start == c, seg_at(first + c * SUB - 1).astype(F32), lead)
-    lead_ref[...] = flag(col == lead)
+    lead_ref[...] = flag(col == lead).astype(BF)
     inner = lax.rem(iota((SUB, SET), 1), SUB)
     tall = iota((SUB, SET), 0)
     for c in range(count // SUB):
@@ -269,7 +271,7 @@
 
 
 def local_kernel(base, u_ref, head_ref, q_ref, halo_ref, sw_ref, skip_ref, rates_ref, res_ref, rate_ref, flat_ref,
-                 wide_ref, lead_ref, col_ref, shift_ref, tri_ref, keep_ref, out_ref, gate_ref, cross_ref):
+                 wide_ref, lead_ref, col_ref, tri_ref, keep_ref, out_ref, gate_ref, cross_ref):
     count, wide = out_ref.shape
     modes = rates_ref.shape[0]
     members = 16
@@ -322,27 +324,24 @@
             inner.append(got[:SUB])
             sums.append(got[SUB:])
             cross_ref[rows, at] = (table * far[c : c + 1] * col_ref[0, rows]).astype(BF)
+        tableb = table.astype(BF)
         state = sums[0]
         local = [inner[0]]
         for c in range(1, spans):
             rows = slice(c * SUB, (c + 1) * SUB)
-            reach = lead_ref[rows]
+            reach = lead_ref[rows].astype(F32)
             right = jnp.concatenate([state.astype(BF)] * groups, axis=0) * holds
-            local.append(inner[c] + jnp.dot((table * reach).astype(BF), right, preferred_element_type=F32))
+            local.append(inner[c] + jnp.dot(tableb * lead_ref[rows], right, preferred_element_type=F32))
             state = fall * reach[SUB - 1 :] * state + sums[c]
-        out_ref[:, at] = jnp.concatenate(local, axis=0) + skip_ref[:, to] * ub.astype(F32)
-    for part in range(wide // SET):
-        at = slice(part * SET, (part + 1) * SET)
-        to = slice(base + part * SET, base + (part + 1) * SET)
-        moved = jnp.dot(shift_ref[...], q_ref[:, to], preferred_element_type=F32)
+        x = q_ref[:, to].astype(F32)
         q = (
-            sw_ref[0, 0:1, to] * q_ref[:, to].astype(F32)
-            + sw_ref[1, 0:1, to] * moved[:count]
-            + sw_ref[2, 0:1, to] * moved[count:]
+            sw_ref[0, 0:1, to] * x
+            + sw_ref[1, 0:1, to] * (col_ref[2] * pltpu.roll(x, 1, 0))
+            + sw_ref[2, 0:1, to] * (col_ref[3] * pltpu.roll(x, 2, 0))
         )
         q = jnp.concatenate([q[:8] + pad(halo_ref[:, to], 8), q[8:]], axis=0)
         gate_ref[:, at] = q
-        out_ref[:, at] = q * out_ref[:, at]
+        out_ref[:, at] = q * (jnp.concatenate(local, axis=0) + skip_ref[:, to] * ub.astype(F32))
 
 
 def last_kernel(pieces, state_ref, *refs):
@@ -399,15 +398,15 @@
     halo = lax.ppermute(feat[:, count - 2 :], "ctx", [(i, i + 1) for i in range(blocks - 1)])
 
     hbm = pl.BlockSpec(memory_space=pltpu.HBM)
-    u, q, sums, rate, flat, edge, cols, shifts, weights = pl.pallas_call(
+    u, q, sums, rate, flat, edge, cols, weights = pl.pallas_call(
         first_kernel,
         in_specs=[sm, hbm, hbm, hbm, hbm],
-        out_specs=[vm] * 9,
+        out_specs=[vm] * 8,
         out_shape=[out(count, width, dtype=BF), out(count, width, dtype=BF), out(modes, width), out(modes, width),
-                   out(1, width), out(4, width), out(2, count, LANES), out(2 * count, count, dtype=BF),
+                   out(1, width), out(4, width), out(4, count, LANES),
                    out(*short_weight.shape)],
         scratch_shapes=[
-            pltpu.VMEM((count, LANES), BF), pltpu.VMEM((2, count, width), BF), pltpu.VMEM(segs.shape, jnp.int32),
+            pltpu.VMEM((count, LANES), BF), pltpu.VMEM((2 * count, count), BF), pltpu.VMEM((2, count, width), BF), pltpu.VMEM(segs.shape, jnp.int32),
             pltpu.VMEM(rates_t.shape, F32), pltpu.SemaphoreType.DMA((2 * (width // WIDE) + 4,)),
         ],
         compiler_params=params(),
@@ -416,28 +415,28 @@
 
     total, head, halo_q = pl.pallas_call(
         lambda *refs: head_kernel(count, *refs),
-        in_specs=[sm] + [vm] * 9,
+        in_specs=[sm] + [vm] * 7,
         out_specs=[vm] * 3,
         out_shape=[out(2, modes, width // 2, dtype=BF), out(2, width), out(2, width)],
         compiler_params=params(),
         name="head",
-    )(pos1, segs, edge, halo, early, weights, rate, sums, u, q)
+    )(pos1, segs, edge, halo, early, weights, rate, sums)
 
     even = (pos & 1) == 0
     other = swap(total, 1)
     steps = 1 + sum(2 * radix - 1 for radix in rounds)
     wflat, lead, tris, keeps, halves, fulls = pl.pallas_call(
         lambda *refs: plan_kernel(count, rounds, *refs),
-        in_specs=[sm, vm, sm] + [vm] * 6,
+        in_specs=[sm, vm, sm] + [vm] * 4,
         out_specs=[vm] * 6,
         out_shape=[
-            out(1, width), out(count, LANES), out(count, SET, dtype=BF), out(count // SUB * 16, SET, dtype=BF),
+            out(1, width), out(count, LANES, dtype=BF), out(count, SET, dtype=BF), out(count // SUB * 16, SET, dtype=BF),
             out(steps, modes, width // 2), out(2, modes, width),
         ],
         compiler_params=params(),
         cost_estimate=pl.CostEstimate(flops=1 << 30, bytes_accessed=5 << 20, transcendentals=0),
         name="plan",
-    )(pos1, segs, segment_ids, rates_t, res_t, rate, cols, u, q)
+    )(pos1, segs, segment_ids, rates_t, res_t, rate, cols)
 
     pieces = width // WIDE
     parts = []
@@ -445,13 +444,13 @@
     def local(piece, head):
         return pl.pallas_call(
             lambda *refs: local_kernel(piece * WIDE, *refs),
-            in_specs=[vm] * 16,
+            in_specs=[vm] * 15,
             out_specs=[vm] * 3,
             out_shape=[out(count, WIDE), out(count, WIDE), out(count, WIDE, dtype=BF)],
             compiler_params=params(),
             cost_estimate=pl.CostEstimate(flops=4 << 30, bytes_accessed=5 << 20, transcendentals=0),
             name="local",
-        )(u, head, q, halo_q, weights, skip, rates_t, res_t, rate, flat, wflat, lead, cols, shifts, tris, keeps)
+        )(u, head, q, halo_q, weights, skip, rates_t, res_t, rate, flat, wflat, lead, cols, tris, keeps)
 
     low_total = jnp.where(even, total, other)
     own_half = lambda value: jnp.where(even, value[0], value[1]).astype(F32)

time: 36 us -> 33.8 us (0.939)
  local copies, waits for them, and re-layouts: 3.37 us -> 2.34 us
  Pallas kernels: 19.1 us -> 18.1 us
    pallas_call x4, Pallas kernels: 10 us -> 8.96 us  [local(): pl.pallas_call(lambda *refs: local_kernel(piece * WIDE, *refs), in_specs=...]
    unnamed x16, local copies, waits for them, and re-layouts: 2.38 us -> 1.35 us
  transfers between devices with their start and end apart: 7 -> 7, of which waited for: 1 -> 2; matrix products, arithmetic and copies ran while one was open for 0% -> 0% of each run, Pallas kernels for 47% -> 47%
where the time goes in v4:
time: 33.8 us; the launch traced here: 33.7 us
  Pallas kernels  18.1 us (54%)
  starting transfers between devices  11.1 us (33%)
  local copies, waits for them, and re-layouts  2.34 us (7%)
  waiting for transfers between devices  1.46 us (4%)
  between operations  0.38 us (1%)
    pallas_call x4, Pallas kernels, local(): pl.pallas_call(lambda *refs: local_kernel(piece * WIDE, *refs), in_specs=...  8.96 us
    ppermute x6, starting transfers between devices, body(): lax.ppermute(value, 'ctx', [(i, i ^ by) for i in range(blocks)])  8.76 us
    pallas_call x1, Pallas kernels, body(): pl.pallas_call(first_kernel, in_specs=[sm, hbm, hbm, hbm, hbm], out_specs...  5.53 us
    ppermute x1, starting transfers between devices, body(): lax.ppermute(feat[:, count - 2:], 'ctx', [(i, i + 1) for i in range(block...  2.36 us
    pallas_call x1, Pallas kernels, body(): pl.pallas_call(lambda *refs: last_kernel(pieces, *refs), in_specs=[vm] *...  1.66 us
    ppermute x6, waiting for transfers between devices, body(): lax.ppermute(value, 'ctx', [(i, i ^ by) for i in range(blocks)])  1.46 us
    pallas_call x1, Pallas kernels, body(): pl.pallas_call(lambda *refs: plan_kernel(count, rounds, *refs), in_specs=...  1.42 us
    unnamed x16, local copies, waits for them, and re-layouts  1.35 us
  transfers between devices with their start and end apart: 7, of which 2 were waited for; matrix products, arithmetic and copies ran while one was open for 0% of the time, Pallas kernels for 47%

profile of v4, /device:TPU:0, one launch (start us, length us, event | category | flops | bytes accessed | tf_op | source)
XLA Modules:
  0.0 33.7 jit_solution(6533750786709909286)
XLA Ops:
  0.0 1.0 %slice.66 = bf16[3,2,4096]{2,1,0:T(2,128)(2,1)S(1)} slice(bf16[3,256,4096]{2,1,0:T(8,128)(2,1)} %bitcast.97), slice={[0:3], [254:256], [0:4096]} | slice | bytes 98304 | tf_op jit(solution)/shard_map/slice | solution.py:398
  1.0 2.4 %collective-permute-start = (bf16[3,2,4096]{2,1,0:T(2,128)(2,1)S(1)}, bf16[3,2,4096]{2,1,0:T(2,128)(2,1)S(1)}, u32[]{:S(2)}, u32[]{:S(2)}) collective-permute-start(bf16[3,2,4096]{2,1,0:T(2,128)(2,1)S(1)} %slice.66), channel_id=1, source_target_pairs={{0,1},{1,2},{2,3},{3,4},{4,5},{5,6},{6,7},{7,8},{8,9},{9,10},{10,1... | collective-permute-start | bytes 147464 | tf_op jit(solution)/shard_map/ppermute | solution.py:398
  3.4 0.0 copy-start
  3.4 0.0 copy-start.5
  3.4 5.5 %first.1 = (bf16[256,4096]{1,0:T(8,128)(2,1)S(1)}, bf16[256,4096]{1,0:T(8,128)(2,1)S(1)}, f32[16,4096]{1,0:T(8,128)S(1)}, f32[16,4096]{1,0:T(8,128)S(1)}, f32[1,...) custom-call(s32[1]{0:T(128)} %bitcast.pos_ref.refs_0_, ...), custom_call_target="tpu_custom_call" | custom-call | tf_op jit(solution)/shard_map/first/pallas_call | solution.py:401
  9.0 1.3 %copy-done.3 = bf16[256,4096]{1,0:T(8,128)(2,1)} copy-done((bf16[256,4096]{1,0:T(8,128)(2,1)}, bf16[256,4096]{1,0:T(8,128)(2,1)S(1)}, u32[]{:S(2)}) %copy-start.3) | copy-done | bytes 2097176
  10.3 0.5 %head.1 = (bf16[2,16,2048]{2,1,0:T(8,128)(2,1)S(1)}, f32[2,4096]{1,0:T(2,128)S(1)}, f32[2,4096]{1,0:T(2,128)S(1)}) custom-call(s32[1]{0:T(128)} %bitcast.pos_ref.refs_0_, s32[32,128]{1,0:T(8,128)S(1)} %bitcast.79, f32[4,4096]{1,0:T(4,128)S(1)} %get-tuple-element.63.refs_2_, bf16[3,2,4096]{2,1,0:T(2,128)(2,1)S(1)} %collective-permute-done.refs_3_, ...), custom_call_target="tpu_custom_call" | custom-call | tf_op jit(solution)/shard_map/head/pallas_call | solution.py:416
  10.8 2.7 %collective-permute-start.1 = (bf16[2,16,2048]{2,1,0:T(8,128)(2,1)S(1)}, bf16[2,16,2048]{2,1,0:T(8,128)(2,1)S(1)}, u32[]{:S(2)}, u32[]{:S(2)}) collective-permute-start(bf16[2,16,2048]{2,1,0:T(8,128)(2,1)S(1)} %get-tuple-element.66), channel_id=1, source_target_pairs={{0,1},{1,0},{2,3},{3,2},{4,5},{5,4},{6,7},{7,6},{8,9},{9,8},{10,11... | collective-permute-start | bytes 393224 | tf_op jit(solution)/shard_map/ppermute | solution.py:395
  13.5 1.4 %plan.1 = (f32[1,4096]{1,0:T(1,128)S(1)}, bf16[256,128]{1,0:T(8,128)(2,1)S(1)}, bf16[256,256]{1,0:T(8,128)(2,1)S(1)}, bf16[128,256]{1,0:T(8,128)(2,1)S(1)}, f32[...) custom-call(s32[1]{0:T(128)} %bitcast.pos_ref.refs_0_, s32[32,128]{1,0:T(8,128)S(1)} %bitcast.80, s32[4096]{0:T(1024)S(1)} %copy-done, ...), custom_call_target="tpu_custom_call" | custom-call | flops 1073741824 | bytes 5242880 | tf_op jit(solution)/shard_map/plan/pallas_call | solution.py:428
  15.0 1.6 %collective-permute-start.2 = (bf16[16,2048]{1,0:T(8,128)(2,1)S(1)}, bf16[16,2048]{1,0:T(8,128)(2,1)S(1)}, u32[]{:S(2)}, u32[]{:S(2)}) collective-permute-start(bf16[16,2048]{1,0:T(8,128)(2,1)S(1)} %convert_element_type.39), channel_id=1, source_target_pairs={{0,2},{1,3},{2,0},{3,1},{4,6},{5,7},{6,4},{7,5},{8,10},{9,11},{10,... | collective-permute-start | bytes 196616 | tf_op jit(solution)/shard_map/ppermute | solution.py:395
  16.6 1.6 %collective-permute-start.3 = (bf16[16,2048]{1,0:T(8,128)(2,1)S(1)}, bf16[16,2048]{1,0:T(8,128)(2,1)S(1)}, u32[]{:S(2)}, u32[]{:S(2)}) collective-permute-start(bf16[16,2048]{1,0:T(8,128)(2,1)S(1)} %convert_element_type.39), channel_id=1, source_target_pairs={{0,4},{1,5},{2,6},{3,7},{4,0},{5,1},{6,2},{7,3},{8,12},{9,13},{10,... | collective-permute-start | bytes 196616 | tf_op jit(solution)/shard_map/ppermute | solution.py:395
  18.2 0.4 %collective-permute-start.4 = (bf16[16,2048]{1,0:T(8,128)(2,1)S(1)}, bf16[16,2048]{1,0:T(8,128)(2,1)S(1)}, u32[]{:S(2)}, u32[]{:S(2)}) collective-permute-start(bf16[16,2048]{1,0:T(8,128)(2,1)S(1)} %convert_element_type.39), channel_id=1, source_target_pairs={{0,6},{1,7},{2,4},{3,5},{4,2},{5,3},{6,0},{7,1},{8,14},{9,15},{10,... | collective-permute-start | bytes 196616 | tf_op jit(solution)/shard_map/ppermute | solution.py:395
  18.6 2.2 %local.4 = (f32[256,1024]{1,0:T(8,128)S(1)}, f32[256,1024]{1,0:T(8,128)S(1)}, bf16[256,1024]{1,0:T(8,128)(2,1)S(1)}) custom-call(bf16[256,4096]{1,0:T(8,128)(2,1)S(1)} %get-tuple-element.69.refs_0_, f32[2,4096]{1,0:T(2,128)S(1)} %get-tuple-element.93.refs_1_, bf16[256,4096]{1,0:T(8,128)(2,1)S(1)} %copy-done.4, f32[2,4096]{1,0:T(2,128)S(1)} %get-tuple-element.72.refs_3_, ...), custom_call_target="tpu_custom_call" | custom-call | flops 4294967296 | bytes 5242880 | tf_op jit(solution)/shard_map/local/pallas_call | solution.py:445
  20.8 2.3 %local.5 = (f32[256,1024]{1,0:T(8,128)S(1)}, f32[256,1024]{1,0:T(8,128)S(1)}, bf16[256,1024]{1,0:T(8,128)(2,1)S(1)}) custom-call(bf16[256,4096]{1,0:T(8,128)(2,1)S(1)} %get-tuple-element.69.refs_0_, f32[2,4096]{1,0:T(2,128)S(1)} %get-tuple-element.93.refs_1_, bf16[256,4096]{1,0:T(8,128)(2,1)S(1)} %copy-done.4, f32[2,4096]{1,0:T(2,128)S(1)} %get-tuple-element.72.refs_3_, ...), custom_call_target="tpu_custom_call" | custom-call | flops 4294967296 | bytes 5242880 | tf_op jit(solution)/shard_map/local/pallas_call | solution.py:445
  23.1 0.2 collective-permute-done.4
  23.4 0.1 fusion.3
  23.4 2.4 %collective-permute-start.5 = (bf16[16,2048]{1,0:T(8,128)(2,1)S(1)}, bf16[16,2048]{1,0:T(8,128)(2,1)S(1)}, u32[]{:S(2)}, u32[]{:S(2)}) collective-permute-start(bf16[16,2048]{1,0:T(8,128)(2,1)S(1)} %fusion.3), channel_id=1, source_target_pairs={{0,8},{1,9},{2,10},{3,11},{4,12},{5,13},{6,14},{7,15},{8,0},{9,1},... | collective-permute-start | bytes 196616 | tf_op jit(solution)/shard_map/ppermute | solution.py:395
  25.9 2.2 %local.6 = (f32[256,1024]{1,0:T(8,128)S(1)}, f32[256,1024]{1,0:T(8,128)S(1)}, bf16[256,1024]{1,0:T(8,128)(2,1)S(1)}) custom-call(bf16[256,4096]{1,0:T(8,128)(2,1)S(1)} %get-tuple-element.69.refs_0_, f32[2,4096]{1,0:T(2,128)S(1)} %get-tuple-element.93.refs_1_, bf16[256,4096]{1,0:T(8,128)(2,1)S(1)} %copy-done.4, f32[2,4096]{1,0:T(2,128)S(1)} %get-tuple-element.72.refs_3_, ...), custom_call_target="tpu_custom_call" | custom-call | flops 4294967296 | bytes 5242880 | tf_op jit(solution)/shard_map/local/pallas_call | solution.py:445
  28.1 2.3 %local.7 = (f32[256,1024]{1,0:T(8,128)S(1)}, f32[256,1024]{1,0:T(8,128)S(1)}, bf16[256,1024]{1,0:T(8,128)(2,1)S(1)}) custom-call(bf16[256,4096]{1,0:T(8,128)(2,1)S(1)} %get-tuple-element.69.refs_0_, f32[2,4096]{1,0:T(2,128)S(1)} %get-tuple-element.93.refs_1_, bf16[256,4096]{1,0:T(8,128)(2,1)S(1)} %copy-done.4, f32[2,4096]{1,0:T(2,128)S(1)} %get-tuple-element.72.refs_3_, ...), custom_call_target="tpu_custom_call" | custom-call | flops 4294967296 | bytes 5242880 | tf_op jit(solution)/shard_map/local/pallas_call | solution.py:445
  30.4 0.1 fusion.7
  30.4 0.1 collective-permute-start.6
  30.5 1.2 %collective-permute-done.6 = bf16[16,2048]{1,0:T(8,128)(2,1)S(1)} collective-permute-done((bf16[16,2048]{1,0:T(8,128)(2,1)S(1)}, bf16[16,2048]{1,0:T(8,128)(2,1)S(1)}, u32[]{:S(2)}, u32[]{:S(2)}) %collective-permute-start.6) | collective-permute-done | bytes 65568 | tf_op jit(solution)/shard_map/ppermute | solution.py:395
  31.8 0.1 fusion.refs_0_
  31.9 1.7 %last.1 = bf16[256,4096]{1,0:T(8,128)(2,1)} custom-call(f32[16,4096]{1,0:T(8,128)S(1)} %fusion.refs_0_, f32[256,1024]{1,0:T(8,128)S(1)} %get-tuple-element.101.refs_1_, f32[256,1024]{1,0:T(8,128)S(1)} %get-tuple-element.102.refs_2_, bf16[256,1024]{1,0:T(8,128)(2,1)S(1)} %get-tuple-element.103.refs_3_, f32[256,1024]{1,0:T(8,128)S(1)} %get-tuple-element.104.refs_4_, ...), custom_call_target="tpu_custom_call" | custom-call | tf_op jit(solution)/shard_map/last/pallas_call | solution.py:482
  (27 shorter events, 0.2 us)
Async XLA Ops:
  1.0 9.3 %collective-permute-start = (bf16[3,2,4096]{2,1,0:T(2,128)(2,1)S(1)}, bf16[3,2,4096]{2,1,0:T(2,128)(2,1)S(1)}, u32[]{:S(2)}, u32[]{:S(2)}) collective-permute-start(bf16[3,2,4096]{2,1,0:T(2,128)(2,1)S(1)} %slice.66), channel_id=1, source_target_pairs={{0,1},{1,2},{2,3},{3,4},{4,5},{5,6},{6,7},{7,8},{8,9},{9,10},{10,1... | collective-permute-start | bytes 147464 | tf_op jit(solution)/shard_map/ppermute | solution.py:398
  3.4 6.9 %copy-start = (s32[4096]{0:T(1024)S(1)}, s32[4096]{0:T(1024)}, u32[]{:S(2)}) copy-start(s32[4096]{0:T(1024)} %refs_2_.1) | copy-start | bytes 49156
  3.4 6.9 %copy-start.1 = (bf16[2,3,4096]{2,0,1:T(2,128)(2,1)S(1)}, bf16[2,3,4096]{2,0,1:T(2,128)(2,1)}, u32[]{:S(2)}) copy-start(bf16[2,3,4096]{2,0,1:T(2,128)(2,1)} %param.14) | copy-start | bytes 147460
  3.4 10.1 %copy-start.2 = (f32[256,16]{0,1:T(8,128)S(1)}, f32[256,16]{0,1:T(8,128)}, u32[]{:S(2)}) copy-start(f32[256,16]{0,1:T(8,128)} %param.11) | copy-start | bytes 49156
  3.4 10.1 %copy-start.5 = (f32[256,16]{0,1:T(8,128)S(1)}, f32[256,16]{0,1:T(8,128)}, u32[]{:S(2)}) copy-start(f32[256,16]{0,1:T(8,128)} %param.10) | copy-start | bytes 49156
  8.9 1.3 %copy-start.3 = (bf16[256,4096]{1,0:T(8,128)(2,1)}, bf16[256,4096]{1,0:T(8,128)(2,1)S(1)}, u32[]{:S(2)}) copy-start(bf16[256,4096]{1,0:T(8,128)(2,1)S(1)} %get-tuple-element.71.refs_2_) | copy-start | bytes 6291460
  10.8 4.1 %collective-permute-start.1 = (bf16[2,16,2048]{2,1,0:T(8,128)(2,1)S(1)}, bf16[2,16,2048]{2,1,0:T(8,128)(2,1)S(1)}, u32[]{:S(2)}, u32[]{:S(2)}) collective-permute-start(bf16[2,16,2048]{2,1,0:T(8,128)(2,1)S(1)} %get-tuple-element.66), channel_id=1, source_target_pairs={{0,1},{1,0},{2,3},{3,2},{4,5},{5,4},{6,7},{7,6},{8,9},{9,8},{10,11... | collective-permute-start | bytes 393224 | tf_op jit(solution)/shard_map/ppermute | solution.py:395
  13.5 5.1 %copy-start.4 = (bf16[256,4096]{1,0:T(8,128)(2,1)S(1)}, bf16[256,4096]{1,0:T(8,128)(2,1)}, u32[]{:S(2)}) copy-start(bf16[256,4096]{1,0:T(8,128)(2,1)} %copy-done.3) | copy-start | bytes 6291460
  13.5 5.1 %copy-start.6 = (f32[4096]{0:T(1024)S(1)}, f32[4096]{0:T(1024)}, u32[]{:S(2)}) copy-start(f32[4096]{0:T(1024)} %param.12) | copy-start | bytes 49156
  15.0 8.0 %collective-permute-start.2 = (bf16[16,2048]{1,0:T(8,128)(2,1)S(1)}, bf16[16,2048]{1,0:T(8,128)(2,1)S(1)}, u32[]{:S(2)}, u32[]{:S(2)}) collective-permute-start(bf16[16,2048]{1,0:T(8,128)(2,1)S(1)} %convert_element_type.39), channel_id=1, source_target_pairs={{0,2},{1,3},{2,0},{3,1},{4,6},{5,7},{6,4},{7,5},{8,10},{9,11},{10,... | collective-permute-start | bytes 196616 | tf_op jit(solution)/shard_map/ppermute | solution.py:395
  16.6 6.5 %collective-permute-start.3 = (bf16[16,2048]{1,0:T(8,128)(2,1)S(1)}, bf16[16,2048]{1,0:T(8,128)(2,1)S(1)}, u32[]{:S(2)}, u32[]{:S(2)}) collective-permute-start(bf16[16,2048]{1,0:T(8,128)(2,1)S(1)} %convert_element_type.39), channel_id=1, source_target_pairs={{0,4},{1,5},{2,6},{3,7},{4,0},{5,1},{6,2},{7,3},{8,12},{9,13},{10,... | collective-permute-start | bytes 196616 | tf_op jit(solution)/shard_map/ppermute | solution.py:395
  18.2 5.2 %collective-permute-start.4 = (bf16[16,2048]{1,0:T(8,128)(2,1)S(1)}, bf16[16,2048]{1,0:T(8,128)(2,1)S(1)}, u32[]{:S(2)}, u32[]{:S(2)}) collective-permute-start(bf16[16,2048]{1,0:T(8,128)(2,1)S(1)} %convert_element_type.39), channel_id=1, source_target_pairs={{0,6},{1,7},{2,4},{3,5},{4,2},{5,3},{6,0},{7,1},{8,14},{9,15},{10,... | collective-permute-start | bytes 196616 | tf_op jit(solution)/shard_map/ppermute | solution.py:395
  23.4 6.9 %collective-permute-start.5 = (bf16[16,2048]{1,0:T(8,128)(2,1)S(1)}, bf16[16,2048]{1,0:T(8,128)(2,1)S(1)}, u32[]{:S(2)}, u32[]{:S(2)}) collective-permute-start(bf16[16,2048]{1,0:T(8,128)(2,1)S(1)} %fusion.3), channel_id=1, source_target_pairs={{0,8},{1,9},{2,10},{3,11},{4,12},{5,13},{6,14},{7,15},{8,0},{9,1},... | collective-permute-start | bytes 196616 | tf_op jit(solution)/shard_map/ppermute | solution.py:395
  28.1 3.7 %copy-start.7 = (f32[16,4096]{1,0:T(8,128)S(1)}, f32[16,4096]{1,0:T(8,128)}, u32[]{:S(2)}) copy-start(f32[16,4096]{1,0:T(8,128)} %param.13) | copy-start | bytes 786436
  30.4 1.3 %collective-permute-start.6 = (bf16[16,2048]{1,0:T(8,128)(2,1)S(1)}, bf16[16,2048]{1,0:T(8,128)(2,1)S(1)}, u32[]{:S(2)}, u32[]{:S(2)}) collective-permute-start(bf16[16,2048]{1,0:T(8,128)(2,1)S(1)} %fusion.7), channel_id=1, source_target_pairs={{0,1},{1,0},{2,3},{3,2},{4,5},{5,4},{6,7},{7,6},{8,9},{9,8},{10,11... | collective-permute-start | bytes 196616 | tf_op jit(solution)/shard_map/ppermute | solution.py:395

commit v5 on v4

--- a/solution.py
+++ b/solution.py
@@ -157,8 +157,8 @@
     q_copy.wait()
 
 
-def head_kernel(count, pos_ref, seg_ref, edge_ref, halo_ref, early_ref, sw_ref, rate_ref, sum_ref,
-                total_ref, head_ref, use_ref):
+def head_kernel(count, pos_ref, seg_ref, edge_ref, halo_ref, early_ref, sw_ref, rate_ref, sum_ref, q_ref,
+                total_ref, head_ref, use_ref, same_ref):
     pos = pos_ref[0]
     width = rate_ref.shape[1]
     per = count // LANES
@@ -413,14 +413,15 @@
         name="first",
     )(pos1, stay(segs), stay(rates_t), stay(feat), stay(short_weight))
 
-    total, head, halo_q = pl.pallas_call(
+    total, head, halo_q, q = pl.pallas_call(
         lambda *refs: head_kernel(count, *refs),
-        in_specs=[sm] + [vm] * 7,
-        out_specs=[vm] * 3,
-        out_shape=[out(2, modes, width // 2, dtype=BF), out(2, width), out(2, width)],
+        in_specs=[sm] + [vm] * 8,
+        out_specs=[vm] * 4,
+        out_shape=[out(2, modes, width // 2, dtype=BF), out(2, width), out(2, width), out(count, width, dtype=BF)],
+        input_output_aliases={8: 3},
         compiler_params=params(),
         name="head",
-    )(pos1, segs, edge, halo, early, weights, rate, sums)
+    )(pos1, segs, edge, halo, early, weights, rate, sums, q)
 
     even = (pos & 1) == 0
     other = swap(total, 1)

time: 33.8 us -> 33.3 us (0.985)
  local copies, waits for them, and re-layouts: 2.34 us -> 1.78 us
    unnamed x16, local copies, waits for them, and re-layouts: 1.35 us -> 0.79 us
  transfers between devices with their start and end apart: 7 -> 7, of which waited for: 2 -> 2; matrix products, arithmetic and copies ran while one was open for 0% -> 0% of each run, Pallas kernels for 47% -> 48%
where the time goes in v5:
time: 33.3 us; the launch traced here: 33.2 us
  Pallas kernels  18.1 us (54%)
  starting transfers between devices  11.1 us (33%)
  local copies, waits for them, and re-layouts  1.78 us (5%)
  waiting for transfers between devices  1.46 us (4%)
  between operations  0.41 us (1%)
    pallas_call x4, Pallas kernels, local(): pl.pallas_call(lambda *refs: local_kernel(piece * WIDE, *refs), in_specs=...  8.96 us
    ppermute x6, starting transfers between devices, body(): lax.ppermute(value, 'ctx', [(i, i ^ by) for i in range(blocks)])  8.71 us
    pallas_call x1, Pallas kernels, body(): pl.pallas_call(first_kernel, in_specs=[sm, hbm, hbm, hbm, hbm], out_specs...  5.58 us
    ppermute x1, starting transfers between devices, body(): lax.ppermute(feat[:, count - 2:], 'ctx', [(i, i + 1) for i in range(block...  2.36 us
    pallas_call x1, Pallas kernels, body(): pl.pallas_call(lambda *refs: last_kernel(pieces, *refs), in_specs=[vm] *...  1.66 us
    ppermute x6, waiting for transfers between devices, body(): lax.ppermute(value, 'ctx', [(i, i ^ by) for i in range(blocks)])  1.46 us
    pallas_call x1, Pallas kernels, body(): pl.pallas_call(lambda *refs: plan_kernel(count, rounds, *refs), in_specs=...  1.42 us
    slice x1, local copies, waits for them, and re-layouts, body(): feat[:, count - 2:]  0.98 us
  transfers between devices with their start and end apart: 7, of which 2 were waited for; matrix products, arithmetic and copies ran while one was open for 0% of the time, Pallas kernels for 48%

profile of v5, /device:TPU:0, one launch (start us, length us, event | category | flops | bytes accessed | tf_op | source)
XLA Modules:
  0.0 33.2 jit_solution(16955157926461738796)
XLA Ops:
  0.0 1.0 %slice.66 = bf16[3,2,4096]{2,1,0:T(2,128)(2,1)S(1)} slice(bf16[3,256,4096]{2,1,0:T(8,128)(2,1)} %bitcast.97), slice={[0:3], [254:256], [0:4096]} | slice | bytes 98304 | tf_op jit(solution)/shard_map/slice | solution.py:398
  1.0 2.4 %collective-permute-start = (bf16[3,2,4096]{2,1,0:T(2,128)(2,1)S(1)}, bf16[3,2,4096]{2,1,0:T(2,128)(2,1)S(1)}, u32[]{:S(2)}, u32[]{:S(2)}) collective-permute-start(bf16[3,2,4096]{2,1,0:T(2,128)(2,1)S(1)} %slice.66), channel_id=1, source_target_pairs={{0,1},{1,2},{2,3},{3,4},{4,5},{5,6},{6,7},{7,8},{8,9},{9,10},{10,1... | collective-permute-start | bytes 147464 | tf_op jit(solution)/shard_map/ppermute | solution.py:398
  3.4 0.0 copy-start
  3.4 5.6 %first.1 = (bf16[256,4096]{1,0:T(8,128)(2,1)S(1)}, bf16[256,4096]{1,0:T(8,128)(2,1)S(1)}, f32[16,4096]{1,0:T(8,128)S(1)}, f32[16,4096]{1,0:T(8,128)S(1)}, f32[1,...) custom-call(s32[1]{0:T(128)} %bitcast.pos_ref.refs_0_, ...), custom_call_target="tpu_custom_call" | custom-call | tf_op jit(solution)/shard_map/first/pallas_call | solution.py:401
  9.0 0.0 copy-start.3
  9.0 0.5 %head.1 = (bf16[2,16,2048]{2,1,0:T(8,128)(2,1)S(1)}, f32[2,4096]{1,0:T(2,128)S(1)}, f32[2,4096]{1,0:T(2,128)S(1)}, bf16[256,4096]{1,0:T(8,128)(2,1)S(1)}) custom-call(s32[1]{0:T(128)} %bitcast.pos_ref.refs_0_, s32[32,128]{1,0:T(8,128)S(1)} %bitcast.79, f32[4,4096]{1,0:T(4,128)S(1)} %get-tuple-element.64.refs_2_, ...), custom_call_target="tpu_custom_call", output_to_operand_aliasing={{3}: (8, {})} | custom-call | tf_op jit(solution)/shard_map/head/pallas_call | solution.py:416
  9.5 0.8 %copy-done.3 = bf16[256,4096]{1,0:T(8,128)(2,1)} copy-done((bf16[256,4096]{1,0:T(8,128)(2,1)}, bf16[256,4096]{1,0:T(8,128)(2,1)S(1)}, u32[]{:S(2)}) %copy-start.3) | copy-done | bytes 2097176
  10.3 2.6 %collective-permute-start.1 = (bf16[2,16,2048]{2,1,0:T(8,128)(2,1)S(1)}, bf16[2,16,2048]{2,1,0:T(8,128)(2,1)S(1)}, u32[]{:S(2)}, u32[]{:S(2)}) collective-permute-start(bf16[2,16,2048]{2,1,0:T(8,128)(2,1)S(1)} %get-tuple-element.68), channel_id=1, source_target_pairs={{0,1},{1,0},{2,3},{3,2},{4,5},{5,4},{6,7},{7,6},{8,9},{9,8},{10,11... | collective-permute-start | bytes 393224 | tf_op jit(solution)/shard_map/ppermute | solution.py:395
  12.9 1.4 %plan.1 = (f32[1,4096]{1,0:T(1,128)S(1)}, bf16[256,128]{1,0:T(8,128)(2,1)S(1)}, bf16[256,256]{1,0:T(8,128)(2,1)S(1)}, bf16[128,256]{1,0:T(8,128)(2,1)S(1)}, f32[...) custom-call(s32[1]{0:T(128)} %bitcast.pos_ref.refs_0_, s32[32,128]{1,0:T(8,128)S(1)} %bitcast.80, s32[4096]{0:T(1024)S(1)} %copy-done, ...), custom_call_target="tpu_custom_call" | custom-call | flops 1073741824 | bytes 5242880 | tf_op jit(solution)/shard_map/plan/pallas_call | solution.py:429
  14.5 1.6 %collective-permute-start.2 = (bf16[16,2048]{1,0:T(8,128)(2,1)S(1)}, bf16[16,2048]{1,0:T(8,128)(2,1)S(1)}, u32[]{:S(2)}, u32[]{:S(2)}) collective-permute-start(bf16[16,2048]{1,0:T(8,128)(2,1)S(1)} %convert_element_type.39), channel_id=1, source_target_pairs={{0,2},{1,3},{2,0},{3,1},{4,6},{5,7},{6,4},{7,5},{8,10},{9,11},{10,... | collective-permute-start | bytes 196616 | tf_op jit(solution)/shard_map/ppermute | solution.py:395
  16.1 1.6 %collective-permute-start.3 = (bf16[16,2048]{1,0:T(8,128)(2,1)S(1)}, bf16[16,2048]{1,0:T(8,128)(2,1)S(1)}, u32[]{:S(2)}, u32[]{:S(2)}) collective-permute-start(bf16[16,2048]{1,0:T(8,128)(2,1)S(1)} %convert_element_type.39), channel_id=1, source_target_pairs={{0,4},{1,5},{2,6},{3,7},{4,0},{5,1},{6,2},{7,3},{8,12},{9,13},{10,... | collective-permute-start | bytes 196616 | tf_op jit(solution)/shard_map/ppermute | solution.py:395
  17.6 0.4 %collective-permute-start.4 = (bf16[16,2048]{1,0:T(8,128)(2,1)S(1)}, bf16[16,2048]{1,0:T(8,128)(2,1)S(1)}, u32[]{:S(2)}, u32[]{:S(2)}) collective-permute-start(bf16[16,2048]{1,0:T(8,128)(2,1)S(1)} %convert_element_type.39), channel_id=1, source_target_pairs={{0,6},{1,7},{2,4},{3,5},{4,2},{5,3},{6,0},{7,1},{8,14},{9,15},{10,... | collective-permute-start | bytes 196616 | tf_op jit(solution)/shard_map/ppermute | solution.py:395
  18.0 2.2 %local.4 = (f32[256,1024]{1,0:T(8,128)S(1)}, f32[256,1024]{1,0:T(8,128)S(1)}, bf16[256,1024]{1,0:T(8,128)(2,1)S(1)}) custom-call(bf16[256,4096]{1,0:T(8,128)(2,1)S(1)} %copy-done.4, f32[2,4096]{1,0:T(2,128)S(1)} %get-tuple-element.95.refs_1_, bf16[256,4096]{1,0:T(8,128)(2,1)S(1)} %get-tuple-element.73.refs_2_, f32[2,4096]{1,0:T(2,128)S(1)} %get-tuple-element.74.refs_3_, ...), custom_call_target="tpu_custom_call" | custom-call | flops 4294967296 | bytes 5242880 | tf_op jit(solution)/shard_map/local/pallas_call | solution.py:446
  20.3 2.3 %local.5 = (f32[256,1024]{1,0:T(8,128)S(1)}, f32[256,1024]{1,0:T(8,128)S(1)}, bf16[256,1024]{1,0:T(8,128)(2,1)S(1)}) custom-call(bf16[256,4096]{1,0:T(8,128)(2,1)S(1)} %copy-done.4, f32[2,4096]{1,0:T(2,128)S(1)} %get-tuple-element.95.refs_1_, bf16[256,4096]{1,0:T(8,128)(2,1)S(1)} %get-tuple-element.73.refs_2_, f32[2,4096]{1,0:T(2,128)S(1)} %get-tuple-element.74.refs_3_, ...), custom_call_target="tpu_custom_call" | custom-call | flops 4294967296 | bytes 5242880 | tf_op jit(solution)/shard_map/local/pallas_call | solution.py:446
  22.6 0.2 collective-permute-done.4
  22.8 0.1 fusion.3
  22.9 2.5 %collective-permute-start.5 = (bf16[16,2048]{1,0:T(8,128)(2,1)S(1)}, bf16[16,2048]{1,0:T(8,128)(2,1)S(1)}, u32[]{:S(2)}, u32[]{:S(2)}) collective-permute-start(bf16[16,2048]{1,0:T(8,128)(2,1)S(1)} %fusion.3), channel_id=1, source_target_pairs={{0,8},{1,9},{2,10},{3,11},{4,12},{5,13},{6,14},{7,15},{8,0},{9,1},... | collective-permute-start | bytes 196616 | tf_op jit(solution)/shard_map/ppermute | solution.py:395
  25.3 2.2 %local.6 = (f32[256,1024]{1,0:T(8,128)S(1)}, f32[256,1024]{1,0:T(8,128)S(1)}, bf16[256,1024]{1,0:T(8,128)(2,1)S(1)}) custom-call(bf16[256,4096]{1,0:T(8,128)(2,1)S(1)} %copy-done.4, f32[2,4096]{1,0:T(2,128)S(1)} %get-tuple-element.95.refs_1_, bf16[256,4096]{1,0:T(8,128)(2,1)S(1)} %get-tuple-element.73.refs_2_, f32[2,4096]{1,0:T(2,128)S(1)} %get-tuple-element.74.refs_3_, ...), custom_call_target="tpu_custom_call" | custom-call | flops 4294967296 | bytes 5242880 | tf_op jit(solution)/shard_map/local/pallas_call | solution.py:446
  27.6 2.3 %local.7 = (f32[256,1024]{1,0:T(8,128)S(1)}, f32[256,1024]{1,0:T(8,128)S(1)}, bf16[256,1024]{1,0:T(8,128)(2,1)S(1)}) custom-call(bf16[256,4096]{1,0:T(8,128)(2,1)S(1)} %copy-done.4, f32[2,4096]{1,0:T(2,128)S(1)} %get-tuple-element.95.refs_1_, bf16[256,4096]{1,0:T(8,128)(2,1)S(1)} %get-tuple-element.73.refs_2_, f32[2,4096]{1,0:T(2,128)S(1)} %get-tuple-element.74.refs_3_, ...), custom_call_target="tpu_custom_call" | custom-call | flops 4294967296 | bytes 5242880 | tf_op jit(solution)/shard_map/local/pallas_call | solution.py:446
  29.9 0.1 fusion.7
  29.9 0.1 collective-permute-start.6
  30.0 1.2 %collective-permute-done.6 = bf16[16,2048]{1,0:T(8,128)(2,1)S(1)} collective-permute-done((bf16[16,2048]{1,0:T(8,128)(2,1)S(1)}, bf16[16,2048]{1,0:T(8,128)(2,1)S(1)}, u32[]{:S(2)}, u32[]{:S(2)}) %collective-permute-start.6) | collective-permute-done | bytes 65568 | tf_op jit(solution)/shard_map/ppermute | solution.py:395
  31.3 0.1 fusion.refs_0_
  31.3 1.7 %last.1 = bf16[256,4096]{1,0:T(8,128)(2,1)} custom-call(f32[16,4096]{1,0:T(8,128)S(1)} %fusion.refs_0_, f32[256,1024]{1,0:T(8,128)S(1)} %get-tuple-element.103.refs_1_, f32[256,1024]{1,0:T(8,128)S(1)} %get-tuple-element.104.refs_2_, bf16[256,1024]{1,0:T(8,128)(2,1)S(1)} %get-tuple-element.105.refs_3_, f32[256,1024]{1,0:T(8,128)S(1)} %get-tuple-element.106.refs_4_, ...), custom_call_target="tpu_custom_call" | custom-call | tf_op jit(solution)/shard_map/last/pallas_call | solution.py:483
  (27 shorter events, 0.2 us)
Async XLA Ops:
  1.0 8.0 %collective-permute-start = (bf16[3,2,4096]{2,1,0:T(2,128)(2,1)S(1)}, bf16[3,2,4096]{2,1,0:T(2,128)(2,1)S(1)}, u32[]{:S(2)}, u32[]{:S(2)}) collective-permute-start(bf16[3,2,4096]{2,1,0:T(2,128)(2,1)S(1)} %slice.66), channel_id=1, source_target_pairs={{0,1},{1,2},{2,3},{3,4},{4,5},{5,6},{6,7},{7,8},{8,9},{9,10},{10,1... | collective-permute-start | bytes 147464 | tf_op jit(solution)/shard_map/ppermute | solution.py:398
  3.4 5.7 %copy-start = (s32[4096]{0:T(1024)S(1)}, s32[4096]{0:T(1024)}, u32[]{:S(2)}) copy-start(s32[4096]{0:T(1024)} %refs_2_.1) | copy-start | bytes 49156
  3.4 5.7 %copy-start.1 = (bf16[2,3,4096]{2,0,1:T(2,128)(2,1)S(1)}, bf16[2,3,4096]{2,0,1:T(2,128)(2,1)}, u32[]{:S(2)}) copy-start(bf16[2,3,4096]{2,0,1:T(2,128)(2,1)} %param.14) | copy-start | bytes 147460
  9.0 1.3 %copy-start.3 = (bf16[256,4096]{1,0:T(8,128)(2,1)}, bf16[256,4096]{1,0:T(8,128)(2,1)S(1)}, u32[]{:S(2)}) copy-start(bf16[256,4096]{1,0:T(8,128)(2,1)S(1)} %get-tuple-element.71.refs_0_) | copy-start | bytes 6291460
  9.0 3.9 %copy-start.2 = (f32[256,16]{0,1:T(8,128)S(1)}, f32[256,16]{0,1:T(8,128)}, u32[]{:S(2)}) copy-start(f32[256,16]{0,1:T(8,128)} %param.11) | copy-start | bytes 49156
  9.0 3.9 %copy-start.5 = (f32[256,16]{0,1:T(8,128)S(1)}, f32[256,16]{0,1:T(8,128)}, u32[]{:S(2)}) copy-start(f32[256,16]{0,1:T(8,128)} %param.10) | copy-start | bytes 49156
  10.3 4.1 %collective-permute-start.1 = (bf16[2,16,2048]{2,1,0:T(8,128)(2,1)S(1)}, bf16[2,16,2048]{2,1,0:T(8,128)(2,1)S(1)}, u32[]{:S(2)}, u32[]{:S(2)}) collective-permute-start(bf16[2,16,2048]{2,1,0:T(8,128)(2,1)S(1)} %get-tuple-element.68), channel_id=1, source_target_pairs={{0,1},{1,0},{2,3},{3,2},{4,5},{5,4},{6,7},{7,6},{8,9},{9,8},{10,11... | collective-permute-start | bytes 393224 | tf_op jit(solution)/shard_map/ppermute | solution.py:395
  12.9 5.1 %copy-start.4 = (bf16[256,4096]{1,0:T(8,128)(2,1)S(1)}, bf16[256,4096]{1,0:T(8,128)(2,1)}, u32[]{:S(2)}) copy-start(bf16[256,4096]{1,0:T(8,128)(2,1)} %copy-done.3) | copy-start | bytes 6291460
  12.9 5.1 %copy-start.6 = (f32[4096]{0:T(1024)S(1)}, f32[4096]{0:T(1024)}, u32[]{:S(2)}) copy-start(f32[4096]{0:T(1024)} %param.12) | copy-start | bytes 49156
  14.5 8.0 %collective-permute-start.2 = (bf16[16,2048]{1,0:T(8,128)(2,1)S(1)}, bf16[16,2048]{1,0:T(8,128)(2,1)S(1)}, u32[]{:S(2)}, u32[]{:S(2)}) collective-permute-start(bf16[16,2048]{1,0:T(8,128)(2,1)S(1)} %convert_element_type.39), channel_id=1, source_target_pairs={{0,2},{1,3},{2,0},{3,1},{4,6},{5,7},{6,4},{7,5},{8,10},{9,11},{10,... | collective-permute-start | bytes 196616 | tf_op jit(solution)/shard_map/ppermute | solution.py:395
  16.1 6.5 %collective-permute-start.3 = (bf16[16,2048]{1,0:T(8,128)(2,1)S(1)}, bf16[16,2048]{1,0:T(8,128)(2,1)S(1)}, u32[]{:S(2)}, u32[]{:S(2)}) collective-permute-start(bf16[16,2048]{1,0:T(8,128)(2,1)S(1)} %convert_element_type.39), channel_id=1, source_target_pairs={{0,4},{1,5},{2,6},{3,7},{4,0},{5,1},{6,2},{7,3},{8,12},{9,13},{10,... | collective-permute-start | bytes 196616 | tf_op jit(solution)/shard_map/ppermute | solution.py:395
  17.6 5.2 %collective-permute-start.4 = (bf16[16,2048]{1,0:T(8,128)(2,1)S(1)}, bf16[16,2048]{1,0:T(8,128)(2,1)S(1)}, u32[]{:S(2)}, u32[]{:S(2)}) collective-permute-start(bf16[16,2048]{1,0:T(8,128)(2,1)S(1)} %convert_element_type.39), channel_id=1, source_target_pairs={{0,6},{1,7},{2,4},{3,5},{4,2},{5,3},{6,0},{7,1},{8,14},{9,15},{10,... | collective-permute-start | bytes 196616 | tf_op jit(solution)/shard_map/ppermute | solution.py:395
  22.9 7.0 %collective-permute-start.5 = (bf16[16,2048]{1,0:T(8,128)(2,1)S(1)}, bf16[16,2048]{1,0:T(8,128)(2,1)S(1)}, u32[]{:S(2)}, u32[]{:S(2)}) collective-permute-start(bf16[16,2048]{1,0:T(8,128)(2,1)S(1)} %fusion.3), channel_id=1, source_target_pairs={{0,8},{1,9},{2,10},{3,11},{4,12},{5,13},{6,14},{7,15},{8,0},{9,1},... | collective-permute-start | bytes 196616 | tf_op jit(solution)/shard_map/ppermute | solution.py:395
  27.6 3.7 %copy-start.7 = (f32[16,4096]{1,0:T(8,128)S(1)}, f32[16,4096]{1,0:T(8,128)}, u32[]{:S(2)}) copy-start(f32[16,4096]{1,0:T(8,128)} %param.13) | copy-start | bytes 786436
  29.9 1.3 %collective-permute-start.6 = (bf16[16,2048]{1,0:T(8,128)(2,1)S(1)}, bf16[16,2048]{1,0:T(8,128)(2,1)S(1)}, u32[]{:S(2)}, u32[]{:S(2)}) collective-permute-start(bf16[16,2048]{1,0:T(8,128)(2,1)S(1)} %fusion.7), channel_id=1, source_target_pairs={{0,1},{1,0},{2,3},{3,2},{4,5},{5,4},{6,7},{7,6},{8,9},{9,8},{10,11... | collective-permute-start | bytes 196616 | tf_op jit(solution)/shard_map/ppermute | solution.py:395

commit v6 on v5

--- a/solution.py
+++ b/solution.py
@@ -10,6 +10,7 @@
 LANES = 128
 SET = 256
 WIDE = 1024
+PIECE = 2048
 SUB = 32
 
 
@@ -439,15 +440,15 @@
         name="plan",
     )(pos1, segs, segment_ids, rates_t, res_t, rate, cols)
 
-    pieces = width // WIDE
+    pieces = width // PIECE
     parts = []
 
     def local(piece, head):
         return pl.pallas_call(
-            lambda *refs: local_kernel(piece * WIDE, *refs),
+            lambda *refs: local_kernel(piece * PIECE, *refs),
             in_specs=[vm] * 15,
             out_specs=[vm] * 3,
-            out_shape=[out(count, WIDE), out(count, WIDE), out(count, WIDE, dtype=BF)],
+            out_shape=[out(count, PIECE), out(count, PIECE), out(count, PIECE, dtype=BF)],
             compiler_params=params(),
             cost_estimate=pl.CostEstimate(flops=4 << 30, bytes_accessed=5 << 20, transcendentals=0),
             name="local",

time: 33.3 us -> 33 us (level)
    pallas_call x4 -> x2, Pallas kernels: 8.96 us -> 8.56 us  [local(): pl.pallas_call(lambda *refs: local_kernel(piece * PIECE, *refs), in_specs...]
  transfers between devices with their start and end apart: 7 -> 7, of which waited for: 2 -> 2; matrix products, arithmetic and copies ran while one was open for 0% -> 0% of each run, Pallas kernels for 48% -> 47%
where the time goes in v6:
time: 33 us; the launch traced here: 32.9 us
  Pallas kernels  17.8 us (54%)
  starting transfers between devices  10.9 us (33%)
  local copies, waits for them, and re-layouts  1.78 us (5%)
  waiting for transfers between devices  1.66 us (5%)
  between operations  0.41 us (1%)
    pallas_call x2, Pallas kernels, local(): pl.pallas_call(lambda *refs: local_kernel(piece * PIECE, *refs), in_specs...  8.56 us
    ppermute x6, starting transfers between devices, body(): lax.ppermute(value, 'ctx', [(i, i ^ by) for i in range(blocks)])  8.51 us
    pallas_call x1, Pallas kernels, body(): pl.pallas_call(first_kernel, in_specs=[sm, hbm, hbm, hbm, hbm], out_specs...  5.58 us
    ppermute x1, starting transfers between devices, body(): lax.ppermute(feat[:, count - 2:], 'ctx', [(i, i + 1) for i in range(block...  2.36 us
    pallas_call x1, Pallas kernels, body(): pl.pallas_call(lambda *refs: last_kernel(pieces, *refs), in_specs=[vm] *...  1.78 us
    ppermute x6, waiting for transfers between devices, body(): lax.ppermute(value, 'ctx', [(i, i ^ by) for i in range(blocks)])  1.65 us
    pallas_call x1, Pallas kernels, body(): pl.pallas_call(lambda *refs: plan_kernel(count, rounds, *refs), in_specs=...  1.42 us
    slice x1, local copies, waits for them, and re-layouts, body(): feat[:, count - 2:]  0.98 us
  transfers between devices with their start and end apart: 7, of which 2 were waited for; matrix products, arithmetic and copies ran while one was open for 0% of the time, Pallas kernels for 47%

profile of v6, /device:TPU:0, one launch (start us, length us, event | category | flops | bytes accessed | tf_op | source)
XLA Modules:
  0.0 32.9 jit_solution(5890366985988905467)
XLA Ops:
  0.0 1.0 %slice.66 = bf16[3,2,4096]{2,1,0:T(2,128)(2,1)S(1)} slice(bf16[3,256,4096]{2,1,0:T(8,128)(2,1)} %bitcast.91), slice={[0:3], [254:256], [0:4096]} | slice | bytes 98304 | tf_op jit(solution)/shard_map/slice | solution.py:399
  1.0 2.4 %collective-permute-start = (bf16[3,2,4096]{2,1,0:T(2,128)(2,1)S(1)}, bf16[3,2,4096]{2,1,0:T(2,128)(2,1)S(1)}, u32[]{:S(2)}, u32[]{:S(2)}) collective-permute-start(bf16[3,2,4096]{2,1,0:T(2,128)(2,1)S(1)} %slice.66), channel_id=1, source_target_pairs={{0,1},{1,2},{2,3},{3,4},{4,5},{5,6},{6,7},{7,8},{8,9},{9,10},{10,1... | collective-permute-start | bytes 147464 | tf_op jit(solution)/shard_map/ppermute | solution.py:399
  3.4 0.0 copy-start
  3.4 0.0 copy-start.1
  3.4 5.6 %first.1 = (bf16[256,4096]{1,0:T(8,128)(2,1)S(1)}, bf16[256,4096]{1,0:T(8,128)(2,1)S(1)}, f32[16,4096]{1,0:T(8,128)S(1)}, f32[16,4096]{1,0:T(8,128)S(1)}, f32[1,...) custom-call(s32[1]{0:T(128)} %bitcast.pos_ref.refs_0_, ...), custom_call_target="tpu_custom_call" | custom-call | tf_op jit(solution)/shard_map/first/pallas_call | solution.py:402
  9.0 0.0 copy-start.3
  9.0 0.0 copy-start.5
  9.0 0.5 %head.1 = (bf16[2,16,2048]{2,1,0:T(8,128)(2,1)S(1)}, f32[2,4096]{1,0:T(2,128)S(1)}, f32[2,4096]{1,0:T(2,128)S(1)}, bf16[256,4096]{1,0:T(8,128)(2,1)S(1)}) custom-call(s32[1]{0:T(128)} %bitcast.pos_ref.refs_0_, s32[32,128]{1,0:T(8,128)S(1)} %bitcast.79, f32[4,4096]{1,0:T(4,128)S(1)} %get-tuple-element.49.refs_2_, ...), custom_call_target="tpu_custom_call", output_to_operand_aliasing={{3}: (8, {})} | custom-call | tf_op jit(solution)/shard_map/head/pallas_call | solution.py:417
  9.5 0.8 %copy-done.3 = bf16[256,4096]{1,0:T(8,128)(2,1)} copy-done((bf16[256,4096]{1,0:T(8,128)(2,1)}, bf16[256,4096]{1,0:T(8,128)(2,1)S(1)}, u32[]{:S(2)}) %copy-start.3) | copy-done | bytes 2097176
  10.3 2.6 %collective-permute-start.1 = (bf16[2,16,2048]{2,1,0:T(8,128)(2,1)S(1)}, bf16[2,16,2048]{2,1,0:T(8,128)(2,1)S(1)}, u32[]{:S(2)}, u32[]{:S(2)}) collective-permute-start(bf16[2,16,2048]{2,1,0:T(8,128)(2,1)S(1)} %get-tuple-element.53), channel_id=1, source_target_pairs={{0,1},{1,0},{2,3},{3,2},{4,5},{5,4},{6,7},{7,6},{8,9},{9,8},{10,11... | collective-permute-start | bytes 393224 | tf_op jit(solution)/shard_map/ppermute | solution.py:396
  12.9 1.4 %plan.1 = (f32[1,4096]{1,0:T(1,128)S(1)}, bf16[256,128]{1,0:T(8,128)(2,1)S(1)}, bf16[256,256]{1,0:T(8,128)(2,1)S(1)}, bf16[128,256]{1,0:T(8,128)(2,1)S(1)}, f32[...) custom-call(s32[1]{0:T(128)} %bitcast.pos_ref.refs_0_, s32[32,128]{1,0:T(8,128)S(1)} %bitcast.80, s32[4096]{0:T(1024)S(1)} %copy-done, ...), custom_call_target="tpu_custom_call" | custom-call | flops 1073741824 | bytes 5242880 | tf_op jit(solution)/shard_map/plan/pallas_call | solution.py:430
  14.5 1.6 %collective-permute-start.2 = (bf16[16,2048]{1,0:T(8,128)(2,1)S(1)}, bf16[16,2048]{1,0:T(8,128)(2,1)S(1)}, u32[]{:S(2)}, u32[]{:S(2)}) collective-permute-start(bf16[16,2048]{1,0:T(8,128)(2,1)S(1)} %convert_element_type.39), channel_id=1, source_target_pairs={{0,2},{1,3},{2,0},{3,1},{4,6},{5,7},{6,4},{7,5},{8,10},{9,11},{10,... | collective-permute-start | bytes 196616 | tf_op jit(solution)/shard_map/ppermute | solution.py:396
  16.1 1.6 %collective-permute-start.3 = (bf16[16,2048]{1,0:T(8,128)(2,1)S(1)}, bf16[16,2048]{1,0:T(8,128)(2,1)S(1)}, u32[]{:S(2)}, u32[]{:S(2)}) collective-permute-start(bf16[16,2048]{1,0:T(8,128)(2,1)S(1)} %convert_element_type.39), channel_id=1, source_target_pairs={{0,4},{1,5},{2,6},{3,7},{4,0},{5,1},{6,2},{7,3},{8,12},{9,13},{10,... | collective-permute-start | bytes 196616 | tf_op jit(solution)/shard_map/ppermute | solution.py:396
  17.6 0.4 %collective-permute-start.4 = (bf16[16,2048]{1,0:T(8,128)(2,1)S(1)}, bf16[16,2048]{1,0:T(8,128)(2,1)S(1)}, u32[]{:S(2)}, u32[]{:S(2)}) collective-permute-start(bf16[16,2048]{1,0:T(8,128)(2,1)S(1)} %convert_element_type.39), channel_id=1, source_target_pairs={{0,6},{1,7},{2,4},{3,5},{4,2},{5,3},{6,0},{7,1},{8,14},{9,15},{10,... | collective-permute-start | bytes 196616 | tf_op jit(solution)/shard_map/ppermute | solution.py:396
  18.0 4.3 %local.2 = (f32[256,2048]{1,0:T(8,128)S(1)}, f32[256,2048]{1,0:T(8,128)S(1)}, bf16[256,2048]{1,0:T(8,128)(2,1)S(1)}) custom-call(bf16[256,4096]{1,0:T(8,128)(2,1)S(1)} %copy-done.4, f32[2,4096]{1,0:T(2,128)S(1)} %get-tuple-element.74.refs_1_, bf16[256,4096]{1,0:T(8,128)(2,1)S(1)} %get-tuple-element.58.refs_2_, f32[2,4096]{1,0:T(2,128)S(1)} %get-tuple-element.59.refs_3_, ...), custom_call_target="tpu_custom_call" | custom-call | flops 4294967296 | bytes 5242880 | tf_op jit(solution)/shard_map/local/pallas_call | solution.py:447
  22.4 0.4 %collective-permute-done.4 = bf16[16,2048]{1,0:T(8,128)(2,1)S(1)} collective-permute-done((bf16[16,2048]{1,0:T(8,128)(2,1)S(1)}, bf16[16,2048]{1,0:T(8,128)(2,1)S(1)}, u32[]{:S(2)}, u32[]{:S(2)}) %collective-permute-start.4) | collective-permute-done | bytes 65568 | tf_op jit(solution)/shard_map/ppermute | solution.py:396
  22.8 0.1 fusion.3
  22.9 2.3 %collective-permute-start.5 = (bf16[16,2048]{1,0:T(8,128)(2,1)S(1)}, bf16[16,2048]{1,0:T(8,128)(2,1)S(1)}, u32[]{:S(2)}, u32[]{:S(2)}) collective-permute-start(bf16[16,2048]{1,0:T(8,128)(2,1)S(1)} %fusion.3), channel_id=1, source_target_pairs={{0,8},{1,9},{2,10},{3,11},{4,12},{5,13},{6,14},{7,15},{8,0},{9,1},... | collective-permute-start | bytes 196616 | tf_op jit(solution)/shard_map/ppermute | solution.py:396
  25.1 4.3 %local.3 = (f32[256,2048]{1,0:T(8,128)S(1)}, f32[256,2048]{1,0:T(8,128)S(1)}, bf16[256,2048]{1,0:T(8,128)(2,1)S(1)}) custom-call(bf16[256,4096]{1,0:T(8,128)(2,1)S(1)} %copy-done.4, f32[2,4096]{1,0:T(2,128)S(1)} %get-tuple-element.74.refs_1_, bf16[256,4096]{1,0:T(8,128)(2,1)S(1)} %get-tuple-element.58.refs_2_, f32[2,4096]{1,0:T(2,128)S(1)} %get-tuple-element.59.refs_3_, ...), custom_call_target="tpu_custom_call" | custom-call | flops 4294967296 | bytes 5242880 | tf_op jit(solution)/shard_map/local/pallas_call | solution.py:447
  29.5 0.1 fusion.7
  29.5 0.1 collective-permute-start.6
  29.6 1.2 %collective-permute-done.6 = bf16[16,2048]{1,0:T(8,128)(2,1)S(1)} collective-permute-done((bf16[16,2048]{1,0:T(8,128)(2,1)S(1)}, bf16[16,2048]{1,0:T(8,128)(2,1)S(1)}, u32[]{:S(2)}, u32[]{:S(2)}) %collective-permute-start.6) | collective-permute-done | bytes 65568 | tf_op jit(solution)/shard_map/ppermute | solution.py:396
  30.9 0.1 fusion.refs_0_
  30.9 1.8 %last.1 = bf16[256,4096]{1,0:T(8,128)(2,1)} custom-call(f32[16,4096]{1,0:T(8,128)S(1)} %fusion.refs_0_, f32[256,2048]{1,0:T(8,128)S(1)} %get-tuple-element.79.refs_1_, f32[256,2048]{1,0:T(8,128)S(1)} %get-tuple-element.80.refs_2_, bf16[256,2048]{1,0:T(8,128)(2,1)S(1)} %get-tuple-element.81.refs_3_, f32[256,2048]{1,0:T(8,128)S(1)} %get-tuple-element.82.refs_4_, ...), custom_call_target="tpu_custom_call" | custom-call | tf_op jit(solution)/shard_map/last/pallas_call | solution.py:484
  (25 shorter events, 0.2 us)
Async XLA Ops:
  1.0 8.0 %collective-permute-start = (bf16[3,2,4096]{2,1,0:T(2,128)(2,1)S(1)}, bf16[3,2,4096]{2,1,0:T(2,128)(2,1)S(1)}, u32[]{:S(2)}, u32[]{:S(2)}) collective-permute-start(bf16[3,2,4096]{2,1,0:T(2,128)(2,1)S(1)} %slice.66), channel_id=1, source_target_pairs={{0,1},{1,2},{2,3},{3,4},{4,5},{5,6},{6,7},{7,8},{8,9},{9,10},{10,1... | collective-permute-start | bytes 147464 | tf_op jit(solution)/shard_map/ppermute | solution.py:399
  3.4 5.7 %copy-start = (s32[4096]{0:T(1024)S(1)}, s32[4096]{0:T(1024)}, u32[]{:S(2)}) copy-start(s32[4096]{0:T(1024)} %refs_2_.1) | copy-start | bytes 49156
  3.4 5.7 %copy-start.1 = (bf16[2,3,4096]{2,0,1:T(2,128)(2,1)S(1)}, bf16[2,3,4096]{2,0,1:T(2,128)(2,1)}, u32[]{:S(2)}) copy-start(bf16[2,3,4096]{2,0,1:T(2,128)(2,1)} %param.14) | copy-start | bytes 147460
  9.0 1.3 %copy-start.3 = (bf16[256,4096]{1,0:T(8,128)(2,1)}, bf16[256,4096]{1,0:T(8,128)(2,1)S(1)}, u32[]{:S(2)}) copy-start(bf16[256,4096]{1,0:T(8,128)(2,1)S(1)} %get-tuple-element.56.refs_0_) | copy-start | bytes 6291460
  9.0 3.9 %copy-start.2 = (f32[256,16]{0,1:T(8,128)S(1)}, f32[256,16]{0,1:T(8,128)}, u32[]{:S(2)}) copy-start(f32[256,16]{0,1:T(8,128)} %param.11) | copy-start | bytes 49156
  9.0 3.9 %copy-start.5 = (f32[256,16]{0,1:T(8,128)S(1)}, f32[256,16]{0,1:T(8,128)}, u32[]{:S(2)}) copy-start(f32[256,16]{0,1:T(8,128)} %param.10) | copy-start | bytes 49156
  10.3 4.1 %collective-permute-start.1 = (bf16[2,16,2048]{2,1,0:T(8,128)(2,1)S(1)}, bf16[2,16,2048]{2,1,0:T(8,128)(2,1)S(1)}, u32[]{:S(2)}, u32[]{:S(2)}) collective-permute-start(bf16[2,16,2048]{2,1,0:T(8,128)(2,1)S(1)} %get-tuple-element.53), channel_id=1, source_target_pairs={{0,1},{1,0},{2,3},{3,2},{4,5},{5,4},{6,7},{7,6},{8,9},{9,8},{10,11... | collective-permute-start | bytes 393224 | tf_op jit(solution)/shard_map/ppermute | solution.py:396
  12.9 5.1 %copy-start.4 = (bf16[256,4096]{1,0:T(8,128)(2,1)S(1)}, bf16[256,4096]{1,0:T(8,128)(2,1)}, u32[]{:S(2)}) copy-start(bf16[256,4096]{1,0:T(8,128)(2,1)} %copy-done.3) | copy-start | bytes 6291460
  12.9 5.1 %copy-start.6 = (f32[4096]{0:T(1024)S(1)}, f32[4096]{0:T(1024)}, u32[]{:S(2)}) copy-start(f32[4096]{0:T(1024)} %param.12) | copy-start | bytes 49156
  14.5 7.8 %collective-permute-start.2 = (bf16[16,2048]{1,0:T(8,128)(2,1)S(1)}, bf16[16,2048]{1,0:T(8,128)(2,1)S(1)}, u32[]{:S(2)}, u32[]{:S(2)}) collective-permute-start(bf16[16,2048]{1,0:T(8,128)(2,1)S(1)} %convert_element_type.39), channel_id=1, source_target_pairs={{0,2},{1,3},{2,0},{3,1},{4,6},{5,7},{6,4},{7,5},{8,10},{9,11},{10,... | collective-permute-start | bytes 196616 | tf_op jit(solution)/shard_map/ppermute | solution.py:396
  16.1 6.3 %collective-permute-start.3 = (bf16[16,2048]{1,0:T(8,128)(2,1)S(1)}, bf16[16,2048]{1,0:T(8,128)(2,1)S(1)}, u32[]{:S(2)}, u32[]{:S(2)}) collective-permute-start(bf16[16,2048]{1,0:T(8,128)(2,1)S(1)} %convert_element_type.39), channel_id=1, source_target_pairs={{0,4},{1,5},{2,6},{3,7},{4,0},{5,1},{6,2},{7,3},{8,12},{9,13},{10,... | collective-permute-start | bytes 196616 | tf_op jit(solution)/shard_map/ppermute | solution.py:396
  17.6 5.2 %collective-permute-start.4 = (bf16[16,2048]{1,0:T(8,128)(2,1)S(1)}, bf16[16,2048]{1,0:T(8,128)(2,1)S(1)}, u32[]{:S(2)}, u32[]{:S(2)}) collective-permute-start(bf16[16,2048]{1,0:T(8,128)(2,1)S(1)} %convert_element_type.39), channel_id=1, source_target_pairs={{0,6},{1,7},{2,4},{3,5},{4,2},{5,3},{6,0},{7,1},{8,14},{9,15},{10,... | collective-permute-start | bytes 196616 | tf_op jit(solution)/shard_map/ppermute | solution.py:396
  22.9 8.0 %copy-start.7 = (f32[16,4096]{1,0:T(8,128)S(1)}, f32[16,4096]{1,0:T(8,128)}, u32[]{:S(2)}) copy-start(f32[16,4096]{1,0:T(8,128)} %param.13) | copy-start | bytes 786436
  22.9 6.5 %collective-permute-start.5 = (bf16[16,2048]{1,0:T(8,128)(2,1)S(1)}, bf16[16,2048]{1,0:T(8,128)(2,1)S(1)}, u32[]{:S(2)}, u32[]{:S(2)}) collective-permute-start(bf16[16,2048]{1,0:T(8,128)(2,1)S(1)} %fusion.3), channel_id=1, source_target_pairs={{0,8},{1,9},{2,10},{3,11},{4,12},{5,13},{6,14},{7,15},{8,0},{9,1},... | collective-permute-start | bytes 196616 | tf_op jit(solution)/shard_map/ppermute | solution.py:396
  29.5 1.3 %collective-permute-start.6 = (bf16[16,2048]{1,0:T(8,128)(2,1)S(1)}, bf16[16,2048]{1,0:T(8,128)(2,1)S(1)}, u32[]{:S(2)}, u32[]{:S(2)}) collective-permute-start(bf16[16,2048]{1,0:T(8,128)(2,1)S(1)} %fusion.7), channel_id=1, source_target_pairs={{0,1},{1,0},{2,3},{3,2},{4,5},{5,4},{6,7},{7,6},{8,9},{9,8},{10,11... | collective-permute-start | bytes 196616 | tf_op jit(solution)/shard_map/ppermute | solution.py:396

commit v7 on v4

--- a/solution.py
+++ b/solution.py
@@ -10,6 +10,7 @@
 LANES = 128
 SET = 256
 WIDE = 1024
+PIECE = 2048
 SUB = 32
 
 
@@ -38,7 +39,7 @@
 
 
 def first_kernel(pos_ref, seg_hbm, rates_hbm, feat_ref, taps_hbm,
-                 u_ref, q_ref, sum_ref, rate_ref, flat_ref, edge_ref, col_ref, taps_ref,
+                 u_ref, sum_ref, rate_ref, flat_ref, edge_ref, col_ref, taps_ref,
                  keep_ref, shift_ref, kv_ref, seg_ref, rates_ref, sems):
     pos = pos_ref[0]
     count, width = u_ref.shape
@@ -57,13 +58,11 @@
         pltpu.make_async_copy(source, target, sems.at[2 * chunks + i])
         for i, (source, target) in enumerate(((seg_hbm, seg_ref), (rates_hbm, rates_ref), (taps_hbm, taps_ref)))
     ]
-    q_copy = pltpu.make_async_copy(feat_ref.at[0], q_ref, sems.at[2 * chunks + 3])
     for copy in small:
         copy.start()
     for chunk in range(chunks):
         for copy in copies(chunk):
             copy.start()
-    q_copy.start()
     for copy in small:
         copy.wait()
 
@@ -153,8 +152,6 @@
     def _():
         for i in range(width // SET):
             sums_of(i * SET)
-
-    q_copy.wait()
 
 
 def head_kernel(count, pos_ref, seg_ref, edge_ref, halo_ref, early_ref, sw_ref, rate_ref, sum_ref,
@@ -199,75 +196,87 @@
         total_ref[part] = (sum_ref[:, at] + drop * (u1[:, at] + jnp.exp(-rate) * u0[:, at])).astype(BF)
 
 
-def plan_kernel(count, rounds, pos_ref, seg_ref, ids_ref, rates_ref, res_ref, rate_ref, col_ref,
-                wide_ref, lead_ref, tri_ref, keep_ref, half_ref, full_ref):
+def plan_kernel(count, rounds, pos_ref, seg_ref, ids_ref, rates_ref, res_ref, rate_ref, col_ref, feat_ref,
+                wide_ref, lead_ref, tri_ref, keep_ref, half_ref, full_ref, q_ref, sem):
+    q_copies = [
+        pltpu.make_async_copy(feat_ref.at[0, i * 32 : (i + 1) * 32], q_ref.at[i * 32 : (i + 1) * 32], sem.at[i])
+        for i in range(count // 32)
+    ]
+    for copy in q_copies:
+        copy.start()
     pos = pos_ref[0]
-    modes = rates_ref.shape[0]
-    width = rate_ref.shape[1]
-    members = width // rates_ref.shape[1]
-
-    def seg_at(spot):
-        at = jnp.maximum(spot, 0)
-        return jnp.where(spot < 0, 0, ids_ref[at])
-
-    first = pos * count
-    col = col_ref[1]
-    start = iota((count, LANES), 0) // SUB
-    lead = jnp.zeros((count, LANES), F32)
-    for c in range(count // SUB):
-        lead = jnp.where(start == c, seg_at(first + c * SUB - 1).astype(F32), lead)
-    lead_ref[...] = flag(col == lead).astype(BF)
-    inner = lax.rem(iota((SUB, SET), 1), SUB)
-    tall = iota((SUB, SET), 0)
-    for c in range(count // SUB):
-        row = seg_ref[pl.ds((count // LANES) * pos + c * SUB // LANES, 1), :].astype(F32)
-        shift = (c * SUB) % LANES
-        base = row if shift == 0 else pltpu.roll(row, LANES - shift, 1)
-        base = jnp.where(iota((1, LANES), 1) < SUB, base, 0.0)
-        base = base + pltpu.roll(base, SUB, 1)
-        base = base + pltpu.roll(base, 2 * SUB, 1)
-        base = jnp.concatenate([base] * (SET // LANES), axis=1)
-        mine = jnp.concatenate([col[c * SUB : (c + 1) * SUB]] * (SET // LANES), axis=1)
-        tri_ref[c * SUB : (c + 1) * SUB, :] = flag((tall >= inner) & (mine == base)).astype(BF)
-        keep_ref[c * modes : (c + 1) * modes, :] = jnp.broadcast_to(
-            flag(base == ids_ref[first + (c + 1) * SUB - 1].astype(F32)), (modes, SET)).astype(BF)
-    weight = res_ref[...] * jnp.sqrt(rates_ref[...])
-    per = LANES * members
-    onehot = flag(iota((LANES, per), 0) == iota((LANES, per), 1) // members).astype(BF)
-    pick = iota((modes, per), 0) == lax.rem(iota((modes, per), 1), modes)
-    for block in range(width // per):
-        at = slice(block * LANES, (block + 1) * LANES)
-        to = slice(block * per, (block + 1) * per)
-        (spread,) = spread_out([weight[:, at]], onehot)
-        wide_ref[:, to] = jnp.sum(jnp.where(pick, spread, 0.0), axis=0, keepdims=True)
-
-    def decay(rate, low, high):
-        alive = flag(seg_at(low * count - 1) == seg_at(high * count - 1))
-        return jnp.exp(-rate * (count * (high - low)).astype(F32)) * alive
-
-    core = lax.rem(pos, 2)
-    chip = pos // 2
-    rate = rate_ref[:, pl.ds(pl.multiple_of(core * (width // 2), LANES), width // 2)]
-    half_ref[0] = decay(rate, 2 * chip + 1, 2 * chip + 2)
-    spot = 1
-    reach = 1
-    for radix in rounds:
-        size = reach * radix
-        top = 2 * (chip // size) * size + 2 * size
-        own = 2 * (chip // reach) * reach + 2 * reach
-        half_ref[spot] = decay(rate, own, top)
-        for other in range(1, radix):
-            group = (chip // reach) ^ other
-            finish = 2 * (group + 1) * reach
-            ahead = group < chip // reach
-            half_ref[spot + 1] = flag(ahead) * decay(rate, jnp.where(ahead, finish, 0), 2 * chip)
-            half_ref[spot + 2] = decay(rate, finish, top)
-            spot += 2
-        spot += 1
-        reach = size
-    rate = rate_ref[...]
-    full_ref[0] = jnp.where(core == 0, 1.0, decay(rate, 2 * chip, 2 * chip + 1))
-    full_ref[1] = decay(rate, jnp.zeros_like(pos), pos)
+
+    @pl.when(pos >= 0)
+    def _():
+        modes = rates_ref.shape[0]
+        width = rate_ref.shape[1]
+        members = width // rates_ref.shape[1]
+
+        def seg_at(spot):
+            at = jnp.maximum(spot, 0)
+            return jnp.where(spot < 0, 0, ids_ref[at])
+
+        first = pos * count
+        col = col_ref[1]
+        start = iota((count, LANES), 0) // SUB
+        lead = jnp.zeros((count, LANES), F32)
+        for c in range(count // SUB):
+            lead = jnp.where(start == c, seg_at(first + c * SUB - 1).astype(F32), lead)
+        lead_ref[...] = flag(col == lead).astype(BF)
+        inner = lax.rem(iota((SUB, SET), 1), SUB)
+        tall = iota((SUB, SET), 0)
+        for c in range(count // SUB):
+            row = seg_ref[pl.ds((count // LANES) * pos + c * SUB // LANES, 1), :].astype(F32)
+            shift = (c * SUB) % LANES
+            base = row if shift == 0 else pltpu.roll(row, LANES - shift, 1)
+            base = jnp.where(iota((1, LANES), 1) < SUB, base, 0.0)
+            base = base + pltpu.roll(base, SUB, 1)
+            base = base + pltpu.roll(base, 2 * SUB, 1)
+            base = jnp.concatenate([base] * (SET // LANES), axis=1)
+            mine = jnp.concatenate([col[c * SUB : (c + 1) * SUB]] * (SET // LANES), axis=1)
+            tri_ref[c * SUB : (c + 1) * SUB, :] = flag((tall >= inner) & (mine == base)).astype(BF)
+            keep_ref[c * modes : (c + 1) * modes, :] = jnp.broadcast_to(
+                flag(base == ids_ref[first + (c + 1) * SUB - 1].astype(F32)), (modes, SET)).astype(BF)
+        weight = res_ref[...] * jnp.sqrt(rates_ref[...])
+        per = LANES * members
+        onehot = flag(iota((LANES, per), 0) == iota((LANES, per), 1) // members).astype(BF)
+        pick = iota((modes, per), 0) == lax.rem(iota((modes, per), 1), modes)
+        for block in range(width // per):
+            at = slice(block * LANES, (block + 1) * LANES)
+            to = slice(block * per, (block + 1) * per)
+            (spread,) = spread_out([weight[:, at]], onehot)
+            wide_ref[:, to] = jnp.sum(jnp.where(pick, spread, 0.0), axis=0, keepdims=True)
+
+        def decay(rate, low, high):
+            alive = flag(seg_at(low * count - 1) == seg_at(high * count - 1))
+            return jnp.exp(-rate * (count * (high - low)).astype(F32)) * alive
+
+        core = lax.rem(pos, 2)
+        chip = pos // 2
+        rate = rate_ref[:, pl.ds(pl.multiple_of(core * (width // 2), LANES), width // 2)]
+        half_ref[0] = decay(rate, 2 * chip + 1, 2 * chip + 2)
+        spot = 1
+        reach = 1
+        for radix in rounds:
+            size = reach * radix
+            top = 2 * (chip // size) * size + 2 * size
+            own = 2 * (chip // reach) * reach + 2 * reach
+            half_ref[spot] = decay(rate, own, top)
+            for other in range(1, radix):
+                group = (chip // reach) ^ other
+                finish = 2 * (group + 1) * reach
+                ahead = group < chip // reach
+                half_ref[spot + 1] = flag(ahead) * decay(rate, jnp.where(ahead, finish, 0), 2 * chip)
+                half_ref[spot + 2] = decay(rate, finish, top)
+                spot += 2
+            spot += 1
+            reach = size
+        rate = rate_ref[...]
+        full_ref[0] = jnp.where(core == 0, 1.0, decay(rate, 2 * chip, 2 * chip + 1))
+        full_ref[1] = decay(rate, jnp.zeros_like(pos), pos)
+
+    for copy in q_copies:
+        copy.wait()
 
 
 def local_kernel(base, u_ref, head_ref, q_ref, halo_ref, sw_ref, skip_ref, rates_ref, res_ref, rate_ref, flat_ref,
@@ -398,16 +407,16 @@
     halo = lax.ppermute(feat[:, count - 2 :], "ctx", [(i, i + 1) for i in range(blocks - 1)])
 
     hbm = pl.BlockSpec(memory_space=pltpu.HBM)
-    u, q, sums, rate, flat, edge, cols, weights = pl.pallas_call(
+    u, sums, rate, flat, edge, cols, weights = pl.pallas_call(
         first_kernel,
         in_specs=[sm, hbm, hbm, hbm, hbm],
-        out_specs=[vm] * 8,
-        out_shape=[out(count, width, dtype=BF), out(count, width, dtype=BF), out(modes, width), out(modes, width),
+        out_specs=[vm] * 7,
+        out_shape=[out(count, width, dtype=BF), out(modes, width), out(modes, width),
                    out(1, width), out(4, width), out(4, count, LANES),
                    out(*short_weight.shape)],
         scratch_shapes=[
             pltpu.VMEM((count, LANES), BF), pltpu.VMEM((2 * count, count), BF), pltpu.VMEM((2, count, width), BF), pltpu.VMEM(segs.shape, jnp.int32),
-            pltpu.VMEM(rates_t.shape, F32), pltpu.SemaphoreType.DMA((2 * (width // WIDE) + 4,)),
+            pltpu.VMEM(rates_t.shape, F32), pltpu.SemaphoreType.DMA((2 * (width // WIDE) + 3,)),
         ],
         compiler_params=params(),
         name="first",
@@ -425,28 +434,29 @@
     even = (pos & 1) == 0
     other = swap(total, 1)
     steps = 1 + sum(2 * radix - 1 for radix in rounds)
-    wflat, lead, tris, keeps, halves, fulls = pl.pallas_call(
+    wflat, lead, tris, keeps, halves, fulls, q = pl.pallas_call(
         lambda *refs: plan_kernel(count, rounds, *refs),
-        in_specs=[sm, vm, sm] + [vm] * 4,
-        out_specs=[vm] * 6,
+        in_specs=[sm, vm, sm] + [vm] * 4 + [hbm],
+        out_specs=[vm] * 7,
         out_shape=[
             out(1, width), out(count, LANES, dtype=BF), out(count, SET, dtype=BF), out(count // SUB * 16, SET, dtype=BF),
-            out(steps, modes, width // 2), out(2, modes, width),
+            out(steps, modes, width // 2), out(2, modes, width), out(count, width, dtype=BF),
         ],
+        scratch_shapes=[pltpu.SemaphoreType.DMA((count // 32,))],
         compiler_params=params(),
         cost_estimate=pl.CostEstimate(flops=1 << 30, bytes_accessed=5 << 20, transcendentals=0),
         name="plan",
-    )(pos1, segs, segment_ids, rates_t, res_t, rate, cols)
-
-    pieces = width // WIDE
+    )(pos1, segs, segment_ids, rates_t, res_t, rate, cols, stay(feat))
+
+    pieces = width // PIECE
     parts = []
 
     def local(piece, head):
         return pl.pallas_call(
-            lambda *refs: local_kernel(piece * WIDE, *refs),
+            lambda *refs: local_kernel(piece * PIECE, *refs),
             in_specs=[vm] * 15,
             out_specs=[vm] * 3,
-            out_shape=[out(count, WIDE), out(count, WIDE), out(count, WIDE, dtype=BF)],
+            out_shape=[out(count, PIECE), out(count, PIECE), out(count, PIECE, dtype=BF)],
             compiler_params=params(),
             cost_estimate=pl.CostEstimate(flops=4 << 30, bytes_accessed=5 << 20, transcendentals=0),
             name="local",

time: 33.8 us -> 33.1 us (0.979)
  local copies, waits for them, and re-layouts: 2.34 us -> 1.03 us
  Pallas kernels: 18.1 us -> 18.6 us
    unnamed x16 -> x12, local copies, waits for them, and re-layouts: 1.35 us -> 0.04 us
    pallas_call x1, Pallas kernels: 1.42 us -> 2.37 us  [body(): pl.pallas_call(lambda *refs: plan_kernel(count, rounds, *refs), in_specs=...]
    pallas_call x4 -> x2, Pallas kernels: 8.96 us -> 8.56 us  [local(): pl.pallas_call(lambda *refs: local_kernel(piece * PIECE, *refs), in_specs...]
  transfers between devices with their start and end apart: 7 -> 7, of which waited for: 2 -> 2; matrix products, arithmetic and copies ran while one was open for 0% -> 0% of each run, Pallas kernels for 47% -> 49%
where the time goes in v7:
time: 33.1 us; the launch traced here: 32.9 us
  Pallas kernels  18.6 us (56%)
  starting transfers between devices  10.9 us (33%)
  waiting for transfers between devices  1.66 us (5%)
  local copies, waits for them, and re-layouts  1.03 us (3%)
  between operations  0.4 us (1%)
    ppermute x6, starting transfers between devices, body(): lax.ppermute(value, 'ctx', [(i, i ^ by) for i in range(blocks)])  8.56 us
    pallas_call x2, Pallas kernels, local(): pl.pallas_call(lambda *refs: local_kernel(piece * PIECE, *refs), in_specs...  8.56 us
    pallas_call x1, Pallas kernels, body(): pl.pallas_call(first_kernel, in_specs=[sm, hbm, hbm, hbm, hbm], out_specs...  5.35 us
    pallas_call x1, Pallas kernels, body(): pl.pallas_call(lambda *refs: plan_kernel(count, rounds, *refs), in_specs=...  2.37 us
    ppermute x1, starting transfers between devices, body(): lax.ppermute(feat[:, count - 2:], 'ctx', [(i, i + 1) for i in range(block...  2.36 us
    pallas_call x1, Pallas kernels, body(): pl.pallas_call(lambda *refs: last_kernel(pieces, *refs), in_specs=[vm] *...  1.78 us
    ppermute x6, waiting for transfers between devices, body(): lax.ppermute(value, 'ctx', [(i, i ^ by) for i in range(blocks)])  1.65 us
    slice x1, local copies, waits for them, and re-layouts, body(): feat[:, count - 2:]  0.98 us
  transfers between devices with their start and end apart: 7, of which 2 were waited for; matrix products, arithmetic and copies ran while one was open for 0% of the time, Pallas kernels for 49%

profile of v7, /device:TPU:0, one launch (start us, length us, event | category | flops | bytes accessed | tf_op | source)
XLA Modules:
  0.0 32.9 jit_solution(12066170527862264945)
XLA Ops:
  0.0 1.0 %slice.66 = bf16[3,2,4096]{2,1,0:T(2,128)(2,1)S(1)} slice(bf16[3,256,4096]{2,1,0:T(8,128)(2,1)} %bitcast.91), slice={[0:3], [254:256], [0:4096]} | slice | bytes 98304 | tf_op jit(solution)/shard_map/slice | solution.py:407
  1.0 2.4 %collective-permute-start = (bf16[3,2,4096]{2,1,0:T(2,128)(2,1)S(1)}, bf16[3,2,4096]{2,1,0:T(2,128)(2,1)S(1)}, u32[]{:S(2)}, u32[]{:S(2)}) collective-permute-start(bf16[3,2,4096]{2,1,0:T(2,128)(2,1)S(1)} %slice.66), channel_id=1, source_target_pairs={{0,1},{1,2},{2,3},{3,4},{4,5},{5,6},{6,7},{7,8},{8,9},{9,10},{10,1... | collective-permute-start | bytes 147464 | tf_op jit(solution)/shard_map/ppermute | solution.py:407
  3.4 0.0 copy-start
  3.4 0.0 copy-start.2
  3.4 0.0 copy-start.1
  3.4 0.0 copy-start.3
  3.4 5.3 %first.1 = (bf16[256,4096]{1,0:T(8,128)(2,1)S(1)}, f32[16,4096]{1,0:T(8,128)S(1)}, f32[16,4096]{1,0:T(8,128)S(1)}, f32[1,4096]{1,0:T(1,128)S(1)}, f32[4,4096]{1,...) custom-call(s32[1]{0:T(128)} %bitcast.pos_ref.refs_0_, s32[32,128]{1,0:T(8,128)} %bitcast.78, ...), custom_call_target="tpu_custom_call" | custom-call | tf_op jit(solution)/shard_map/first/pallas_call | solution.py:410
  8.8 0.5 %head.1 = (bf16[2,16,2048]{2,1,0:T(8,128)(2,1)S(1)}, f32[2,4096]{1,0:T(2,128)S(1)}, f32[2,4096]{1,0:T(2,128)S(1)}) custom-call(s32[1]{0:T(128)} %bitcast.pos_ref.refs_0_, s32[32,128]{1,0:T(8,128)S(1)} %bitcast.79, f32[4,4096]{1,0:T(4,128)S(1)} %get-tuple-element.48.refs_2_, bf16[3,2,4096]{2,1,0:T(2,128)(2,1)S(1)} %collective-permute-done.refs_3_, ...), custom_call_target="tpu_custom_call" | custom-call | tf_op jit(solution)/shard_map/head/pallas_call | solution.py:425
  9.3 2.7 %collective-permute-start.1 = (bf16[2,16,2048]{2,1,0:T(8,128)(2,1)S(1)}, bf16[2,16,2048]{2,1,0:T(8,128)(2,1)S(1)}, u32[]{:S(2)}, u32[]{:S(2)}) collective-permute-start(bf16[2,16,2048]{2,1,0:T(8,128)(2,1)S(1)} %get-tuple-element.51), channel_id=1, source_target_pairs={{0,1},{1,0},{2,3},{3,2},{4,5},{5,4},{6,7},{7,6},{8,9},{9,8},{10,11... | collective-permute-start | bytes 393224 | tf_op jit(solution)/shard_map/ppermute | solution.py:404
  12.0 2.4 %plan.1 = (f32[1,4096]{1,0:T(1,128)S(1)}, bf16[256,128]{1,0:T(8,128)(2,1)S(1)}, bf16[256,256]{1,0:T(8,128)(2,1)S(1)}, bf16[128,256]{1,0:T(8,128)(2,1)S(1)}, f32[...) custom-call(s32[1]{0:T(128)} %bitcast.pos_ref.refs_0_, s32[32,128]{1,0:T(8,128)S(1)} %bitcast.80, ...), custom_call_target="tpu_custom_call" | custom-call | flops 1073741824 | bytes 5242880 | tf_op jit(solution)/shard_map/plan/pallas_call | solution.py:437
  14.5 1.6 %collective-permute-start.2 = (bf16[16,2048]{1,0:T(8,128)(2,1)S(1)}, bf16[16,2048]{1,0:T(8,128)(2,1)S(1)}, u32[]{:S(2)}, u32[]{:S(2)}) collective-permute-start(bf16[16,2048]{1,0:T(8,128)(2,1)S(1)} %convert_element_type.39), channel_id=1, source_target_pairs={{0,2},{1,3},{2,0},{3,1},{4,6},{5,7},{6,4},{7,5},{8,10},{9,11},{10,... | collective-permute-start | bytes 196616 | tf_op jit(solution)/shard_map/ppermute | solution.py:404
  16.1 1.6 %collective-permute-start.3 = (bf16[16,2048]{1,0:T(8,128)(2,1)S(1)}, bf16[16,2048]{1,0:T(8,128)(2,1)S(1)}, u32[]{:S(2)}, u32[]{:S(2)}) collective-permute-start(bf16[16,2048]{1,0:T(8,128)(2,1)S(1)} %convert_element_type.39), channel_id=1, source_target_pairs={{0,4},{1,5},{2,6},{3,7},{4,0},{5,1},{6,2},{7,3},{8,12},{9,13},{10,... | collective-permute-start | bytes 196616 | tf_op jit(solution)/shard_map/ppermute | solution.py:404
  17.7 0.4 %collective-permute-start.4 = (bf16[16,2048]{1,0:T(8,128)(2,1)S(1)}, bf16[16,2048]{1,0:T(8,128)(2,1)S(1)}, u32[]{:S(2)}, u32[]{:S(2)}) collective-permute-start(bf16[16,2048]{1,0:T(8,128)(2,1)S(1)} %convert_element_type.39), channel_id=1, source_target_pairs={{0,6},{1,7},{2,4},{3,5},{4,2},{5,3},{6,0},{7,1},{8,14},{9,15},{10,... | collective-permute-start | bytes 196616 | tf_op jit(solution)/shard_map/ppermute | solution.py:404
  18.0 4.3 %local.2 = (f32[256,2048]{1,0:T(8,128)S(1)}, f32[256,2048]{1,0:T(8,128)S(1)}, bf16[256,2048]{1,0:T(8,128)(2,1)S(1)}) custom-call(bf16[256,4096]{1,0:T(8,128)(2,1)S(1)} %get-tuple-element.54.refs_0_, f32[2,4096]{1,0:T(2,128)S(1)} %get-tuple-element.72.refs_1_, bf16[256,4096]{1,0:T(8,128)(2,1)S(1)} %get-tuple-element.56.refs_2_, ...), custom_call_target="tpu_custom_call" | custom-call | flops 4294967296 | bytes 5242880 | tf_op jit(solution)/shard_map/local/pallas_call | solution.py:455
  22.4 0.4 %collective-permute-done.4 = bf16[16,2048]{1,0:T(8,128)(2,1)S(1)} collective-permute-done((bf16[16,2048]{1,0:T(8,128)(2,1)S(1)}, bf16[16,2048]{1,0:T(8,128)(2,1)S(1)}, u32[]{:S(2)}, u32[]{:S(2)}) %collective-permute-start.4) | collective-permute-done | bytes 65568 | tf_op jit(solution)/shard_map/ppermute | solution.py:404
  22.8 0.1 fusion.3
  22.9 0.0 copy-start.5
  22.9 2.2 %collective-permute-start.5 = (bf16[16,2048]{1,0:T(8,128)(2,1)S(1)}, bf16[16,2048]{1,0:T(8,128)(2,1)S(1)}, u32[]{:S(2)}, u32[]{:S(2)}) collective-permute-start(bf16[16,2048]{1,0:T(8,128)(2,1)S(1)} %fusion.3), channel_id=1, source_target_pairs={{0,8},{1,9},{2,10},{3,11},{4,12},{5,13},{6,14},{7,15},{8,0},{9,1},... | collective-permute-start | bytes 196616 | tf_op jit(solution)/shard_map/ppermute | solution.py:404
  25.1 4.3 %local.3 = (f32[256,2048]{1,0:T(8,128)S(1)}, f32[256,2048]{1,0:T(8,128)S(1)}, bf16[256,2048]{1,0:T(8,128)(2,1)S(1)}) custom-call(bf16[256,4096]{1,0:T(8,128)(2,1)S(1)} %get-tuple-element.54.refs_0_, f32[2,4096]{1,0:T(2,128)S(1)} %get-tuple-element.72.refs_1_, bf16[256,4096]{1,0:T(8,128)(2,1)S(1)} %get-tuple-element.56.refs_2_, ...), custom_call_target="tpu_custom_call" | custom-call | flops 4294967296 | bytes 5242880 | tf_op jit(solution)/shard_map/local/pallas_call | solution.py:455
  29.5 0.1 fusion.7
  29.5 0.1 collective-permute-start.6
  29.6 1.2 %collective-permute-done.6 = bf16[16,2048]{1,0:T(8,128)(2,1)S(1)} collective-permute-done((bf16[16,2048]{1,0:T(8,128)(2,1)S(1)}, bf16[16,2048]{1,0:T(8,128)(2,1)S(1)}, u32[]{:S(2)}, u32[]{:S(2)}) %collective-permute-start.6) | collective-permute-done | bytes 65568 | tf_op jit(solution)/shard_map/ppermute | solution.py:404
  30.9 0.1 fusion.refs_0_
  30.9 1.8 %last.1 = bf16[256,4096]{1,0:T(8,128)(2,1)} custom-call(f32[16,4096]{1,0:T(8,128)S(1)} %fusion.refs_0_, f32[256,2048]{1,0:T(8,128)S(1)} %get-tuple-element.77.refs_1_, f32[256,2048]{1,0:T(8,128)S(1)} %get-tuple-element.78.refs_2_, bf16[256,2048]{1,0:T(8,128)(2,1)S(1)} %get-tuple-element.79.refs_3_, f32[256,2048]{1,0:T(8,128)S(1)} %get-tuple-element.80.refs_4_, ...), custom_call_target="tpu_custom_call" | custom-call | tf_op jit(solution)/shard_map/last/pallas_call | solution.py:492
  (21 shorter events, 0.2 us)
Async XLA Ops:
  1.0 7.8 %collective-permute-start = (bf16[3,2,4096]{2,1,0:T(2,128)(2,1)S(1)}, bf16[3,2,4096]{2,1,0:T(2,128)(2,1)S(1)}, u32[]{:S(2)}, u32[]{:S(2)}) collective-permute-start(bf16[3,2,4096]{2,1,0:T(2,128)(2,1)S(1)} %slice.66), channel_id=1, source_target_pairs={{0,1},{1,2},{2,3},{3,4},{4,5},{5,6},{6,7},{7,8},{8,9},{9,10},{10,1... | collective-permute-start | bytes 147464 | tf_op jit(solution)/shard_map/ppermute | solution.py:407
  3.4 5.4 %copy-start = (s32[4096]{0:T(1024)S(1)}, s32[4096]{0:T(1024)}, u32[]{:S(2)}) copy-start(s32[4096]{0:T(1024)} %refs_2_.1) | copy-start | bytes 49156
  3.4 5.4 %copy-start.2 = (bf16[2,3,4096]{2,0,1:T(2,128)(2,1)S(1)}, bf16[2,3,4096]{2,0,1:T(2,128)(2,1)}, u32[]{:S(2)}) copy-start(bf16[2,3,4096]{2,0,1:T(2,128)(2,1)} %param.14) | copy-start | bytes 147460
  3.4 8.6 %copy-start.1 = (f32[256,16]{0,1:T(8,128)S(1)}, f32[256,16]{0,1:T(8,128)}, u32[]{:S(2)}) copy-start(f32[256,16]{0,1:T(8,128)} %param.11) | copy-start | bytes 49156
  3.4 8.6 %copy-start.3 = (f32[256,16]{0,1:T(8,128)S(1)}, f32[256,16]{0,1:T(8,128)}, u32[]{:S(2)}) copy-start(f32[256,16]{0,1:T(8,128)} %param.10) | copy-start | bytes 49156
  9.3 5.1 %collective-permute-start.1 = (bf16[2,16,2048]{2,1,0:T(8,128)(2,1)S(1)}, bf16[2,16,2048]{2,1,0:T(8,128)(2,1)S(1)}, u32[]{:S(2)}, u32[]{:S(2)}) collective-permute-start(bf16[2,16,2048]{2,1,0:T(8,128)(2,1)S(1)} %get-tuple-element.51), channel_id=1, source_target_pairs={{0,1},{1,0},{2,3},{3,2},{4,5},{5,4},{6,7},{7,6},{8,9},{9,8},{10,11... | collective-permute-start | bytes 393224 | tf_op jit(solution)/shard_map/ppermute | solution.py:404
  12.0 6.0 %copy-start.4 = (f32[4096]{0:T(1024)S(1)}, f32[4096]{0:T(1024)}, u32[]{:S(2)}) copy-start(f32[4096]{0:T(1024)} %param.12) | copy-start | bytes 49156
  14.5 7.8 %collective-permute-start.2 = (bf16[16,2048]{1,0:T(8,128)(2,1)S(1)}, bf16[16,2048]{1,0:T(8,128)(2,1)S(1)}, u32[]{:S(2)}, u32[]{:S(2)}) collective-permute-start(bf16[16,2048]{1,0:T(8,128)(2,1)S(1)} %convert_element_type.39), channel_id=1, source_target_pairs={{0,2},{1,3},{2,0},{3,1},{4,6},{5,7},{6,4},{7,5},{8,10},{9,11},{10,... | collective-permute-start | bytes 196616 | tf_op jit(solution)/shard_map/ppermute | solution.py:404
  16.1 6.3 %collective-permute-start.3 = (bf16[16,2048]{1,0:T(8,128)(2,1)S(1)}, bf16[16,2048]{1,0:T(8,128)(2,1)S(1)}, u32[]{:S(2)}, u32[]{:S(2)}) collective-permute-start(bf16[16,2048]{1,0:T(8,128)(2,1)S(1)} %convert_element_type.39), channel_id=1, source_target_pairs={{0,4},{1,5},{2,6},{3,7},{4,0},{5,1},{6,2},{7,3},{8,12},{9,13},{10,... | collective-permute-start | bytes 196616 | tf_op jit(solution)/shard_map/ppermute | solution.py:404
  17.7 5.2 %collective-permute-start.4 = (bf16[16,2048]{1,0:T(8,128)(2,1)S(1)}, bf16[16,2048]{1,0:T(8,128)(2,1)S(1)}, u32[]{:S(2)}, u32[]{:S(2)}) collective-permute-start(bf16[16,2048]{1,0:T(8,128)(2,1)S(1)} %convert_element_type.39), channel_id=1, source_target_pairs={{0,6},{1,7},{2,4},{3,5},{4,2},{5,3},{6,0},{7,1},{8,14},{9,15},{10,... | collective-permute-start | bytes 196616 | tf_op jit(solution)/shard_map/ppermute | solution.py:404
  22.9 8.0 %copy-start.5 = (f32[16,4096]{1,0:T(8,128)S(1)}, f32[16,4096]{1,0:T(8,128)}, u32[]{:S(2)}) copy-start(f32[16,4096]{1,0:T(8,128)} %param.13) | copy-start | bytes 786436
  22.9 6.5 %collective-permute-start.5 = (bf16[16,2048]{1,0:T(8,128)(2,1)S(1)}, bf16[16,2048]{1,0:T(8,128)(2,1)S(1)}, u32[]{:S(2)}, u32[]{:S(2)}) collective-permute-start(bf16[16,2048]{1,0:T(8,128)(2,1)S(1)} %fusion.3), channel_id=1, source_target_pairs={{0,8},{1,9},{2,10},{3,11},{4,12},{5,13},{6,14},{7,15},{8,0},{9,1},... | collective-permute-start | bytes 196616 | tf_op jit(solution)/shard_map/ppermute | solution.py:404
  29.5 1.3 %collective-permute-start.6 = (bf16[16,2048]{1,0:T(8,128)(2,1)S(1)}, bf16[16,2048]{1,0:T(8,128)(2,1)S(1)}, u32[]{:S(2)}, u32[]{:S(2)}) collective-permute-start(bf16[16,2048]{1,0:T(8,128)(2,1)S(1)} %fusion.7), channel_id=1, source_target_pairs={{0,1},{1,0},{2,3},{3,2},{4,5},{5,4},{6,7},{7,6},{8,9},{9,8},{10,11... | collective-permute-start | bytes 196616 | tf_op jit(solution)/shard_map/ppermute | solution.py:404
